TPU v7x, 32 devices: a whole 2x2x4 slice. The times are simulated.
32 devices in a mesh: grp: 2 (over y), gz: 4 (over z), af: 4 (over x, core).
Axes of the slice: x: 2, y: 2, z: 4, core: 2. Of those that a mesh axis runs over, the one named last changes fastest.
Arguments:
- volume: float32 [64, 16, 16, 256], P('af', ('grp', 'gz')), parts along dimension 1, may hold values from -6 to 6
- out_grad: float32 [128, 8, 8, 128], P('af', ('grp', 'gz')), parts along dimension 1, may hold values from -6 to 6
- weight: float32 [128, 1728], P('af'), may hold values from -0.15625 to 0.15625
Outputs:
- input_grad: float32 [64, 16, 16, 256], P('af', ('grp', 'gz')), parts along dimension 1
- weight_grad: float32 [128, 3456], P('af', 'grp'), parts along dimension 1
There are 2 independent parts, one for each index of `grp`. A program takes and returns all parts, laid end to end along the dimension named above; an argument that names none is the same for every part. Nothing has to cross between parts.
All inputs are finite; a program needn't handle non-finite values.
Results may differ from a plain program's by a relative error of at most 0.0003.
Values sent between devices are 32-bit elements; how exact they have to be, the bound alone decides.
No kernel may reach another device: no remote copies, remote signals or barrier semaphores. Data moves between devices by JAX's collectives and lax.ppermute only.
A program may use at most 128 MiB of HBM per device.

v0:
```python
import math

import jax
import jax.numpy as jnp
from jax import lax
from jax.sharding import PartitionSpec as P


def shifted(value, axis, steps):
    count = lax.axis_size(axis)
    leading, last = (max(0, -steps), min(count, count - steps))
    return lax.ppermute(value, axis, [(source, source + steps) for source in range(leading, last)])


def tap_matrix(extended, out_depth, out_rows, out_cols):
    channels = extended.shape[0]
    padded = jnp.pad(extended, ((0, 0), (0, 1), (1, 1), (1, 1)))
    split = padded.reshape(channels, out_depth + 1, 2, out_rows + 1, 2, out_cols + 1, 2)
    pieces = []
    for depth_tap in range(3):
        for row_tap in range(3):
            for col_tap in range(3):
                dz_lo = depth_tap // 2
                dy_lo = row_tap // 2
                dx_lo = col_tap // 2
                pieces.append(
                    split[
                        :,
                        dz_lo : dz_lo + out_depth,
                        depth_tap % 2,
                        dy_lo : dy_lo + out_rows,
                        row_tap % 2,
                        dx_lo : dx_lo + out_cols,
                        col_tap % 2,
                    ]
                )
    stacked = jnp.stack(pieces, axis=0)
    return stacked.reshape(27 * channels, out_depth * out_rows * out_cols)


def place_terms(tap_terms, channels, depth_count, out_rows, out_cols, planes, rows, cols):
    shaped = tap_terms.reshape(27, channels, depth_count, out_rows, out_cols)
    phases = {}
    for depth_tap in range(3):
        for row_tap in range(3):
            for col_tap in range(3):
                index = 9 * depth_tap + 3 * row_tap + col_tap
                dz_lo = depth_tap // 2
                dy_lo = row_tap // 2
                dx_lo = col_tap // 2
                moved = jnp.pad(
                    shaped[index],
                    ((0, 0), (dz_lo, 1 - dz_lo), (dy_lo, 1 - dy_lo), (dx_lo, 1 - dx_lo)),
                )
                parity = (depth_tap % 2, row_tap % 2, col_tap % 2)
                phases[parity] = moved if parity not in phases else phases[parity] + moved
    depth_pairs = []
    for depth_bit in range(2):
        row_pairs = []
        for row_bit in range(2):
            col_pair = jnp.stack(
                [phases[depth_bit, row_bit, 0], phases[depth_bit, row_bit, 1]], axis=-1
            )
            row_pairs.append(col_pair)
        depth_pairs.append(jnp.stack(row_pairs, axis=3))
    woven = jnp.stack(depth_pairs, axis=2)
    canvas = woven.reshape(channels, 2 * (depth_count + 1), 2 * (out_rows + 1), 2 * (out_cols + 1))
    return canvas[:, 1 : planes + 1, 1 : rows + 1, 1 : cols + 1]


def local(volume, out_grad, weight):
    channels, planes, rows, cols = volume.shape
    filters, out_depth, out_rows, out_cols = out_grad.shape
    in_total = weight.shape[1] // 27
    factor = 1.0 / math.sqrt(out_depth * lax.axis_size("gz") * out_rows * out_cols)
    lower_rim = shifted(volume[:, planes - 1 : planes], "gz", 1)
    extended = jnp.concatenate([lower_rim, volume], axis=1)
    upper_rim = shifted(out_grad, "gz", -1)
    grad_ext = jnp.concatenate([out_grad, upper_rim], axis=1)
    grads_all, weight_all = (
        lax.all_gather(grad_ext, "af", axis=0, tiled=True),
        lax.all_gather(weight, "af", axis=0, tiled=True),
    )
    all_filters = grads_all.shape[0]
    channel_first = lax.axis_index("af") * channels
    weight_cube = weight_all.reshape(all_filters, 27, in_total)
    own_weight = lax.dynamic_slice_in_dim(weight_cube, channel_first, channels, 2).reshape(
        all_filters, 27 * channels
    )
    tap_terms = lax.dot_general(
        own_weight,
        grads_all.reshape(all_filters, -1),
        (((0,), (0,)), ((), ())),
        precision=lax.Precision.HIGHEST,
        preferred_element_type=jnp.float32,
    )
    input_grad = place_terms(
        tap_terms, channels, out_depth + 1, out_rows, out_cols, planes, rows, cols
    )
    local_grads = out_grad.reshape(filters, -1)
    portion = lax.all_gather(extended, "af", axis=0, tiled=True)
    count = portion.shape[0]
    tap_rows = tap_matrix(portion, out_depth, out_rows, out_cols)
    partial_grad = lax.dot_general(
        local_grads,
        tap_rows,
        (((1,), (1,)), ((), ())),
        precision=lax.Precision.HIGHEST,
        preferred_element_type=jnp.float32,
    )
    partial_grad = partial_grad.reshape(filters, 27, count)
    summed = lax.psum(partial_grad, "gz")
    weight_grad = (summed * factor).reshape(filters, 27 * in_total)
    return (input_grad, weight_grad)


def solution(mesh):
    return jax.shard_map(
        local,
        mesh=mesh,
        in_specs=(
            P("af", ("grp", "gz"), None, None),
            P("af", ("grp", "gz"), None, None),
            P("af", None),
        ),
        out_specs=(P("af", ("grp", "gz"), None, None), P("af", "grp")),
        check_vma=False,
    )
```

profile of v0, /device:TPU:0, one launch (start us, length us, event | category | flops | bytes accessed | tf_op | source)
XLA Modules:
  0.0 200.1 jit_solution(6348233589967276725)
XLA Ops:
  7.2 1.3 collective-permute-start
  8.5 7.3 %collective-permute-done = f32[32,1,8,128]{3,2,1,0:T(8,128)S(1)} collective-permute-done((f32[32,1,8,128]{3,2,1,0:T(8,128)}, f32[32,1,8,128]{3,2,1,0:T(8,128)S(1)}, u32[]{:S(2)}, u32[]{:S(2)}) %collective-permute-start) | collective-permute-done | bytes 131104 | tf_op jit(solution)/shard_map/ppermute | solution.py:12
  15.8 1.6 pad_maximum_fusion.2
  17.6 1.0 slice.223
  18.5 3.7 %collective-permute-start.1 = (f32[16,1,16,256]{3,2,1,0:T(8,128)S(1)}, f32[16,1,16,256]{3,2,1,0:T(8,128)S(1)}, u32[]{:S(2)}, u32[]{:S(2)}) collective-permute-start(f32[16,1,16,256]{3,2,1,0:T(8,128)S(1)} %slice.223), channel_id=1, source_target_pairs={{0,4},{4,8},{8,12},{1,5},{5,9},{9,13},{2,6},{6,10},{10,14},{3,7},{... | collective-permute-start | bytes 786440 | tf_op jit(solution)/shard_map/ppermute | solution.py:12
  22.2 4.7 %collective-permute-done.1 = f32[16,1,16,256]{3,2,1,0:T(8,128)S(1)} collective-permute-done((f32[16,1,16,256]{3,2,1,0:T(8,128)S(1)}, f32[16,1,16,256]{3,2,1,0:T(8,128)S(1)}, u32[]{:S(2)}, u32[]{:S(2)}) %collective-permute-start.1) | collective-permute-done | bytes 262176 | tf_op jit(solution)/shard_map/ppermute | solution.py:12
  26.9 2.0 pad_maximum_fusion.1
  28.9 10.2 %all_gather.9 = f32[128,1728]{1,0:T(8,128)S(1)} all-gather(f32[32,1728]{1,0:T(8,128)} %param.5), channel_id=1, replica_groups=mesh['grp'=2,'gz'=4,'af'=4] {'af'}, dimensions={0}, use_global_device_ids=true | all-gather | bytes 1105920 | tf_op jit(solution)/shard_map/all_gather | solution.py:82
  39.5 4.3 %fusion.6 = f32[432,2048]{1,0:T(8,128)S(1)} fusion(f32[128,432]{0,1:T(8,128)S(1)} %bitcast.271, f32[16,8,16,128]{3,2,1,0:T(8,128)} %bitcast.270), kind=kOutput, calls=%fused_computation.7 | convolution fusion | flops 1358954496 | bytes 4808704 | tf_op jit(solution)/shard_map/dot_general | solution.py:90
  47.9 1.4 maximum_bitcast_fusion
  49.3 16.4 %all-gather.5.cloned.1.call-done = f32[64,3,16,256]{3,2,1,0:T(8,128)} async-done(((f32[16,3,16,256]{3,2,1,0:T(8,128)}), f32[64,3,16,256]{3,2,1,0:T(8,128)}) %all-gather.5.cloned.1.call-update) | async-done | bytes 3145744 | tf_op jit(solution)/shard_map/all_gather | solution.py:101
  65.6 6.6 %copy.233 = f32[64,3,16,256]{0,1,3,2:T(4,128)} copy(f32[64,3,16,256]{3,2,1,0:T(8,128)} %all-gather.5.cloned.1.call-done) | data formatting | bytes 6291456
  72.3 8.7 %pad.120.clone = f32[64,4,18,258]{0,1,3,2:T(4,128)} pad(f32[64,3,16,256]{0,1,3,2:T(4,128)} %copy.233, f32[]{:T(128)} %constant.12.clone.1), padding=0_0x0_1x1_1x1_1 | pad | bytes 7901188 | tf_op jit(solution)/shard_map/jit(_pad)/pad | solution.py:17
  80.9 5.4 %fusion.12 = (f32[64,1,1,8,1,128,1]{0,2,1,6,5,4,3:T(1,128)S(1)}, f32[64,1,1,8,1,128,1]{0,2,1,6,5,4,3:T(1,128)S(1)}, f32[64,1,1,8,1,128,1]{0,2,1,6,5,4,3:T(1,128)...) fusion(f32[64,2,2,9,2,129,2]{0,2,1,6,5,4,3:T(2,128)} %bitcast.239), kind=kLoop, calls=%fused_computation.83 | loop fusion | bytes 4194304 | tf_op jit(solution)/shard_map/slice | solution.py:27
  86.3 15.3 %fusion.11 = (f32[64,1,1,8,1,128,1]{0,2,1,6,5,4,3:T(1,128)S(1)}, f32[64,1,1,8,1,128,1]{0,2,1,6,5,4,3:T(1,128)S(1)}, f32[64,1,1,8,1,128,1]{0,2,1,6,5,4,3:T(1,128)...) fusion(f32[64,2,2,9,2,129,2]{0,2,1,6,5,4,3:T(2,128)} %bitcast.240), kind=kLoop, calls=%fused_computation.82 | loop fusion | bytes 9961472 | tf_op jit(solution)/shard_map/slice | solution.py:27
  103.3 0.9 constant_dynamic-update-slice_fusion.24
  104.2 0.9 constant_dynamic-update-slice_fusion.23
  110.1 0.9 constant_dynamic-update-slice_fusion.16
  114.3 0.9 constant_dynamic-update-slice_fusion.11
  115.2 0.9 constant_dynamic-update-slice_fusion.10
  117.8 0.9 constant_dynamic-update-slice_fusion.7
  122.0 0.9 constant_dynamic-update-slice_fusion.2
  124.6 11.8 %copy.205 = f32[27,64,1,8,128]{4,3,1,0,2:T(8,128)} copy(f32[27,64,1,8,128]{1,4,3,2,0:T(8,128)} %constant_dynamic-update-slice_fusion) | data formatting | bytes 14155776 | tf_op jit(solution)/shard_map/stack | solution.py:37
  136.3 10.1 %fusion.3 = f32[32,1728]{1,0:T(8,128)S(1)} fusion(f32[216,8,8,128]{3,2,1,0:T(8,128)} %bitcast.241, f32[4,8,8,128]{3,2,1,0:T(8,128)S(1)} %bitcast.272), kind=kOutput, calls=%fused_computation.4 | convolution fusion | flops 679477248 | bytes 7430144 | tf_op jit(solution)/shard_map/dot_general | solution.py:104
  146.4 1.1 reshape.93
  147.6 1.9 pad_maximum_fusion
  149.5 16.1 %copy.176 = f32[16,3,2,9,2,129,2]{0,6,5,4,3,2,1:T(2,128)} copy(f32[16,3,2,9,2,129,2]{5,0,6,3,1,4,2:T(8,128)S(1)} %pad_maximum_fusion) | data formatting | bytes 3566592 | tf_op jit(solution)/shard_map/stack | solution.py:66
  165.7 17.7 %reshape.89 = f32[16,6,18,258]{0,3,2,1:T(8,128)} reshape(f32[16,3,2,9,2,129,2]{0,6,5,4,3,2,1:T(2,128)} %copy.176) | data formatting | bytes 3566592 | tf_op jit(solution)/shard_map/reshape | solution.py:67
  183.3 4.7 %slice.278 = f32[16,2,16,256]{0,3,2,1:T(8,128)} slice(f32[16,6,18,258]{0,3,2,1:T(8,128)} %reshape.89), slice={[0:16], [1:3], [1:17], [1:257]} | slice | bytes 1048576 | tf_op jit(solution)/shard_map/slice | solution.py:68
  188.0 3.5 %copy.206 = f32[16,2,16,256]{3,2,1,0:T(8,128)} copy(f32[16,2,16,256]{0,3,2,1:T(8,128)} %slice.278) | data formatting | bytes 1048576
  191.6 1.1 broadcast_multiply_fusion
  192.7 0.9 reshape.94
  (97 shorter events, 21.1 us)
Async XLA Ops:
  7.2 32.3 %all-gather.3.cloned.1.call-start = ((), (), s32[]{:S(2)}) async-start(), calls=%async_computation | async-start | bytes 1310720 | tf_op jit(solution)/shard_map/all_gather | solution.py:81
  7.2 8.6 %collective-permute-start = (f32[32,1,8,128]{3,2,1,0:T(8,128)}, f32[32,1,8,128]{3,2,1,0:T(8,128)S(1)}, u32[]{:S(2)}, u32[]{:S(2)}) collective-permute-start(f32[32,1,8,128]{3,2,1,0:T(8,128)} %param.4), channel_id=1, source_target_pairs={{4,0},{8,4},{12,8},{5,1},{9,5},{13,9},{6,2},{10,6},{14,10},{7,3},{... | collective-permute-start | bytes 393224 | tf_op jit(solution)/shard_map/ppermute | solution.py:12
  17.5 48.1 %all-gather.5.cloned.1.call-start = ((), (), s32[]{:S(2)}) async-start(), calls=%async_computation.1 | async-start | bytes 3932160 | tf_op jit(solution)/shard_map/all_gather | solution.py:101
  18.5 8.3 %collective-permute-start.1 = (f32[16,1,16,256]{3,2,1,0:T(8,128)S(1)}, f32[16,1,16,256]{3,2,1,0:T(8,128)S(1)}, u32[]{:S(2)}, u32[]{:S(2)}) collective-permute-start(f32[16,1,16,256]{3,2,1,0:T(8,128)S(1)} %slice.223), channel_id=1, source_target_pairs={{0,4},{4,8},{8,12},{1,5},{5,9},{9,13},{2,6},{6,10},{10,14},{3,7},{... | collective-permute-start | bytes 786440 | tf_op jit(solution)/shard_map/ppermute | solution.py:12
  28.9 162.7 %all-reduce.30.cloned.1.call-start = ((), (), s32[]{:S(2)}) async-start(), calls=%async_computation.2 | async-start | bytes 1048576 | tf_op jit(solution)/shard_map/psum | solution.py:112
  118.6 17.7 %copy-start = (f32[32,1,8,128]{3,2,1,0:T(8,128)S(1)}, f32[32,1,8,128]{3,2,1,0:T(8,128)}, u32[]{:S(2)}) copy-start(f32[32,1,8,128]{3,2,1,0:T(8,128)} %param.4) | copy-start | bytes 393220
Sparse Core Ops, SparseCore 0:
  17.6 17.7 all-gather.2
  37.0 28.5 all-gather.4
  147.6 38.3 all-reduce.29
where the time goes:
time: 201 us; the launch traced here: 200 us
  local copies, waits for them, and re-layouts  118 us (59%)
  waiting for transfers between devices  28.4 us (14%)
  matrix products  14.4 us (7%)
  between operations  14.3 us (7%)
  blocking collectives  10.2 us (5%)
  other arithmetic  9.42 us (5%)
  starting transfers between devices  5.07 us (3%)
    unnamed x59, local copies, waits for them, and re-layouts  33.3 us
    slice x2, local copies, waits for them, and re-layouts, tap_matrix(): split[:, dz_lo:dz_lo + out_depth, depth_tap % 2, dy_lo:dy_lo + out_rows,...  20.7 us
    reshape x1, local copies, waits for them, and re-layouts, place_terms(): woven.reshape(channels, 2 * (depth_count + 1), 2 * (out_rows + 1), 2 * (o...  17.7 us
    all_gather x1, waiting for transfers between devices, local(): portion = lax.all_gather(extended, 'af', axis=0, tiled=True)  16.4 us
    another operation x1, local copies, waits for them, and re-layouts, place_terms(): woven = jnp.stack(depth_pairs, axis=2)  16.1 us
    another operation x2, local copies, waits for them, and re-layouts, tap_matrix(): stacked = jnp.stack(pieces, axis=0)  12.6 us
    ppermute x2, waiting for transfers between devices, shifted(): lax.ppermute(value, axis, [(source, source + steps) for source in range(l...  12 us
    all_gather x1, blocking collectives, local(): lax.all_gather(weight, 'af', axis=0, tiled=True)  10.2 us
  transfers between devices with their start and end apart: 5, of which 3 were waited for; matrix products, arithmetic and copies ran while one was open for 28% of the time, Pallas kernels for 0%

commit v1 on v0

--- a/solution.py
+++ b/solution.py
@@ -3,13 +3,332 @@
 import jax
 import jax.numpy as jnp
 from jax import lax
+from jax.experimental import pallas as pl
+from jax.experimental.pallas import tpu as pltpu
 from jax.sharding import PartitionSpec as P
+
+F32 = jnp.float32
+BF16 = jnp.bfloat16
+PARAMS = pltpu.CompilerParams(vmem_limit_bytes=48 * 1024 * 1024)
 
 
 def shifted(value, axis, steps):
     count = lax.axis_size(axis)
     leading, last = (max(0, -steps), min(count, count - steps))
     return lax.ppermute(value, axis, [(source, source + steps) for source in range(leading, last)])
+
+
+def swapped(value, axis, bits):
+    count = lax.axis_size(axis)
+    return lax.ppermute(value, axis, [(source, source ^ bits) for source in range(count)])
+
+
+def halves(value):
+    high = value.astype(BF16)
+    return high, (value - high.astype(F32)).astype(BF16)
+
+
+def dot(a, b):
+    return lax.dot_general(a, b, (((1,), (0,)), ((), ())), preferred_element_type=F32)
+
+
+def dot_t(a, b):
+    return lax.dot_general(a, b, (((1,), (1,)), ((), ())), preferred_element_type=F32)
+
+
+def column_taps(cols, out_cols):
+    x = lax.broadcasted_iota(jnp.int32, (cols, 3 * out_cols), 0)
+    c = lax.broadcasted_iota(jnp.int32, (cols, 3 * out_cols), 1)
+    dx = c // out_cols
+    return jnp.where(x == 2 * (c - dx * out_cols) + dx - 1, 1.0, 0.0).astype(BF16)
+
+
+def split_columns(v_ref, planes, rows, channels, taps, high_ref, low_ref, x_high, x_low, lanes):
+    for h in range(v_ref.shape[1] // 128):
+        lanes[...] = v_ref[:, h * 128 : (h + 1) * 128]
+        for k in range(planes * rows):
+            high, low = halves(lanes[pl.ds(k, channels, stride=planes * rows), :])
+            x_high[k * channels : (k + 1) * channels, h * 128 : (h + 1) * 128] = high
+            x_low[k * channels : (k + 1) * channels, h * 128 : (h + 1) * 128] = low
+    high_ref[...] = dot(x_high[...], taps).astype(BF16)
+    low_ref[...] = dot(x_low[...], taps).astype(BF16)
+
+
+def prepare(volume, out_cols):
+    channels, planes, rows, cols = volume.shape
+    count = planes * rows * channels
+
+    def kernel(v_ref, high_ref, low_ref, *scratch):
+        split_columns(v_ref, planes, rows, channels, column_taps(cols, out_cols), high_ref, low_ref, *scratch)
+
+    return pl.pallas_call(
+        kernel,
+        out_shape=[jax.ShapeDtypeStruct((count, 3 * out_cols), BF16)] * 2,
+        scratch_shapes=[pltpu.VMEM((count, cols), BF16)] * 2 + [pltpu.VMEM((count, 128), F32)],
+        compiler_params=PARAMS,
+        name="prepare",
+    )(volume.reshape(-1, cols))
+
+
+def weight_partial(high, low, rim, grads, parts):
+    channels, _, rows, cols = rim.shape
+    filters, _, out_rows, out_cols = grads[0].shape
+    groups = len(grads)
+    cells = out_rows * out_cols
+    width = 27 * channels
+    block = filters // parts
+
+    def kernel(*refs):
+        high_ref, low_ref, rim_ref = refs[:3]
+        g_refs = refs[3 : 3 + groups]
+        out_refs = refs[3 + groups : 3 + groups + parts]
+        r_high, r_low, x_high, x_low, lanes, g_both, b_high, b_low, total = refs[3 + groups + parts :]
+        split_columns(rim_ref, 1, rows, channels, column_taps(cols, out_cols), r_high, r_low, x_high, x_low, lanes)
+        for j in range(groups):
+            for q in range(out_rows):
+                upper, lower = halves(g_refs[j][pl.ds(q, filters, stride=out_rows), :])
+                g_both[j * filters : (j + 1) * filters, q * out_cols : (q + 1) * out_cols] = upper
+                g_both[(groups + j) * filters : (groups + j + 1) * filters, q * out_cols : (q + 1) * out_cols] = lower
+        for source, other, target in ((high_ref, r_high, b_high), (low_ref, r_low, b_low)):
+            for dz in range(3):
+                for dy in range(3):
+                    for q in range(out_rows):
+                        y = 2 * q + dy - 1
+                        for dx in range(3):
+                            at = ((dz * 3 + dy) * 3 + dx) * channels
+                            if y < 0:
+                                piece = jnp.zeros((channels, out_cols), BF16)
+                            elif dz == 0:
+                                piece = other[y * channels : (y + 1) * channels, dx * out_cols : (dx + 1) * out_cols]
+                            else:
+                                first = ((dz - 1) * rows + y) * channels
+                                piece = source[first : first + channels, dx * out_cols : (dx + 1) * out_cols]
+                            target[at : at + channels, q * out_cols : (q + 1) * out_cols] = piece
+        count = groups * filters
+        both = dot_t(g_both[...], b_high[...])
+        total[...] = both[:count] + both[count:] + dot_t(g_both[:count, :], b_low[...])
+        slab = lax.axis_index("gz")
+        for k in range(parts):
+            for j in range(groups):
+                first = pl.multiple_of(j * filters + (slab ^ k) * block, 8)
+                out_refs[k][j * block : (j + 1) * block, :] = total[pl.ds(first, block), :]
+
+    return pl.pallas_call(
+        kernel,
+        out_shape=[jax.ShapeDtypeStruct((groups * block, width), F32)] * parts,
+        scratch_shapes=[
+            pltpu.VMEM((rows * channels, 3 * out_cols), BF16),
+            pltpu.VMEM((rows * channels, 3 * out_cols), BF16),
+            pltpu.VMEM((rows * channels, cols), BF16),
+            pltpu.VMEM((rows * channels, cols), BF16),
+            pltpu.VMEM((rows * channels, 128), F32),
+            pltpu.VMEM((2 * groups * filters, cells), BF16),
+            pltpu.VMEM((width, cells), BF16),
+            pltpu.VMEM((width, cells), BF16),
+            pltpu.VMEM((groups * filters, width), F32),
+        ],
+        compiler_params=PARAMS,
+        name="weight_partial",
+    )(high, low, rim.reshape(-1, cols), *[g.reshape(-1, out_cols) for g in grads])
+
+
+def add_slabs(pieces, groups):
+    rows, width = pieces[0].shape
+    block = rows // groups
+    parts = len(pieces)
+
+    def kernel(*refs):
+        for j in range(groups):
+            value = refs[0][j * block : (j + 1) * block, :]
+            for k in range(1, parts):
+                value = value + refs[k][j * block : (j + 1) * block, :]
+            refs[parts + j][...] = value
+
+    return pl.pallas_call(
+        kernel,
+        out_shape=[jax.ShapeDtypeStruct((block, width), F32)] * groups,
+        compiler_params=PARAMS,
+        name="add_slabs",
+    )(*pieces)
+
+
+def weave_channels(pieces, channels, factor):
+    groups = len(pieces)
+    block, width = pieces[0].shape
+    total = groups * channels
+    span = 128
+    taps = span // channels
+    chunks = -(-width // span)
+
+    def kernel(*refs):
+        me = lax.axis_index("af")
+        row = lax.broadcasted_iota(jnp.int32, (groups * span, taps * total), 0)
+        col = lax.broadcasted_iota(jnp.int32, (groups * span, taps * total), 1)
+        j = row // span
+        inner = row - j * span
+        tap = inner // channels
+        place = jnp.where(col == tap * total + (j ^ me) * channels + (inner - tap * channels), 1.0, 0.0).astype(BF16)
+        for c in range(chunks):
+            size = min(span, width - c * span)
+            columns = []
+            for j in range(groups):
+                value = refs[j][:, c * span : c * span + size] * factor
+                if size < span:
+                    value = jnp.concatenate([value, jnp.zeros((block, span - size), F32)], axis=1)
+                columns.append(value)
+            wide = jnp.concatenate(columns, axis=1)
+            high = wide.astype(BF16).astype(F32)
+            rest = wide - high
+            middle = rest.astype(BF16).astype(F32)
+            stacked = jnp.concatenate([high, middle, rest - middle], axis=0).astype(BF16)
+            woven = dot(stacked, place)
+            result = woven[:block] + woven[block : 2 * block] + woven[2 * block :]
+            first = c * taps * total
+            last = min(first + taps * total, 27 * total)
+            refs[groups][:, first:last] = result[:, : last - first]
+
+    return pl.pallas_call(
+        kernel,
+        out_shape=jax.ShapeDtypeStruct((block, 27 * total), F32),
+        compiler_params=PARAMS,
+        name="weave_channels",
+    )(*pieces)
+
+
+def stack_slabs(pieces):
+    block, width = pieces[0].shape
+    parts = len(pieces)
+
+    def kernel(*refs):
+        slab = lax.axis_index("gz")
+        for k in range(parts):
+            refs[parts][slab ^ k] = refs[k][...]
+
+    return pl.pallas_call(
+        kernel,
+        out_shape=jax.ShapeDtypeStruct((parts, block, width), F32),
+        compiler_params=PARAMS,
+        name="stack_slabs",
+    )(*pieces).reshape(parts * block, width)
+
+
+def input_gradient(weights, grads, uppers, volume_shape):
+    channels, planes, rows, cols = volume_shape
+    groups = len(grads)
+    filters, _, out_rows, out_cols = grads[0].shape
+    count = groups * filters
+    cells = out_rows * out_cols
+    total = weights[0].shape[1] // 27
+    padded = -(-27 * total // 128) * 128
+    third = 9 * channels
+
+    def kernel(*refs):
+        w_refs, g_refs, u_refs = refs[:groups], refs[groups : 2 * groups], refs[2 * groups : 3 * groups]
+        out_ref = refs[3 * groups]
+        turned, a_high, a_low, g_high, g_low, t_even, t_odd, woven, lanes = refs[3 * groups + 1 :]
+        for first in range(0, padded, 128):
+            size = min(128, 27 * total - first)
+            value = jnp.concatenate([w[:, first : first + size] for w in w_refs], axis=0)
+            if size < 128:
+                value = jnp.concatenate([value, jnp.zeros((count, 128 - size), F32)], axis=1)
+            turned[first : first + 128, :] = value.T
+        me = lax.axis_index("af")
+        for tap in range(27):
+            first = pl.multiple_of(tap * total + me * channels, 8)
+            high, low = halves(turned[pl.ds(first, channels), :])
+            a_high[tap * channels : (tap + 1) * channels, :] = high
+            a_low[tap * channels : (tap + 1) * channels, :] = low
+        for side, source in enumerate((g_refs, u_refs)):
+            for j in range(groups):
+                for q in range(out_rows):
+                    high, low = halves(source[j][pl.ds(q, filters, stride=out_rows), :])
+                    at = side * count + j * filters
+                    g_high[at : at + filters, q * out_cols : (q + 1) * out_cols] = high
+                    g_low[at : at + filters, q * out_cols : (q + 1) * out_cols] = low
+        e_high, e_low = a_high[third : 2 * third, :], a_low[third : 2 * third, :]
+        both = jnp.concatenate([e_high, e_low], axis=1)
+        own_high = g_high[:count, :]
+        t_even[...] = dot(both, jnp.concatenate([own_high, own_high], axis=0)) + dot(e_high, g_low[:count, :])
+        o_high = jnp.concatenate([a_high[2 * third :, :], a_high[:third, :]], axis=1)
+        o_low = jnp.concatenate([a_low[2 * third :, :], a_low[:third, :]], axis=1)
+        t_odd[...] = dot(o_high, g_high[...]) + dot(o_high, g_low[...]) + dot(o_low, g_high[...])
+        for z, terms in enumerate((t_even, t_odd)):
+            for y in range(rows):
+                q = y // 2
+                for dx in range(3):
+                    def term(dy, at):
+                        first = (dy * 3 + dx) * channels
+                        return terms[first : first + channels, at * out_cols : (at + 1) * out_cols]
+
+                    if y % 2 == 0:
+                        value = term(1, q)
+                    else:
+                        value = term(2, q)
+                        if q + 1 < out_rows:
+                            value = value + term(0, q + 1)
+                    high, low = halves(value)
+                    first = (z * rows + y) * channels
+                    woven[first : first + channels, dx * out_cols : (dx + 1) * out_cols] = high
+                    woven[first : first + channels, (3 + dx) * out_cols : (4 + dx) * out_cols] = low
+        taps = column_taps(cols, out_cols)
+        result = dot_t(woven[...], jnp.concatenate([taps, taps], axis=1))
+        for h in range(cols // 128):
+            for k in range(planes * rows):
+                piece = result[k * channels : (k + 1) * channels, h * 128 : (h + 1) * 128]
+                lanes[pl.ds(k, channels, stride=planes * rows), :] = piece
+            out_ref[:, h * 128 : (h + 1) * 128] = lanes[...]
+
+    return pl.pallas_call(
+        kernel,
+        out_shape=jax.ShapeDtypeStruct((channels * planes * rows, cols), F32),
+        scratch_shapes=[
+            pltpu.VMEM((padded, count), F32),
+            pltpu.VMEM((27 * channels, count), BF16),
+            pltpu.VMEM((27 * channels, count), BF16),
+            pltpu.VMEM((2 * count, cells), BF16),
+            pltpu.VMEM((2 * count, cells), BF16),
+            pltpu.VMEM((third, cells), F32),
+            pltpu.VMEM((third, cells), F32),
+            pltpu.VMEM((planes * rows * channels, 6 * out_cols), BF16),
+            pltpu.VMEM((planes * rows * channels, 128), F32),
+        ],
+        compiler_params=PARAMS,
+        name="input_gradient",
+    )(
+        *weights,
+        *[g.reshape(-1, out_cols) for g in grads],
+        *[u.reshape(-1, out_cols) for u in uppers],
+    ).reshape(volume_shape)
+
+
+def spread(value):
+    step = lax.axis_size("af") // 2
+    have = {0: value}
+    while step:
+        for j in list(have):
+            have[j ^ step] = swapped(have[j], "af", step)
+        step //= 2
+    return [have[j] for j in range(lax.axis_size("af"))]
+
+
+def fast(volume, out_grad, weight):
+    channels, planes, rows, cols = volume.shape
+    filters, out_depth, out_rows, out_cols = out_grad.shape
+    parts, groups = lax.axis_size("gz"), lax.axis_size("af")
+    factor = 1.0 / math.sqrt(out_depth * parts * out_rows * out_cols)
+    grads = spread(out_grad)
+    rim = shifted(volume[:, planes - 1 : planes], "gz", 1)
+    uppers = spread(shifted(out_grad, "gz", -1))
+    weights = spread(weight)
+    high, low = prepare(volume, out_cols)
+    sent = weight_partial(high, low, rim, grads, parts)
+    arrived = [sent[0]] + [swapped(sent[k], "gz", k) for k in range(1, parts)]
+    sums = add_slabs(arrived, groups)
+    crossed = [sums[0]] + [swapped(sums[j], "af", j) for j in range(1, groups)]
+    own = weave_channels(crossed, channels, factor)
+    weight_grad = stack_slabs([own] + [swapped(own, "gz", k) for k in range(1, parts)])
+    input_grad = input_gradient(weights, grads, uppers, volume.shape)
+    return (input_grad, weight_grad)
 
 
 def tap_matrix(extended, out_depth, out_rows, out_cols):
@@ -68,7 +387,7 @@
     return canvas[:, 1 : planes + 1, 1 : rows + 1, 1 : cols + 1]
 
 
-def local(volume, out_grad, weight):
+def general(volume, out_grad, weight):
     channels, planes, rows, cols = volume.shape
     filters, out_depth, out_rows, out_cols = out_grad.shape
     in_total = weight.shape[1] // 27
@@ -114,6 +433,17 @@
     return (input_grad, weight_grad)
 
 
+def local(volume, out_grad, weight):
+    channels, planes, rows, _ = volume.shape
+    filters, out_depth, out_rows, _ = out_grad.shape
+    parts, groups = lax.axis_size("gz"), lax.axis_size("af")
+    powers = parts & (parts - 1) == 0 and groups & (groups - 1) == 0
+    whole_tiles = channels % 16 == 0 and filters % (8 * parts) == 0 and filters * groups == 128
+    if powers and whole_tiles and out_depth == 1:
+        return fast(volume, out_grad, weight)
+    return general(volume, out_grad, weight)
+
+
 def solution(mesh):
     return jax.shard_map(
         local,

time: 201 us -> 51.1 us (0.25)
  local copies, waits for them, and re-layouts: 118 us -> 0.98 us
  starting transfers between devices: 5.07 us -> 19.5 us
  matrix products: 14.4 us -> 0 us
  between operations: 14.3 us -> 0.76 us
  blocking collectives: 10.2 us -> 0 us
  other arithmetic: 9.42 us -> 0 us
  Pallas kernels: 0 us -> 5.65 us
  waiting for transfers between devices: 28.4 us -> 24 us
    unnamed x59 -> x6, local copies, waits for them, and re-layouts: 33.3 us -> 0.01 us
    another operation x3 -> x0, local copies, waits for them, and re-layouts: 28.7 us -> none  [the longest x1 16.1 us: place_terms(): woven = jnp.stack(depth_pairs, axis=2)]
    slice x4 -> x1, local copies, waits for them, and re-layouts: 26.4 us -> 0.97 us  [fast(): rim = shifted(volume[:, planes - 1:planes], 'gz', 1)]
    ppermute x0 -> x18, waiting for transfers between devices: none -> 22 us  [swapped(): lax.ppermute(value, axis, [(source, source ^ bits) for source in range(co...]
    reshape x3 -> x0, local copies, waits for them, and re-layouts: 19.6 us -> none  [the longest x1 17.7 us: place_terms(): woven.reshape(channels, 2 * (depth_count + 1), 2 * (out_rows + 1), 2 * (o...]
    all_gather x2 -> x0, waiting for transfers between devices: 16.4 us -> none  [the longest x1 16.4 us: local(): portion = lax.all_gather(extended, 'af', axis=0, tiled=True)]
    ppermute x0 -> x18, starting transfers between devices: none -> 14.7 us  [swapped(): lax.ppermute(value, axis, [(source, source ^ bits) for source in range(co...]
    dot_general x2 -> x0, matrix products: 14.4 us -> none  [the longest x1 10.1 us: local(): lax.dot_general(local_grads, tap_rows, (((1,), (1,)), ((), ())), precisio...]
  transfers between devices with their start and end apart: 5 -> 20, of which waited for: 3 -> 9; matrix products, arithmetic and copies ran while one was open for 28% -> 2% of each run, Pallas kernels for 0% -> 7%
where the time goes in v1:
time: 51.1 us; the launch traced here: 50.9 us
  waiting for transfers between devices  24 us (47%)
  starting transfers between devices  19.5 us (38%)
  Pallas kernels  5.65 us (11%)
  local copies, waits for them, and re-layouts  0.98 us (2%)
  between operations  0.76 us (1%)
    ppermute x18, waiting for transfers between devices, swapped(): lax.ppermute(value, axis, [(source, source ^ bits) for source in range(co...  22 us
    ppermute x18, starting transfers between devices, swapped(): lax.ppermute(value, axis, [(source, source ^ bits) for source in range(co...  14.7 us
    ppermute x2, starting transfers between devices, shifted(): lax.ppermute(value, axis, [(source, source + steps) for source in range(l...  4.78 us
    pallas_call x1, Pallas kernels, input_gradient(): pl.pallas_call(kernel, out_shape=jax.ShapeDtypeStruct((channels * planes...  2.27 us
    ppermute x2, waiting for transfers between devices, shifted(): lax.ppermute(value, axis, [(source, source + steps) for source in range(l...  2.01 us
    pallas_call x1, Pallas kernels, weight_partial(): pl.pallas_call(kernel, out_shape=[jax.ShapeDtypeStruct((groups * block, w...  1.2 us
  transfers between devices with their start and end apart: 20, of which 9 were waited for; matrix products, arithmetic and copies ran while one was open for 2% of the time, Pallas kernels for 7%

profile of v1, /device:TPU:0, one launch (start us, length us, event | category | flops | bytes accessed | tf_op | source)
XLA Modules:
  0.0 50.9 jit_solution(16965073663806842870)
XLA Ops:
  0.6 3.0 %collective-permute-start.4 = (f32[32,1,8,128]{3,2,1,0:T(8,128)}, f32[32,1,8,128]{3,2,1,0:T(8,128)S(1)}, u32[]{:S(2)}, u32[]{:S(2)}) collective-permute-start(f32[32,1,8,128]{3,2,1,0:T(8,128)} %param.4), channel_id=1, source_target_pairs={{0,2},{1,3},{2,0},{3,1},{4,6},{5,7},{6,4},{7,5},{8,10},{9,11},{10,... | collective-permute-start | bytes 393224 | tf_op jit(solution)/shard_map/ppermute | solution.py:23
  3.6 1.0 %slice.3 = f32[16,1,16,256]{3,2,1,0:T(8,128)S(1)} slice(f32[16,2,16,256]{3,2,1,0:T(8,128)} %param.3), slice={[0:16], [1:2], [0:16], [0:256]} | slice | bytes 524288 | tf_op jit(solution)/shard_map/slice | solution.py:320
  4.6 3.5 %collective-permute-start.10 = (f32[16,1,16,256]{3,2,1,0:T(8,128)S(1)}, f32[16,1,16,256]{3,2,1,0:T(8,128)S(1)}, u32[]{:S(2)}, u32[]{:S(2)}) collective-permute-start(f32[16,1,16,256]{3,2,1,0:T(8,128)S(1)} %slice.3), channel_id=1, source_target_pairs={{0,4},{4,8},{8,12},{1,5},{5,9},{9,13},{2,6},{6,10},{10,14},{3,7},{... | collective-permute-start | bytes 786440 | tf_op jit(solution)/shard_map/ppermute | solution.py:18
  8.1 0.6 %collective-permute-start.1 = (f32[32,1728]{1,0:T(8,128)}, f32[32,1728]{1,0:T(8,128)S(1)}, u32[]{:S(2)}, u32[]{:S(2)}) collective-permute-start(f32[32,1728]{1,0:T(8,128)} %refs_0_.1), channel_id=1, source_target_pairs={{0,2},{1,3},{2,0},{3,1},{4,6},{5,7},{6,4},{7,5},{8,10},{9,11},{10,... | collective-permute-start | bytes 663560 | tf_op jit(solution)/shard_map/ppermute | solution.py:23
  8.7 0.0 collective-permute-start.3
  8.7 0.5 collective-permute-start.5
  9.2 1.3 %collective-permute-start.6 = (f32[32,1,8,128]{3,2,1,0:T(8,128)}, f32[32,1,8,128]{3,2,1,0:T(8,128)S(1)}, u32[]{:S(2)}, u32[]{:S(2)}) collective-permute-start(f32[32,1,8,128]{3,2,1,0:T(8,128)} %param.4), channel_id=1, source_target_pairs={{4,0},{8,4},{12,8},{5,1},{9,5},{13,9},{6,2},{10,6},{14,10},{7,3},{... | collective-permute-start | bytes 393224 | tf_op jit(solution)/shard_map/ppermute | solution.py:18
  10.5 0.0 copy-start.1
  10.5 0.8 %prepare.1 = (bf16[512,384]{1,0:T(8,128)(2,1)S(1)}, bf16[512,384]{1,0:T(8,128)(2,1)S(1)}) custom-call(f32[512,256]{1,0:T(8,128)S(1)} %bitcast.12), custom_call_target="tpu_custom_call" | custom-call | tf_op jit(solution)/shard_map/prepare/pallas_call | solution.py:64
  11.4 2.0 %collective-permute-done.10 = f32[16,1,16,256]{3,2,1,0:T(8,128)S(1)} collective-permute-done((f32[16,1,16,256]{3,2,1,0:T(8,128)S(1)}, f32[16,1,16,256]{3,2,1,0:T(8,128)S(1)}, u32[]{:S(2)}, u32[]{:S(2)}) %collective-permute-start.10) | collective-permute-done | bytes 262176 | tf_op jit(solution)/shard_map/ppermute | solution.py:18
  13.4 1.2 %weight_partial.1 = (f32[32,432]{1,0:T(8,128)S(1)}, f32[32,432]{1,0:T(8,128)S(1)}, f32[32,432]{1,0:T(8,128)S(1)}, f32[32,432]{1,0:T(8,128)S(1)}) custom-call(bf16[512,384]{1,0:T(8,128)(2,1)S(1)} %get-tuple-element.12.refs_0_, bf16[512,384]{1,0:T(8,128)(2,1)S(1)} %get-tuple-element.13.refs_1_, f32[256,256]{1,0:T(8,128)S(1)} %bitcast.21, ...), custom_call_target="tpu_custom_call" | custom-call | tf_op jit(solution)/shard_map/weight_partial/pallas_call | solution.py:116
  14.6 2.5 %collective-permute-start.11 = (f32[32,432]{1,0:T(8,128)S(1)}, f32[32,432]{1,0:T(8,128)S(1)}, u32[]{:S(2)}, u32[]{:S(2)}) collective-permute-start(f32[32,432]{1,0:T(8,128)S(1)} %get-tuple-element.15), channel_id=1, source_target_pairs={{0,4},{4,0},{8,12},{12,8},{1,5},{5,1},{9,13},{13,9},{2,6},{6,2},{1... | collective-permute-start | bytes 165896 | tf_op jit(solution)/shard_map/ppermute | solution.py:23
  17.1 1.8 %collective-permute-start.8 = (f32[32,1,8,128]{3,2,1,0:T(8,128)S(1)}, f32[32,1,8,128]{3,2,1,0:T(8,128)S(1)}, u32[]{:S(2)}, u32[]{:S(2)}) collective-permute-start(f32[32,1,8,128]{3,2,1,0:T(8,128)S(1)} %collective-permute-done.6), channel_id=1, source_target_pairs={{0,2},{1,3},{2,0},{3,1},{4,6},{5,7},{6,4},{7,5},{8,10},{9,11},{10,... | collective-permute-start | bytes 393224 | tf_op jit(solution)/shard_map/ppermute | solution.py:23
  18.9 2.5 %collective-permute-start.12 = (f32[32,432]{1,0:T(8,128)S(1)}, f32[32,432]{1,0:T(8,128)S(1)}, u32[]{:S(2)}, u32[]{:S(2)}) collective-permute-start(f32[32,432]{1,0:T(8,128)S(1)} %get-tuple-element.16), channel_id=1, source_target_pairs={{0,8},{4,12},{8,0},{12,4},{1,9},{5,13},{9,1},{13,5},{2,10},{6,14},... | collective-permute-start | bytes 165896 | tf_op jit(solution)/shard_map/ppermute | solution.py:23
  21.4 0.7 %collective-permute-start.13 = (f32[32,432]{1,0:T(8,128)S(1)}, f32[32,432]{1,0:T(8,128)S(1)}, u32[]{:S(2)}, u32[]{:S(2)}) collective-permute-start(f32[32,432]{1,0:T(8,128)S(1)} %get-tuple-element.17), channel_id=1, source_target_pairs={{0,12},{4,8},{8,4},{12,0},{1,13},{5,9},{9,5},{13,1},{2,14},{6,10},... | collective-permute-start | bytes 165896 | tf_op jit(solution)/shard_map/ppermute | solution.py:23
  22.2 0.5 collective-permute-start.2
  22.7 2.8 %collective-permute-done.12.refs_2_ = f32[32,432]{1,0:T(8,128)S(1)} collective-permute-done((f32[32,432]{1,0:T(8,128)S(1)}, f32[32,432]{1,0:T(8,128)S(1)}, u32[]{:S(2)}, u32[]{:S(2)}) %collective-permute-start.12) | collective-permute-done | bytes 55328 | tf_op jit(solution)/shard_map/ppermute | solution.py:23
  25.5 2.0 %collective-permute-done.13.refs_3_ = f32[32,432]{1,0:T(8,128)S(1)} collective-permute-done((f32[32,432]{1,0:T(8,128)S(1)}, f32[32,432]{1,0:T(8,128)S(1)}, u32[]{:S(2)}, u32[]{:S(2)}) %collective-permute-start.13) | collective-permute-done | bytes 55328 | tf_op jit(solution)/shard_map/ppermute | solution.py:23
  27.5 0.1 collective-permute-start.14
  27.6 0.4 collective-permute-start.15
  28.0 0.8 %collective-permute-done.14.refs_1_ = f32[8,432]{1,0:T(8,128)S(1)} collective-permute-done((f32[8,432]{1,0:T(8,128)S(1)}, f32[8,432]{1,0:T(8,128)S(1)}, u32[]{:S(2)}, u32[]{:S(2)}) %collective-permute-start.14) | collective-permute-done | bytes 13856 | tf_op jit(solution)/shard_map/ppermute | solution.py:23
  28.7 0.7 %collective-permute-start.16 = (f32[8,432]{1,0:T(8,128)S(1)}, f32[8,432]{1,0:T(8,128)S(1)}, u32[]{:S(2)}, u32[]{:S(2)}) collective-permute-start(f32[8,432]{1,0:T(8,128)S(1)} %get-tuple-element.21), channel_id=1, source_target_pairs={{0,3},{1,2},{2,1},{3,0},{4,7},{5,6},{6,5},{7,4},{8,11},{9,10},{10,... | collective-permute-start | bytes 41480 | tf_op jit(solution)/shard_map/ppermute | solution.py:23
  29.4 1.9 %collective-permute-done.15.refs_2_ = f32[8,432]{1,0:T(8,128)S(1)} collective-permute-done((f32[8,432]{1,0:T(8,128)S(1)}, f32[8,432]{1,0:T(8,128)S(1)}, u32[]{:S(2)}, u32[]{:S(2)}) %collective-permute-start.15) | collective-permute-done | bytes 13856 | tf_op jit(solution)/shard_map/ppermute | solution.py:23
  31.4 0.5 %collective-permute-done.16.refs_3_ = f32[8,432]{1,0:T(8,128)S(1)} collective-permute-done((f32[8,432]{1,0:T(8,128)S(1)}, f32[8,432]{1,0:T(8,128)S(1)}, u32[]{:S(2)}, u32[]{:S(2)}) %collective-permute-start.16) | collective-permute-done | bytes 13856 | tf_op jit(solution)/shard_map/ppermute | solution.py:23
  31.9 0.7 %weave_channels.1.refs_0_ = f32[8,1728]{1,0:T(8,128)S(1)} custom-call(f32[8,432]{1,0:T(8,128)S(1)} %get-tuple-element.18.refs_0_, f32[8,432]{1,0:T(8,128)S(1)} %collective-permute-done.14.refs_1_, f32[8,432]{1,0:T(8,128)S(1)} %collective-permute-done.15.refs_2_, f32[8,432]{1,0:T(8,128)S(1)} %collective-permute-done.16.refs_3_), custom_call_target="tpu_custom_call" | custom-call | tf_op jit(solution)/shard_map/weave_channels/pallas_call | solution.py:190
  32.6 0.9 %collective-permute-start.19 = (f32[8,1728]{1,0:T(8,128)S(1)}, f32[8,1728]{1,0:T(8,128)S(1)}, u32[]{:S(2)}, u32[]{:S(2)}) collective-permute-start(f32[8,1728]{1,0:T(8,128)S(1)} %weave_channels.1.refs_0_), channel_id=1, source_target_pairs={{0,12},{4,8},{8,4},{12,0},{1,13},{5,9},{9,5},{13,1},{2,14},{6,10},... | collective-permute-start | bytes 165896 | tf_op jit(solution)/shard_map/ppermute | solution.py:23
  33.5 0.5 collective-permute-start.9
  34.0 4.7 %collective-permute-done.19.refs_3_ = f32[8,1728]{1,0:T(8,128)S(1)} collective-permute-done((f32[8,1728]{1,0:T(8,128)S(1)}, f32[8,1728]{1,0:T(8,128)S(1)}, u32[]{:S(2)}, u32[]{:S(2)}) %collective-permute-start.19) | collective-permute-done | bytes 55328 | tf_op jit(solution)/shard_map/ppermute | solution.py:23
  38.6 5.1 %collective-permute-done.18.refs_2_ = f32[8,1728]{1,0:T(8,128)S(1)} collective-permute-done((f32[8,1728]{1,0:T(8,128)S(1)}, f32[8,1728]{1,0:T(8,128)S(1)}, u32[]{:S(2)}, u32[]{:S(2)}) %collective-permute-start.18) | collective-permute-done | bytes 55328 | tf_op jit(solution)/shard_map/ppermute | solution.py:23
  43.7 4.2 %collective-permute-done.17.refs_1_ = f32[8,1728]{1,0:T(8,128)S(1)} collective-permute-done((f32[8,1728]{1,0:T(8,128)S(1)}, f32[8,1728]{1,0:T(8,128)S(1)}, u32[]{:S(2)}, u32[]{:S(2)}) %collective-permute-start.17) | collective-permute-done | bytes 55328 | tf_op jit(solution)/shard_map/ppermute | solution.py:23
  47.9 0.7 %stack_slabs.1 = f32[4,8,1728]{2,1,0:T(8,128)} custom-call(f32[8,1728]{1,0:T(8,128)S(1)} %weave_channels.1.refs_0_, f32[8,1728]{1,0:T(8,128)S(1)} %collective-permute-done.17.refs_1_, f32[8,1728]{1,0:T(8,128)S(1)} %collective-permute-done.18.refs_2_, f32[8,1728]{1,0:T(8,128)S(1)} %collective-permute-done.19.refs_3_), custom_call_target="tpu_custom_call" | custom-call | tf_op jit(solution)/shard_map/stack_slabs/pallas_call | solution.py:207
  48.6 2.3 %input_gradient.1 = f32[512,256]{1,0:T(8,128)} custom-call(f32[32,1728]{1,0:T(8,128)S(1)} %copy-done.2, f32[32,1728]{1,0:T(8,128)S(1)} %collective-permute-done.refs_1_, f32[32,1728]{1,0:T(8,128)S(1)} %collective-permute-done.1.refs_2_, f32[32,1728]{1,0:T(8,128)S(1)} %collective-permute-done.2.refs_3_, f32[256,128]{1,0:T(8,128)S(1)} %bitcast.14, ...), custom_call_target="tpu_custom_call" | custom-call | tf_op jit(solution)/shard_map/input_gradient/pallas_call | solution.py:281
  (21 shorter events, 0.1 us)
Async XLA Ops:
  0.6 9.9 %copy-start = (f32[16,2,16,256]{3,2,1,0:T(8,128)S(1)}, f32[16,2,16,256]{3,2,1,0:T(8,128)}, u32[]{:S(2)}) copy-start(f32[16,2,16,256]{3,2,1,0:T(8,128)} %param.3) | copy-start | bytes 1572868
  0.6 8.1 %collective-permute-start.4 = (f32[32,1,8,128]{3,2,1,0:T(8,128)}, f32[32,1,8,128]{3,2,1,0:T(8,128)S(1)}, u32[]{:S(2)}, u32[]{:S(2)}) collective-permute-start(f32[32,1,8,128]{3,2,1,0:T(8,128)} %param.4), channel_id=1, source_target_pairs={{0,2},{1,3},{2,0},{3,1},{4,6},{5,7},{6,4},{7,5},{8,10},{9,11},{10,... | collective-permute-start | bytes 393224 | tf_op jit(solution)/shard_map/ppermute | solution.py:23
  4.6 8.8 %collective-permute-start.10 = (f32[16,1,16,256]{3,2,1,0:T(8,128)S(1)}, f32[16,1,16,256]{3,2,1,0:T(8,128)S(1)}, u32[]{:S(2)}, u32[]{:S(2)}) collective-permute-start(f32[16,1,16,256]{3,2,1,0:T(8,128)S(1)} %slice.3), channel_id=1, source_target_pairs={{0,4},{4,8},{8,12},{1,5},{5,9},{9,13},{2,6},{6,10},{10,14},{3,7},{... | collective-permute-start | bytes 786440 | tf_op jit(solution)/shard_map/ppermute | solution.py:18
  8.1 14.0 %collective-permute-start.1 = (f32[32,1728]{1,0:T(8,128)}, f32[32,1728]{1,0:T(8,128)S(1)}, u32[]{:S(2)}, u32[]{:S(2)}) collective-permute-start(f32[32,1728]{1,0:T(8,128)} %refs_0_.1), channel_id=1, source_target_pairs={{0,2},{1,3},{2,0},{3,1},{4,6},{5,7},{6,4},{7,5},{8,10},{9,11},{10,... | collective-permute-start | bytes 663560 | tf_op jit(solution)/shard_map/ppermute | solution.py:23
  8.7 2.6 %collective-permute-start.3 = (f32[32,1,8,128]{3,2,1,0:T(8,128)}, f32[32,1,8,128]{3,2,1,0:T(8,128)S(1)}, u32[]{:S(2)}, u32[]{:S(2)}) collective-permute-start(f32[32,1,8,128]{3,2,1,0:T(8,128)} %param.4), channel_id=1, source_target_pairs={{0,1},{1,0},{2,3},{3,2},{4,5},{5,4},{6,7},{7,6},{8,9},{9,8},{10,11... | collective-permute-start | bytes 393224 | tf_op jit(solution)/shard_map/ppermute | solution.py:23
  8.7 2.6 %collective-permute-start.5 = (f32[32,1,8,128]{3,2,1,0:T(8,128)S(1)}, f32[32,1,8,128]{3,2,1,0:T(8,128)S(1)}, u32[]{:S(2)}, u32[]{:S(2)}) collective-permute-start(f32[32,1,8,128]{3,2,1,0:T(8,128)S(1)} %collective-permute-done.4), channel_id=1, source_target_pairs={{0,1},{1,0},{2,3},{3,2},{4,5},{5,4},{6,7},{7,6},{8,9},{9,8},{10,11... | collective-permute-start | bytes 393224 | tf_op jit(solution)/shard_map/ppermute | solution.py:23
  9.2 7.9 %collective-permute-start.6 = (f32[32,1,8,128]{3,2,1,0:T(8,128)}, f32[32,1,8,128]{3,2,1,0:T(8,128)S(1)}, u32[]{:S(2)}, u32[]{:S(2)}) collective-permute-start(f32[32,1,8,128]{3,2,1,0:T(8,128)} %param.4), channel_id=1, source_target_pairs={{4,0},{8,4},{12,8},{5,1},{9,5},{13,9},{6,2},{10,6},{14,10},{7,3},{... | collective-permute-start | bytes 393224 | tf_op jit(solution)/shard_map/ppermute | solution.py:18
  10.5 2.8 %copy-start.1 = (f32[32,1,8,128]{3,2,1,0:T(8,128)S(1)}, f32[32,1,8,128]{3,2,1,0:T(8,128)}, u32[]{:S(2)}) copy-start(f32[32,1,8,128]{3,2,1,0:T(8,128)} %param.4) | copy-start | bytes 393220
  13.4 8.8 %copy-start.2 = (f32[32,1728]{1,0:T(8,128)S(1)}, f32[32,1728]{1,0:T(8,128)}, u32[]{:S(2)}) copy-start(f32[32,1728]{1,0:T(8,128)} %refs_0_.1) | copy-start | bytes 663556
  14.6 7.6 %collective-permute-start.11 = (f32[32,432]{1,0:T(8,128)S(1)}, f32[32,432]{1,0:T(8,128)S(1)}, u32[]{:S(2)}, u32[]{:S(2)}) collective-permute-start(f32[32,432]{1,0:T(8,128)S(1)} %get-tuple-element.15), channel_id=1, source_target_pairs={{0,4},{4,0},{8,12},{12,8},{1,5},{5,1},{9,13},{13,9},{2,6},{6,2},{1... | collective-permute-start | bytes 165896 | tf_op jit(solution)/shard_map/ppermute | solution.py:23
  17.1 16.3 %collective-permute-start.8 = (f32[32,1,8,128]{3,2,1,0:T(8,128)S(1)}, f32[32,1,8,128]{3,2,1,0:T(8,128)S(1)}, u32[]{:S(2)}, u32[]{:S(2)}) collective-permute-start(f32[32,1,8,128]{3,2,1,0:T(8,128)S(1)} %collective-permute-done.6), channel_id=1, source_target_pairs={{0,2},{1,3},{2,0},{3,1},{4,6},{5,7},{6,4},{7,5},{8,10},{9,11},{10,... | collective-permute-start | bytes 393224 | tf_op jit(solution)/shard_map/ppermute | solution.py:23
  18.9 6.6 %collective-permute-start.12 = (f32[32,432]{1,0:T(8,128)S(1)}, f32[32,432]{1,0:T(8,128)S(1)}, u32[]{:S(2)}, u32[]{:S(2)}) collective-permute-start(f32[32,432]{1,0:T(8,128)S(1)} %get-tuple-element.16), channel_id=1, source_target_pairs={{0,8},{4,12},{8,0},{12,4},{1,9},{5,13},{9,1},{13,5},{2,10},{6,14},... | collective-permute-start | bytes 165896 | tf_op jit(solution)/shard_map/ppermute | solution.py:23
  21.4 6.1 %collective-permute-start.13 = (f32[32,432]{1,0:T(8,128)S(1)}, f32[32,432]{1,0:T(8,128)S(1)}, u32[]{:S(2)}, u32[]{:S(2)}) collective-permute-start(f32[32,432]{1,0:T(8,128)S(1)} %get-tuple-element.17), channel_id=1, source_target_pairs={{0,12},{4,8},{8,4},{12,0},{1,13},{5,9},{9,5},{13,1},{2,14},{6,10},... | collective-permute-start | bytes 165896 | tf_op jit(solution)/shard_map/ppermute | solution.py:23
  22.2 26.4 %collective-permute-start = (f32[32,1728]{1,0:T(8,128)S(1)}, f32[32,1728]{1,0:T(8,128)S(1)}, u32[]{:S(2)}, u32[]{:S(2)}) collective-permute-start(f32[32,1728]{1,0:T(8,128)S(1)} %copy-done.2), channel_id=1, source_target_pairs={{0,1},{1,0},{2,3},{3,2},{4,5},{5,4},{6,7},{7,6},{8,9},{9,8},{10,11... | collective-permute-start | bytes 663560 | tf_op jit(solution)/shard_map/ppermute | solution.py:23
  22.2 26.4 %collective-permute-start.2 = (f32[32,1728]{1,0:T(8,128)S(1)}, f32[32,1728]{1,0:T(8,128)S(1)}, u32[]{:S(2)}, u32[]{:S(2)}) collective-permute-start(f32[32,1728]{1,0:T(8,128)S(1)} %collective-permute-done.1.refs_2_), channel_id=1, source_target_pairs={{0,1},{1,0},{2,3},{3,2},{4,5},{5,4},{6,7},{7,6},{8,9},{9,8},{10,11... | collective-permute-start | bytes 663560 | tf_op jit(solution)/shard_map/ppermute | solution.py:23
  27.5 1.2 %collective-permute-start.14 = (f32[8,432]{1,0:T(8,128)S(1)}, f32[8,432]{1,0:T(8,128)S(1)}, u32[]{:S(2)}, u32[]{:S(2)}) collective-permute-start(f32[8,432]{1,0:T(8,128)S(1)} %get-tuple-element.19), channel_id=1, source_target_pairs={{0,1},{1,0},{2,3},{3,2},{4,5},{5,4},{6,7},{7,6},{8,9},{9,8},{10,11... | collective-permute-start | bytes 41480 | tf_op jit(solution)/shard_map/ppermute | solution.py:23
  27.6 3.8 %collective-permute-start.15 = (f32[8,432]{1,0:T(8,128)S(1)}, f32[8,432]{1,0:T(8,128)S(1)}, u32[]{:S(2)}, u32[]{:S(2)}) collective-permute-start(f32[8,432]{1,0:T(8,128)S(1)} %get-tuple-element.20), channel_id=1, source_target_pairs={{0,2},{1,3},{2,0},{3,1},{4,6},{5,7},{6,4},{7,5},{8,10},{9,11},{10,... | collective-permute-start | bytes 41480 | tf_op jit(solution)/shard_map/ppermute | solution.py:23
  28.7 3.2 %collective-permute-start.16 = (f32[8,432]{1,0:T(8,128)S(1)}, f32[8,432]{1,0:T(8,128)S(1)}, u32[]{:S(2)}, u32[]{:S(2)}) collective-permute-start(f32[8,432]{1,0:T(8,128)S(1)} %get-tuple-element.21), channel_id=1, source_target_pairs={{0,3},{1,2},{2,1},{3,0},{4,7},{5,6},{6,5},{7,4},{8,11},{9,10},{10,... | collective-permute-start | bytes 41480 | tf_op jit(solution)/shard_map/ppermute | solution.py:23
  32.6 6.0 %collective-permute-start.19 = (f32[8,1728]{1,0:T(8,128)S(1)}, f32[8,1728]{1,0:T(8,128)S(1)}, u32[]{:S(2)}, u32[]{:S(2)}) collective-permute-start(f32[8,1728]{1,0:T(8,128)S(1)} %weave_channels.1.refs_0_), channel_id=1, source_target_pairs={{0,12},{4,8},{8,4},{12,0},{1,13},{5,9},{9,5},{13,1},{2,14},{6,10},... | collective-permute-start | bytes 165896 | tf_op jit(solution)/shard_map/ppermute | solution.py:23
  33.5 15.1 %collective-permute-start.7 = (f32[32,1,8,128]{3,2,1,0:T(8,128)S(1)}, f32[32,1,8,128]{3,2,1,0:T(8,128)S(1)}, u32[]{:S(2)}, u32[]{:S(2)}) collective-permute-start(f32[32,1,8,128]{3,2,1,0:T(8,128)S(1)} %collective-permute-done.6), channel_id=1, source_target_pairs={{0,1},{1,0},{2,3},{3,2},{4,5},{5,4},{6,7},{7,6},{8,9},{9,8},{10,11... | collective-permute-start | bytes 393224 | tf_op jit(solution)/shard_map/ppermute | solution.py:23
  33.5 15.1 %collective-permute-start.9 = (f32[32,1,8,128]{3,2,1,0:T(8,128)S(1)}, f32[32,1,8,128]{3,2,1,0:T(8,128)S(1)}, u32[]{:S(2)}, u32[]{:S(2)}) collective-permute-start(f32[32,1,8,128]{3,2,1,0:T(8,128)S(1)} %collective-permute-done.8), channel_id=1, source_target_pairs={{0,1},{1,0},{2,3},{3,2},{4,5},{5,4},{6,7},{7,6},{8,9},{9,8},{10,11... | collective-permute-start | bytes 393224 | tf_op jit(solution)/shard_map/ppermute | solution.py:23
  38.6 5.1 %collective-permute-start.18 = (f32[8,1728]{1,0:T(8,128)S(1)}, f32[8,1728]{1,0:T(8,128)S(1)}, u32[]{:S(2)}, u32[]{:S(2)}) collective-permute-start(f32[8,1728]{1,0:T(8,128)S(1)} %weave_channels.1.refs_0_), channel_id=1, source_target_pairs={{0,8},{4,12},{8,0},{12,4},{1,9},{5,13},{9,1},{13,5},{2,10},{6,14},... | collective-permute-start | bytes 165896 | tf_op jit(solution)/shard_map/ppermute | solution.py:23
  43.7 4.2 %collective-permute-start.17 = (f32[8,1728]{1,0:T(8,128)S(1)}, f32[8,1728]{1,0:T(8,128)S(1)}, u32[]{:S(2)}, u32[]{:S(2)}) collective-permute-start(f32[8,1728]{1,0:T(8,128)S(1)} %weave_channels.1.refs_0_), channel_id=1, source_target_pairs={{0,4},{4,0},{8,12},{12,8},{1,5},{5,1},{9,13},{13,9},{2,6},{6,2},{1... | collective-permute-start | bytes 165896 | tf_op jit(solution)/shard_map/ppermute | solution.py:23

commit v2 on v1

--- a/solution.py
+++ b/solution.py
@@ -323,11 +323,12 @@
     high, low = prepare(volume, out_cols)
     sent = weight_partial(high, low, rim, grads, parts)
     arrived = [sent[0]] + [swapped(sent[k], "gz", k) for k in range(1, parts)]
+    input_grad = input_gradient(weights, grads, uppers, volume.shape)
+    input_grad, arrived = lax.optimization_barrier((input_grad, arrived))
     sums = add_slabs(arrived, groups)
     crossed = [sums[0]] + [swapped(sums[j], "af", j) for j in range(1, groups)]
     own = weave_channels(crossed, channels, factor)
     weight_grad = stack_slabs([own] + [swapped(own, "gz", k) for k in range(1, parts)])
-    input_grad = input_gradient(weights, grads, uppers, volume.shape)
     return (input_grad, weight_grad)
 
 

time: 51.1 us -> 45.3 us (0.89)
  waiting for transfers between devices: 24 us -> 13.9 us
  starting transfers between devices: 19.5 us -> 23.8 us
    ppermute x18, waiting for transfers between devices: 22 us -> 13.9 us  [swapped(): lax.ppermute(value, axis, [(source, source ^ bits) for source in range(co...]
    ppermute x18, starting transfers between devices: 14.7 us -> 17.8 us  [swapped(): lax.ppermute(value, axis, [(source, source ^ bits) for source in range(co...]
    ppermute x2, waiting for transfers between devices: 2.01 us -> 0.01 us  [shifted(): lax.ppermute(value, axis, [(source, source + steps) for source in range(l...]
    ppermute x2, starting transfers between devices: 4.78 us -> 5.99 us  [shifted(): lax.ppermute(value, axis, [(source, source + steps) for source in range(l...]
  transfers between devices with their start and end apart: 20 -> 20, of which waited for: 9 -> 8; matrix products, arithmetic and copies ran while one was open for 2% -> 2% of each run, Pallas kernels for 7% -> 9%
where the time goes in v2:
time: 45.3 us; the launch traced here: 45.1 us
  starting transfers between devices  23.8 us (53%)
  waiting for transfers between devices  13.9 us (31%)
  Pallas kernels  5.64 us (12%)
  local copies, waits for them, and re-layouts  1.07 us (2%)
  between operations  0.74 us (2%)
    ppermute x18, starting transfers between devices, swapped(): lax.ppermute(value, axis, [(source, source ^ bits) for source in range(co...  17.8 us
    ppermute x18, waiting for transfers between devices, swapped(): lax.ppermute(value, axis, [(source, source ^ bits) for source in range(co...  13.9 us
    ppermute x2, starting transfers between devices, shifted(): lax.ppermute(value, axis, [(source, source + steps) for source in range(l...  5.99 us
    pallas_call x1, Pallas kernels, input_gradient(): pl.pallas_call(kernel, out_shape=jax.ShapeDtypeStruct((channels * planes...  2.26 us
    pallas_call x1, Pallas kernels, weight_partial(): pl.pallas_call(kernel, out_shape=[jax.ShapeDtypeStruct((groups * block, w...  1.2 us
    slice x1, local copies, waits for them, and re-layouts, fast(): rim = shifted(volume[:, planes - 1:planes], 'gz', 1)  0.97 us
  transfers between devices with their start and end apart: 20, of which 8 were waited for; matrix products, arithmetic and copies ran while one was open for 2% of the time, Pallas kernels for 9%

profile of v2, /device:TPU:0, one launch (start us, length us, event | category | flops | bytes accessed | tf_op | source)
XLA Modules:
  0.0 45.1 jit_solution(1011669848663953070)
XLA Ops:
  0.6 1.4 %collective-permute-start.6 = (f32[32,1,8,128]{3,2,1,0:T(8,128)}, f32[32,1,8,128]{3,2,1,0:T(8,128)S(1)}, u32[]{:S(2)}, u32[]{:S(2)}) collective-permute-start(f32[32,1,8,128]{3,2,1,0:T(8,128)} %param.4), channel_id=1, source_target_pairs={{4,0},{8,4},{12,8},{5,1},{9,5},{13,9},{6,2},{10,6},{14,10},{7,3},{... | collective-permute-start | bytes 393224 | tf_op jit(solution)/shard_map/ppermute | solution.py:18
  2.1 3.0 %collective-permute-start.1 = (f32[32,1728]{1,0:T(8,128)}, f32[32,1728]{1,0:T(8,128)S(1)}, u32[]{:S(2)}, u32[]{:S(2)}) collective-permute-start(f32[32,1728]{1,0:T(8,128)} %refs_0_.1), channel_id=1, source_target_pairs={{0,2},{1,3},{2,0},{3,1},{4,6},{5,7},{6,4},{7,5},{8,10},{9,11},{10,... | collective-permute-start | bytes 663560 | tf_op jit(solution)/shard_map/ppermute | solution.py:23
  5.1 0.2 collective-permute-start.4
  5.2 1.0 %slice.3 = f32[16,1,16,256]{3,2,1,0:T(8,128)S(1)} slice(f32[16,2,16,256]{3,2,1,0:T(8,128)} %param.3), slice={[0:16], [1:2], [0:16], [0:256]} | slice | bytes 524288 | tf_op jit(solution)/shard_map/slice | solution.py:320
  6.2 4.6 %collective-permute-start.10 = (f32[16,1,16,256]{3,2,1,0:T(8,128)S(1)}, f32[16,1,16,256]{3,2,1,0:T(8,128)S(1)}, u32[]{:S(2)}, u32[]{:S(2)}) collective-permute-start(f32[16,1,16,256]{3,2,1,0:T(8,128)S(1)} %slice.3), channel_id=1, source_target_pairs={{0,4},{4,8},{8,12},{1,5},{5,9},{9,13},{2,6},{6,10},{10,14},{3,7},{... | collective-permute-start | bytes 786440 | tf_op jit(solution)/shard_map/ppermute | solution.py:18
  10.8 1.9 %collective-permute-start.8 = (f32[32,1,8,128]{3,2,1,0:T(8,128)S(1)}, f32[32,1,8,128]{3,2,1,0:T(8,128)S(1)}, u32[]{:S(2)}, u32[]{:S(2)}) collective-permute-start(f32[32,1,8,128]{3,2,1,0:T(8,128)S(1)} %collective-permute-done.6), channel_id=1, source_target_pairs={{0,2},{1,3},{2,0},{3,1},{4,6},{5,7},{6,4},{7,5},{8,10},{9,11},{10,... | collective-permute-start | bytes 393224 | tf_op jit(solution)/shard_map/ppermute | solution.py:23
  12.7 0.0 collective-permute-done.3
  12.7 1.1 %collective-permute-done.4 = f32[32,1,8,128]{3,2,1,0:T(8,128)S(1)} collective-permute-done((f32[32,1,8,128]{3,2,1,0:T(8,128)}, f32[32,1,8,128]{3,2,1,0:T(8,128)S(1)}, u32[]{:S(2)}, u32[]{:S(2)}) %collective-permute-start.4) | collective-permute-done | bytes 131104 | tf_op jit(solution)/shard_map/ppermute | solution.py:23
  13.8 0.0 collective-permute-start.5
  13.8 0.5 %collective-permute-start.2 = (f32[32,1728]{1,0:T(8,128)S(1)}, f32[32,1728]{1,0:T(8,128)S(1)}, u32[]{:S(2)}, u32[]{:S(2)}) collective-permute-start(f32[32,1728]{1,0:T(8,128)S(1)} %collective-permute-done.1.refs_2_), channel_id=1, source_target_pairs={{0,1},{1,0},{2,3},{3,2},{4,5},{5,4},{6,7},{7,6},{8,9},{9,8},{10,11... | collective-permute-start | bytes 663560 | tf_op jit(solution)/shard_map/ppermute | solution.py:23
  14.3 2.2 %collective-permute-done.8 = f32[32,1,8,128]{3,2,1,0:T(8,128)S(1)} collective-permute-done((f32[32,1,8,128]{3,2,1,0:T(8,128)S(1)}, f32[32,1,8,128]{3,2,1,0:T(8,128)S(1)}, u32[]{:S(2)}, u32[]{:S(2)}) %collective-permute-start.8) | collective-permute-done | bytes 131104 | tf_op jit(solution)/shard_map/ppermute | solution.py:23
  16.5 0.5 %collective-permute-start.9 = (f32[32,1,8,128]{3,2,1,0:T(8,128)S(1)}, f32[32,1,8,128]{3,2,1,0:T(8,128)S(1)}, u32[]{:S(2)}, u32[]{:S(2)}) collective-permute-start(f32[32,1,8,128]{3,2,1,0:T(8,128)S(1)} %collective-permute-done.8), channel_id=1, source_target_pairs={{0,1},{1,0},{2,3},{3,2},{4,5},{5,4},{6,7},{7,6},{8,9},{9,8},{10,11... | collective-permute-start | bytes 393224 | tf_op jit(solution)/shard_map/ppermute | solution.py:23
  17.0 0.8 %prepare.1 = (bf16[512,384]{1,0:T(8,128)(2,1)S(1)}, bf16[512,384]{1,0:T(8,128)(2,1)S(1)}) custom-call(f32[512,256]{1,0:T(8,128)S(1)} %bitcast.12), custom_call_target="tpu_custom_call" | custom-call | tf_op jit(solution)/shard_map/prepare/pallas_call | solution.py:64
  17.8 0.1 copy-done.1
  17.9 1.2 %weight_partial.1 = (f32[32,432]{1,0:T(8,128)S(1)}, f32[32,432]{1,0:T(8,128)S(1)}, f32[32,432]{1,0:T(8,128)S(1)}, f32[32,432]{1,0:T(8,128)S(1)}) custom-call(bf16[512,384]{1,0:T(8,128)(2,1)S(1)} %get-tuple-element.17.refs_0_, bf16[512,384]{1,0:T(8,128)(2,1)S(1)} %get-tuple-element.18.refs_1_, f32[256,256]{1,0:T(8,128)S(1)} %bitcast.21, ...), custom_call_target="tpu_custom_call" | custom-call | tf_op jit(solution)/shard_map/weight_partial/pallas_call | solution.py:116
  19.1 2.5 %collective-permute-start.11 = (f32[32,432]{1,0:T(8,128)S(1)}, f32[32,432]{1,0:T(8,128)S(1)}, u32[]{:S(2)}, u32[]{:S(2)}) collective-permute-start(f32[32,432]{1,0:T(8,128)S(1)} %get-tuple-element.20), channel_id=1, source_target_pairs={{0,4},{4,0},{8,12},{12,8},{1,5},{5,1},{9,13},{13,9},{2,6},{6,2},{1... | collective-permute-start | bytes 165896 | tf_op jit(solution)/shard_map/ppermute | solution.py:23
  21.7 2.8 %collective-permute-start.12 = (f32[32,432]{1,0:T(8,128)S(1)}, f32[32,432]{1,0:T(8,128)S(1)}, u32[]{:S(2)}, u32[]{:S(2)}) collective-permute-start(f32[32,432]{1,0:T(8,128)S(1)} %get-tuple-element.21), channel_id=1, source_target_pairs={{0,8},{4,12},{8,0},{12,4},{1,9},{5,13},{9,1},{13,5},{2,10},{6,14},... | collective-permute-start | bytes 165896 | tf_op jit(solution)/shard_map/ppermute | solution.py:23
  24.4 2.3 %input_gradient.1 = f32[512,256]{1,0:T(8,128)} custom-call(f32[32,1728]{1,0:T(8,128)S(1)} %copy-done.2, f32[32,1728]{1,0:T(8,128)S(1)} %collective-permute-done.refs_1_, f32[32,1728]{1,0:T(8,128)S(1)} %collective-permute-done.1.refs_2_, f32[32,1728]{1,0:T(8,128)S(1)} %collective-permute-done.2.refs_3_, f32[256,128]{1,0:T(8,128)S(1)} %bitcast.14, ...), custom_call_target="tpu_custom_call" | custom-call | tf_op jit(solution)/shard_map/input_gradient/pallas_call | solution.py:281
  26.7 2.4 %collective-permute-done.12.refs_2_ = f32[32,432]{1,0:T(8,128)S(1)} collective-permute-done((f32[32,432]{1,0:T(8,128)S(1)}, f32[32,432]{1,0:T(8,128)S(1)}, u32[]{:S(2)}, u32[]{:S(2)}) %collective-permute-start.12) | collective-permute-done | bytes 55328 | tf_op jit(solution)/shard_map/ppermute | solution.py:23
  29.1 1.5 %collective-permute-done.13.refs_3_ = f32[32,432]{1,0:T(8,128)S(1)} collective-permute-done((f32[32,432]{1,0:T(8,128)S(1)}, f32[32,432]{1,0:T(8,128)S(1)}, u32[]{:S(2)}, u32[]{:S(2)}) %collective-permute-start.13) | collective-permute-done | bytes 55328 | tf_op jit(solution)/shard_map/ppermute | solution.py:23
  30.6 0.1 collective-permute-start.14
  30.7 1.6 %collective-permute-start.15 = (f32[8,432]{1,0:T(8,128)S(1)}, f32[8,432]{1,0:T(8,128)S(1)}, u32[]{:S(2)}, u32[]{:S(2)}) collective-permute-start(f32[8,432]{1,0:T(8,128)S(1)} %get-tuple-element.30), channel_id=1, source_target_pairs={{0,2},{1,3},{2,0},{3,1},{4,6},{5,7},{6,4},{7,5},{8,10},{9,11},{10,... | collective-permute-start | bytes 41480 | tf_op jit(solution)/shard_map/ppermute | solution.py:23
  32.3 0.3 collective-permute-start.16
  32.6 1.9 %collective-permute-done.15.refs_2_ = f32[8,432]{1,0:T(8,128)S(1)} collective-permute-done((f32[8,432]{1,0:T(8,128)S(1)}, f32[8,432]{1,0:T(8,128)S(1)}, u32[]{:S(2)}, u32[]{:S(2)}) %collective-permute-start.15) | collective-permute-done | bytes 13856 | tf_op jit(solution)/shard_map/ppermute | solution.py:23
  34.5 0.9 %collective-permute-done.16.refs_3_ = f32[8,432]{1,0:T(8,128)S(1)} collective-permute-done((f32[8,432]{1,0:T(8,128)S(1)}, f32[8,432]{1,0:T(8,128)S(1)}, u32[]{:S(2)}, u32[]{:S(2)}) %collective-permute-start.16) | collective-permute-done | bytes 13856 | tf_op jit(solution)/shard_map/ppermute | solution.py:23
  35.4 0.7 %weave_channels.1.refs_0_ = f32[8,1728]{1,0:T(8,128)S(1)} custom-call(f32[8,432]{1,0:T(8,128)S(1)} %get-tuple-element.28.refs_0_, f32[8,432]{1,0:T(8,128)S(1)} %collective-permute-done.14.refs_1_, f32[8,432]{1,0:T(8,128)S(1)} %collective-permute-done.15.refs_2_, f32[8,432]{1,0:T(8,128)S(1)} %collective-permute-done.16.refs_3_), custom_call_target="tpu_custom_call" | custom-call | tf_op jit(solution)/shard_map/weave_channels/pallas_call | solution.py:190
  36.1 1.9 %collective-permute-start.19 = (f32[8,1728]{1,0:T(8,128)S(1)}, f32[8,1728]{1,0:T(8,128)S(1)}, u32[]{:S(2)}, u32[]{:S(2)}) collective-permute-start(f32[8,1728]{1,0:T(8,128)S(1)} %weave_channels.1.refs_0_), channel_id=1, source_target_pairs={{0,12},{4,8},{8,4},{12,0},{1,13},{5,9},{9,5},{13,1},{2,14},{6,10},... | collective-permute-start | bytes 165896 | tf_op jit(solution)/shard_map/ppermute | solution.py:23
  38.0 0.3 collective-permute-start.18
  38.3 2.2 %collective-permute-start.17 = (f32[8,1728]{1,0:T(8,128)S(1)}, f32[8,1728]{1,0:T(8,128)S(1)}, u32[]{:S(2)}, u32[]{:S(2)}) collective-permute-start(f32[8,1728]{1,0:T(8,128)S(1)} %weave_channels.1.refs_0_), channel_id=1, source_target_pairs={{0,4},{4,0},{8,12},{12,8},{1,5},{5,1},{9,13},{13,9},{2,6},{6,2},{1... | collective-permute-start | bytes 165896 | tf_op jit(solution)/shard_map/ppermute | solution.py:23
  40.5 2.1 %collective-permute-done.19.refs_3_ = f32[8,1728]{1,0:T(8,128)S(1)} collective-permute-done((f32[8,1728]{1,0:T(8,128)S(1)}, f32[8,1728]{1,0:T(8,128)S(1)}, u32[]{:S(2)}, u32[]{:S(2)}) %collective-permute-start.19) | collective-permute-done | bytes 55328 | tf_op jit(solution)/shard_map/ppermute | solution.py:23
  42.7 1.7 %collective-permute-done.18.refs_2_ = f32[8,1728]{1,0:T(8,128)S(1)} collective-permute-done((f32[8,1728]{1,0:T(8,128)S(1)}, f32[8,1728]{1,0:T(8,128)S(1)}, u32[]{:S(2)}, u32[]{:S(2)}) %collective-permute-start.18) | collective-permute-done | bytes 55328 | tf_op jit(solution)/shard_map/ppermute | solution.py:23
  44.4 0.7 %stack_slabs.1 = f32[4,8,1728]{2,1,0:T(8,128)} custom-call(f32[8,1728]{1,0:T(8,128)S(1)} %weave_channels.1.refs_0_, f32[8,1728]{1,0:T(8,128)S(1)} %collective-permute-done.17.refs_1_, f32[8,1728]{1,0:T(8,128)S(1)} %collective-permute-done.18.refs_2_, f32[8,1728]{1,0:T(8,128)S(1)} %collective-permute-done.19.refs_3_), custom_call_target="tpu_custom_call" | custom-call | tf_op jit(solution)/shard_map/stack_slabs/pallas_call | solution.py:207
  (21 shorter events, 0.1 us)
Async XLA Ops:
  0.6 16.4 %copy-start = (f32[16,2,16,256]{3,2,1,0:T(8,128)S(1)}, f32[16,2,16,256]{3,2,1,0:T(8,128)}, u32[]{:S(2)}) copy-start(f32[16,2,16,256]{3,2,1,0:T(8,128)} %param.3) | copy-start | bytes 1572868
  0.6 10.1 %collective-permute-start.6 = (f32[32,1,8,128]{3,2,1,0:T(8,128)}, f32[32,1,8,128]{3,2,1,0:T(8,128)S(1)}, u32[]{:S(2)}, u32[]{:S(2)}) collective-permute-start(f32[32,1,8,128]{3,2,1,0:T(8,128)} %param.4), channel_id=1, source_target_pairs={{4,0},{8,4},{12,8},{5,1},{9,5},{13,9},{6,2},{10,6},{14,10},{7,3},{... | collective-permute-start | bytes 393224 | tf_op jit(solution)/shard_map/ppermute | solution.py:18
  2.1 11.7 %collective-permute-start.1 = (f32[32,1728]{1,0:T(8,128)}, f32[32,1728]{1,0:T(8,128)S(1)}, u32[]{:S(2)}, u32[]{:S(2)}) collective-permute-start(f32[32,1728]{1,0:T(8,128)} %refs_0_.1), channel_id=1, source_target_pairs={{0,2},{1,3},{2,0},{3,1},{4,6},{5,7},{6,4},{7,5},{8,10},{9,11},{10,... | collective-permute-start | bytes 663560 | tf_op jit(solution)/shard_map/ppermute | solution.py:23
  5.1 7.7 %collective-permute-start.3 = (f32[32,1,8,128]{3,2,1,0:T(8,128)}, f32[32,1,8,128]{3,2,1,0:T(8,128)S(1)}, u32[]{:S(2)}, u32[]{:S(2)}) collective-permute-start(f32[32,1,8,128]{3,2,1,0:T(8,128)} %param.4), channel_id=1, source_target_pairs={{0,1},{1,0},{2,3},{3,2},{4,5},{5,4},{6,7},{7,6},{8,9},{9,8},{10,11... | collective-permute-start | bytes 393224 | tf_op jit(solution)/shard_map/ppermute | solution.py:23
  5.1 8.7 %collective-permute-start.4 = (f32[32,1,8,128]{3,2,1,0:T(8,128)}, f32[32,1,8,128]{3,2,1,0:T(8,128)S(1)}, u32[]{:S(2)}, u32[]{:S(2)}) collective-permute-start(f32[32,1,8,128]{3,2,1,0:T(8,128)} %param.4), channel_id=1, source_target_pairs={{0,2},{1,3},{2,0},{3,1},{4,6},{5,7},{6,4},{7,5},{8,10},{9,11},{10,... | collective-permute-start | bytes 393224 | tf_op jit(solution)/shard_map/ppermute | solution.py:23
  6.2 11.6 %collective-permute-start.10 = (f32[16,1,16,256]{3,2,1,0:T(8,128)S(1)}, f32[16,1,16,256]{3,2,1,0:T(8,128)S(1)}, u32[]{:S(2)}, u32[]{:S(2)}) collective-permute-start(f32[16,1,16,256]{3,2,1,0:T(8,128)S(1)} %slice.3), channel_id=1, source_target_pairs={{0,4},{4,8},{8,12},{1,5},{5,9},{9,13},{2,6},{6,10},{10,14},{3,7},{... | collective-permute-start | bytes 786440 | tf_op jit(solution)/shard_map/ppermute | solution.py:18
  10.8 5.7 %collective-permute-start.8 = (f32[32,1,8,128]{3,2,1,0:T(8,128)S(1)}, f32[32,1,8,128]{3,2,1,0:T(8,128)S(1)}, u32[]{:S(2)}, u32[]{:S(2)}) collective-permute-start(f32[32,1,8,128]{3,2,1,0:T(8,128)S(1)} %collective-permute-done.6), channel_id=1, source_target_pairs={{0,2},{1,3},{2,0},{3,1},{4,6},{5,7},{6,4},{7,5},{8,10},{9,11},{10,... | collective-permute-start | bytes 393224 | tf_op jit(solution)/shard_map/ppermute | solution.py:23
  12.7 8.9 %collective-permute-start = (f32[32,1728]{1,0:T(8,128)}, f32[32,1728]{1,0:T(8,128)S(1)}, u32[]{:S(2)}, u32[]{:S(2)}) collective-permute-start(f32[32,1728]{1,0:T(8,128)} %refs_0_.1), channel_id=1, source_target_pairs={{0,1},{1,0},{2,3},{3,2},{4,5},{5,4},{6,7},{7,6},{8,9},{9,8},{10,11... | collective-permute-start | bytes 663560 | tf_op jit(solution)/shard_map/ppermute | solution.py:23
  13.8 2.7 %collective-permute-start.5 = (f32[32,1,8,128]{3,2,1,0:T(8,128)S(1)}, f32[32,1,8,128]{3,2,1,0:T(8,128)S(1)}, u32[]{:S(2)}, u32[]{:S(2)}) collective-permute-start(f32[32,1,8,128]{3,2,1,0:T(8,128)S(1)} %collective-permute-done.4), channel_id=1, source_target_pairs={{0,1},{1,0},{2,3},{3,2},{4,5},{5,4},{6,7},{7,6},{8,9},{9,8},{10,11... | collective-permute-start | bytes 393224 | tf_op jit(solution)/shard_map/ppermute | solution.py:23
  13.8 10.6 %collective-permute-start.2 = (f32[32,1728]{1,0:T(8,128)S(1)}, f32[32,1728]{1,0:T(8,128)S(1)}, u32[]{:S(2)}, u32[]{:S(2)}) collective-permute-start(f32[32,1728]{1,0:T(8,128)S(1)} %collective-permute-done.1.refs_2_), channel_id=1, source_target_pairs={{0,1},{1,0},{2,3},{3,2},{4,5},{5,4},{6,7},{7,6},{8,9},{9,8},{10,11... | collective-permute-start | bytes 663560 | tf_op jit(solution)/shard_map/ppermute | solution.py:23
  16.5 7.9 %collective-permute-start.7 = (f32[32,1,8,128]{3,2,1,0:T(8,128)S(1)}, f32[32,1,8,128]{3,2,1,0:T(8,128)S(1)}, u32[]{:S(2)}, u32[]{:S(2)}) collective-permute-start(f32[32,1,8,128]{3,2,1,0:T(8,128)S(1)} %collective-permute-done.6), channel_id=1, source_target_pairs={{0,1},{1,0},{2,3},{3,2},{4,5},{5,4},{6,7},{7,6},{8,9},{9,8},{10,11... | collective-permute-start | bytes 393224 | tf_op jit(solution)/shard_map/ppermute | solution.py:23
  16.5 7.9 %collective-permute-start.9 = (f32[32,1,8,128]{3,2,1,0:T(8,128)S(1)}, f32[32,1,8,128]{3,2,1,0:T(8,128)S(1)}, u32[]{:S(2)}, u32[]{:S(2)}) collective-permute-start(f32[32,1,8,128]{3,2,1,0:T(8,128)S(1)} %collective-permute-done.8), channel_id=1, source_target_pairs={{0,1},{1,0},{2,3},{3,2},{4,5},{5,4},{6,7},{7,6},{8,9},{9,8},{10,11... | collective-permute-start | bytes 393224 | tf_op jit(solution)/shard_map/ppermute | solution.py:23
  17.0 0.9 %copy-start.1 = (f32[32,1,8,128]{3,2,1,0:T(8,128)S(1)}, f32[32,1,8,128]{3,2,1,0:T(8,128)}, u32[]{:S(2)}) copy-start(f32[32,1,8,128]{3,2,1,0:T(8,128)} %param.4) | copy-start | bytes 393220
  17.9 6.5 %copy-start.2 = (f32[32,1728]{1,0:T(8,128)S(1)}, f32[32,1728]{1,0:T(8,128)}, u32[]{:S(2)}) copy-start(f32[32,1728]{1,0:T(8,128)} %refs_0_.1) | copy-start | bytes 663556
  19.1 7.6 %collective-permute-start.11 = (f32[32,432]{1,0:T(8,128)S(1)}, f32[32,432]{1,0:T(8,128)S(1)}, u32[]{:S(2)}, u32[]{:S(2)}) collective-permute-start(f32[32,432]{1,0:T(8,128)S(1)} %get-tuple-element.20), channel_id=1, source_target_pairs={{0,4},{4,0},{8,12},{12,8},{1,5},{5,1},{9,13},{13,9},{2,6},{6,2},{1... | collective-permute-start | bytes 165896 | tf_op jit(solution)/shard_map/ppermute | solution.py:23
  21.7 7.5 %collective-permute-start.12 = (f32[32,432]{1,0:T(8,128)S(1)}, f32[32,432]{1,0:T(8,128)S(1)}, u32[]{:S(2)}, u32[]{:S(2)}) collective-permute-start(f32[32,432]{1,0:T(8,128)S(1)} %get-tuple-element.21), channel_id=1, source_target_pairs={{0,8},{4,12},{8,0},{12,4},{1,9},{5,13},{9,1},{13,5},{2,10},{6,14},... | collective-permute-start | bytes 165896 | tf_op jit(solution)/shard_map/ppermute | solution.py:23
  24.4 6.2 %collective-permute-start.13 = (f32[32,432]{1,0:T(8,128)S(1)}, f32[32,432]{1,0:T(8,128)S(1)}, u32[]{:S(2)}, u32[]{:S(2)}) collective-permute-start(f32[32,432]{1,0:T(8,128)S(1)} %get-tuple-element.22), channel_id=1, source_target_pairs={{0,12},{4,8},{8,4},{12,0},{1,13},{5,9},{9,5},{13,1},{2,14},{6,10},... | collective-permute-start | bytes 165896 | tf_op jit(solution)/shard_map/ppermute | solution.py:23
  30.6 1.9 %collective-permute-start.14 = (f32[8,432]{1,0:T(8,128)S(1)}, f32[8,432]{1,0:T(8,128)S(1)}, u32[]{:S(2)}, u32[]{:S(2)}) collective-permute-start(f32[8,432]{1,0:T(8,128)S(1)} %get-tuple-element.29), channel_id=1, source_target_pairs={{0,1},{1,0},{2,3},{3,2},{4,5},{5,4},{6,7},{7,6},{8,9},{9,8},{10,11... | collective-permute-start | bytes 41480 | tf_op jit(solution)/shard_map/ppermute | solution.py:23
  30.7 3.8 %collective-permute-start.15 = (f32[8,432]{1,0:T(8,128)S(1)}, f32[8,432]{1,0:T(8,128)S(1)}, u32[]{:S(2)}, u32[]{:S(2)}) collective-permute-start(f32[8,432]{1,0:T(8,128)S(1)} %get-tuple-element.30), channel_id=1, source_target_pairs={{0,2},{1,3},{2,0},{3,1},{4,6},{5,7},{6,4},{7,5},{8,10},{9,11},{10,... | collective-permute-start | bytes 41480 | tf_op jit(solution)/shard_map/ppermute | solution.py:23
  32.3 3.2 %collective-permute-start.16 = (f32[8,432]{1,0:T(8,128)S(1)}, f32[8,432]{1,0:T(8,128)S(1)}, u32[]{:S(2)}, u32[]{:S(2)}) collective-permute-start(f32[8,432]{1,0:T(8,128)S(1)} %get-tuple-element.31), channel_id=1, source_target_pairs={{0,3},{1,2},{2,1},{3,0},{4,7},{5,6},{6,5},{7,4},{8,11},{9,10},{10,... | collective-permute-start | bytes 41480 | tf_op jit(solution)/shard_map/ppermute | solution.py:23
  36.1 6.6 %collective-permute-start.19 = (f32[8,1728]{1,0:T(8,128)S(1)}, f32[8,1728]{1,0:T(8,128)S(1)}, u32[]{:S(2)}, u32[]{:S(2)}) collective-permute-start(f32[8,1728]{1,0:T(8,128)S(1)} %weave_channels.1.refs_0_), channel_id=1, source_target_pairs={{0,12},{4,8},{8,4},{12,0},{1,13},{5,9},{9,5},{13,1},{2,14},{6,10},... | collective-permute-start | bytes 165896 | tf_op jit(solution)/shard_map/ppermute | solution.py:23
  38.0 6.4 %collective-permute-start.18 = (f32[8,1728]{1,0:T(8,128)S(1)}, f32[8,1728]{1,0:T(8,128)S(1)}, u32[]{:S(2)}, u32[]{:S(2)}) collective-permute-start(f32[8,1728]{1,0:T(8,128)S(1)} %weave_channels.1.refs_0_), channel_id=1, source_target_pairs={{0,8},{4,12},{8,0},{12,4},{1,9},{5,13},{9,1},{13,5},{2,10},{6,14},... | collective-permute-start | bytes 165896 | tf_op jit(solution)/shard_map/ppermute | solution.py:23
  38.3 6.1 %collective-permute-start.17 = (f32[8,1728]{1,0:T(8,128)S(1)}, f32[8,1728]{1,0:T(8,128)S(1)}, u32[]{:S(2)}, u32[]{:S(2)}) collective-permute-start(f32[8,1728]{1,0:T(8,128)S(1)} %weave_channels.1.refs_0_), channel_id=1, source_target_pairs={{0,4},{4,0},{8,12},{12,8},{1,5},{5,1},{9,13},{13,9},{2,6},{6,2},{1... | collective-permute-start | bytes 165896 | tf_op jit(solution)/shard_map/ppermute | solution.py:23

commit v3 on v0

--- a/solution.py
+++ b/solution.py
@@ -3,13 +3,413 @@
 import jax
 import jax.numpy as jnp
 from jax import lax
+from jax.experimental import pallas as pl
+from jax.experimental.pallas import tpu as pltpu
 from jax.sharding import PartitionSpec as P
+
+F32 = jnp.float32
+BF16 = jnp.bfloat16
+VMEM = pl.BlockSpec(memory_space=pltpu.VMEM)
+HBM = pl.BlockSpec(memory_space=pltpu.HBM)
+PARAMS = pltpu.CompilerParams(vmem_limit_bytes=48 * 1024 * 1024)
 
 
 def shifted(value, axis, steps):
     count = lax.axis_size(axis)
     leading, last = (max(0, -steps), min(count, count - steps))
     return lax.ppermute(value, axis, [(source, source + steps) for source in range(leading, last)])
+
+
+def swapped(value, axis, bits):
+    count = lax.axis_size(axis)
+    return lax.ppermute(value, axis, [(source, source ^ bits) for source in range(count)])
+
+
+def in_hbm(value):
+    return pltpu.with_memory_space_constraint(value, pltpu.HBM)
+
+
+def halves(value):
+    high = value.astype(BF16)
+    return high, (value - high.astype(F32)).astype(BF16)
+
+
+def dot(a, b):
+    return lax.dot_general(a, b, (((1,), (0,)), ((), ())), preferred_element_type=F32)
+
+
+def dot_t(a, b):
+    return lax.dot_general(a, b, (((1,), (1,)), ((), ())), preferred_element_type=F32)
+
+
+def column_taps(cols, out_cols):
+    x = lax.broadcasted_iota(jnp.int32, (cols, 3 * out_cols), 0)
+    c = lax.broadcasted_iota(jnp.int32, (cols, 3 * out_cols), 1)
+    dx = c // out_cols
+    return jnp.where(x == 2 * (c - dx * out_cols) + dx - 1, 1.0, 0.0).astype(BF16)
+
+
+def split_rows(g_ref, filters, out_rows, out_cols, high_ref, low_ref, first=0):
+    for q in range(out_rows):
+        pair = halves(g_ref[pl.ds(q, filters, stride=out_rows), :])
+        for target, half in zip((high_ref, low_ref), pair):
+            target[first : first + filters, q * out_cols : (q + 1) * out_cols] = half
+
+
+def gather_taps(volumes, out_grad):
+    filters, _, out_rows, out_cols = out_grad.shape
+    channels, planes, rows, cols = volumes[0].shape
+    cores = len(volumes)
+    count = planes * rows * channels
+    width = planes * 9 * cores * channels
+    cells = out_rows * out_cols
+
+    def kernel(v_hbm, g_hbm, *refs):
+        v_refs = refs[: cores - 1]
+        targets, g_targets = refs[cores - 1 : cores + 1], refs[cores + 1 : cores + 3]
+        x_refs, d_refs = refs[cores + 3 : cores + 5], refs[cores + 5 : cores + 7]
+        own_lanes, lanes, g_ref, sems = refs[cores + 7 :]
+        copies = [
+            pltpu.make_async_copy(v_hbm.at[:, h * 128 : (h + 1) * 128], own_lanes.at[h], sems.at[h])
+            for h in range(cols // 128)
+        ] + [pltpu.make_async_copy(g_hbm, g_ref, sems.at[cols // 128])]
+        for copy in copies:
+            copy.start()
+        taps = column_taps(cols, out_cols)
+        for core in reversed(range(cores)):
+            if core == 0:
+                for copy in copies:
+                    copy.wait()
+            for h in range(cols // 128):
+                source = own_lanes.at[h]
+                if core:
+                    source = lanes
+                    lanes[...] = v_refs[core - 1][:, h * 128 : (h + 1) * 128]
+                for k in range(planes * rows):
+                    pair = halves(source[pl.ds(k, channels, stride=planes * rows), :])
+                    for x_ref, half in zip(x_refs, pair):
+                        x_ref[k * channels : (k + 1) * channels, h * 128 : (h + 1) * 128] = half
+            for x_ref, d_ref, target in zip(x_refs, d_refs, targets):
+                d_ref[...] = dot(x_ref[...], taps).astype(BF16)
+                for z in range(planes):
+                    for dy in range(3):
+                        for q in range(out_rows):
+                            y = 2 * q + dy - 1
+                            for dx in range(3):
+                                at = (((z * 3 + dy) * 3 + dx) * cores + core) * channels
+                                if y < 0:
+                                    piece = jnp.zeros((channels, out_cols), BF16)
+                                else:
+                                    first = (z * rows + y) * channels
+                                    piece = d_ref[first : first + channels, dx * out_cols : (dx + 1) * out_cols]
+                                target[at : at + channels, q * out_cols : (q + 1) * out_cols] = piece
+        split_rows(g_ref, filters, out_rows, out_cols, *g_targets)
+
+    return pl.pallas_call(
+        kernel,
+        in_specs=[HBM, HBM] + [VMEM] * (cores - 1),
+        out_shape=[jax.ShapeDtypeStruct((width, cells), BF16)] * 2
+        + [jax.ShapeDtypeStruct((filters, cells), BF16)] * 2,
+        scratch_shapes=[pltpu.VMEM((count, cols), BF16)] * 2
+        + [pltpu.VMEM((count, 3 * out_cols), BF16)] * 2
+        + [
+            pltpu.VMEM((cols // 128, count, 128), F32),
+            pltpu.VMEM((count, 128), F32),
+            pltpu.VMEM((filters * out_rows, out_cols), F32),
+            pltpu.SemaphoreType.DMA((cols // 128 + 1,)),
+        ],
+        compiler_params=PARAMS,
+        name="gather_taps",
+    )(in_hbm(volumes[0].reshape(-1, cols)), in_hbm(out_grad.reshape(-1, out_cols)), *[v.reshape(-1, cols) for v in volumes[1:]])
+
+
+def weight_terms(high, low, own, across):
+    filters, _, out_rows, out_cols = across.shape
+    cells = out_rows * out_cols
+
+    def kernel(high_ref, low_ref, own_high, own_low, g_ref, out_ref, g_both):
+        g_both[:filters, :] = own_high[...]
+        g_both[2 * filters : 3 * filters, :] = own_low[...]
+        split_rows(g_ref, filters, out_rows, out_cols, g_both.at[filters:], g_both.at[3 * filters :])
+        both = dot_t(g_both[...], high_ref[...])
+        out_ref[...] = both[: 2 * filters] + both[2 * filters :] + dot_t(g_both[: 2 * filters, :], low_ref[...])
+
+    return pl.pallas_call(
+        kernel,
+        out_shape=jax.ShapeDtypeStruct((2 * filters, high.shape[0]), F32),
+        scratch_shapes=[pltpu.VMEM((4 * filters, cells), BF16)],
+        compiler_params=PARAMS,
+        name="weight_terms",
+    )(high, low, *own, across.reshape(-1, out_cols))
+
+
+def weight_partial(high, low, terms, above, parts):
+    filters, _, out_rows, out_cols = above[0].shape
+    cells = out_rows * out_cols
+    third = high.shape[0] // 2
+    block = filters // parts
+    chips = len(above)
+    count = chips * filters
+
+    def kernel(high_ref, low_ref, terms_ref, *refs):
+        g_refs, out_refs = refs[:chips], refs[chips : chips + parts]
+        g_both, total = refs[chips + parts :]
+        for j, g_ref in enumerate(g_refs):
+            split_rows(g_ref, filters, out_rows, out_cols, g_both.at[:count], g_both.at[count:], j * filters)
+        both = dot_t(g_both[...], high_ref[third:, :])
+        total[:, :third] = both[:count] + both[count:] + dot_t(g_both[:count, :], low_ref[third:, :])
+        total[:, third:] = terms_ref[...]
+        slab = lax.axis_index("gz")
+        for k in range(parts):
+            for j in range(chips):
+                first = pl.multiple_of(j * filters + (slab ^ k) * block, 8)
+                out_refs[k][j * block : (j + 1) * block, :] = total[pl.ds(first, block), :]
+
+    return pl.pallas_call(
+        kernel,
+        out_shape=[jax.ShapeDtypeStruct((chips * block, 3 * third), F32)] * parts,
+        scratch_shapes=[
+            pltpu.VMEM((2 * count, cells), BF16),
+            pltpu.VMEM((count, 3 * third), F32),
+        ],
+        compiler_params=PARAMS,
+        name="weight_partial",
+    )(high, low, terms, *[g.reshape(-1, out_cols) for g in above])
+
+
+def add_slabs(pieces, chips):
+    rows, width = pieces[0].shape
+    block = rows // chips
+
+    def kernel(*refs):
+        for j in range(chips):
+            value = refs[0][j * block : (j + 1) * block, :]
+            for piece in refs[1 : len(pieces)]:
+                value = value + piece[j * block : (j + 1) * block, :]
+            refs[len(pieces) + j][...] = value
+
+    return pl.pallas_call(
+        kernel,
+        out_shape=[jax.ShapeDtypeStruct((block, width), F32)] * chips,
+        compiler_params=PARAMS,
+        name="add_slabs",
+    )(*pieces)
+
+
+def weave_channels(pieces, channels, cores, factor):
+    chips = len(pieces)
+    block, width = pieces[0].shape
+    total = chips * cores * channels
+    span = 128
+    taps = span // (cores * channels)
+    chunks = -(-width // span)
+
+    def kernel(*refs):
+        me = lax.axis_index("af")
+        row = lax.broadcasted_iota(jnp.int32, (chips * span, taps * total), 0)
+        col = lax.broadcasted_iota(jnp.int32, (chips * span, taps * total), 1)
+        j = row // span
+        inner = row - j * span
+        tap = inner // (cores * channels)
+        core = (inner // channels) % cores
+        owner = me ^ (j * cores + core)
+        place = jnp.where(col == tap * total + owner * channels + inner % channels, 1.0, 0.0).astype(BF16)
+        for c in range(chunks):
+            size = min(span, width - c * span)
+            columns = []
+            for j in range(chips):
+                value = refs[j][:, c * span : c * span + size] * factor
+                if size < span:
+                    value = jnp.concatenate([value, jnp.zeros((block, span - size), F32)], axis=1)
+                columns.append(value)
+            wide = jnp.concatenate(columns, axis=1)
+            high = wide.astype(BF16).astype(F32)
+            rest = wide - high
+            middle = rest.astype(BF16).astype(F32)
+            stacked = jnp.concatenate([high, middle, rest - middle], axis=0).astype(BF16)
+            woven = dot(stacked, place)
+            result = woven[:block] + woven[block : 2 * block] + woven[2 * block :]
+            first = c * taps * total
+            last = min(first + taps * total, 27 * total)
+            refs[chips][:, first:last] = result[:, : last - first]
+
+    return pl.pallas_call(
+        kernel,
+        out_shape=jax.ShapeDtypeStruct((block, 27 * total), F32),
+        compiler_params=PARAMS,
+        name="weave_channels",
+    )(*pieces)
+
+
+def stack_slabs(pieces):
+    block, width = pieces[0].shape
+    parts = len(pieces)
+
+    def kernel(*refs):
+        slab = lax.axis_index("gz")
+        for k in range(parts):
+            refs[parts][slab ^ k] = refs[k][...]
+
+    return pl.pallas_call(
+        kernel,
+        out_shape=jax.ShapeDtypeStruct((parts, block, width), F32),
+        compiler_params=PARAMS,
+        name="stack_slabs",
+    )(*pieces).reshape(parts * block, width)
+
+
+def pack_weights(weight, cores, channels):
+    filters, width = weight.shape
+    total = width // 27
+    kept = cores * channels
+    span = 128 * total // kept
+    chunks = -(-width // span)
+
+    def kernel(w_ref, own_ref, other_ref):
+        chip = lax.axis_index("af") // cores
+        row = lax.broadcasted_iota(jnp.int32, (span, 128), 0)
+        col = lax.broadcasted_iota(jnp.int32, (span, 128), 1)
+        start = (col // kept) * total + col % kept
+        for target, side in ((own_ref, chip), (other_ref, 1 - chip)):
+            place = jnp.where(row == start + side * kept, 1.0, 0.0).astype(BF16)
+            for c in range(chunks):
+                size = min(span, width - c * span)
+                value = w_ref[:, c * span : c * span + size]
+                if size < span:
+                    value = jnp.concatenate([value, jnp.zeros((filters, span - size), F32)], axis=1)
+                high = value.astype(BF16).astype(F32)
+                rest = value - high
+                middle = rest.astype(BF16).astype(F32)
+                stacked = jnp.concatenate([high, middle, rest - middle], axis=0).astype(BF16)
+                packed = dot(stacked, place)
+                result = packed[:filters] + packed[filters : 2 * filters] + packed[2 * filters :]
+                last = min(128, 27 * kept - c * 128)
+                target[:, c * 128 : c * 128 + last] = result[:, :last]
+
+    return pl.pallas_call(
+        kernel,
+        out_shape=[jax.ShapeDtypeStruct((filters, 27 * kept), F32)] * 2,
+        compiler_params=PARAMS,
+        name="pack_weights",
+    )(weight)
+
+
+def input_partial(weights, own, grads, volume_shape, cores):
+    channels, planes, rows, cols = volume_shape
+    chips = len(weights)
+    filters, _, out_rows, out_cols = grads[0].shape
+    count = chips * filters
+    cells = out_rows * out_cols
+    ninth = cores * channels
+    padded = -(-27 * ninth // 128) * 128
+    third = 9 * ninth
+
+    def kernel(*refs):
+        w_refs, own_refs, g_refs = refs[:chips], refs[chips : chips + 2], refs[chips + 2 : 3 * chips + 1]
+        out_refs = refs[3 * chips + 1 : 3 * chips + 1 + cores]
+        turned, a_both, g_all, t_even, t_odd, woven, lanes = refs[3 * chips + 1 + cores :]
+        for first in range(0, padded, 128):
+            size = min(128, 27 * ninth - first)
+            value = jnp.concatenate([w[:, first : first + size] for w in w_refs], axis=0)
+            high = value.astype(BF16).astype(F32)
+            value = jnp.concatenate([high, value - high], axis=0)
+            if size < 128:
+                value = jnp.concatenate([value, jnp.zeros((2 * count, 128 - size), F32)], axis=1)
+            turned[first : first + 128, :] = value.T
+        core = lax.axis_index("af") % cores
+        for tap in range(27):
+            for h in range(cores):
+                first = pl.multiple_of(tap * ninth + (core ^ h) * channels, 8)
+                at = (tap * cores + h) * channels
+                a_both[at : at + channels, :] = turned[pl.ds(first, channels), :].astype(BF16)
+        for half in range(2):
+            g_all[2 * half * count : 2 * half * count + filters, :] = own_refs[half][...]
+        for k, g_ref in enumerate(g_refs):
+            side, j = (k + 1) // chips, (k + 1) % chips
+            first = side * 4 * count
+            split_rows(g_ref, filters, out_rows, out_cols, g_all.at[first:], g_all.at[first + 2 * count :], j * filters)
+        for at in range(0, 8 * count, 2 * count):
+            g_all[at + count : at + 2 * count, :] = g_all[at : at + count, :]
+        even = a_both[third : 2 * third, :]
+        t_even[...] = dot(jnp.concatenate([even, even], axis=1), g_all[: 4 * count, :])
+        odd, above = a_both[2 * third :, :], a_both[:third, :]
+        t_odd[...] = dot(jnp.concatenate([odd, odd, above, above], axis=1), g_all[...])
+        taps = column_taps(cols, out_cols)
+        taps = jnp.concatenate([taps, taps], axis=1)
+        for h in reversed(range(cores)):
+            for z, terms in enumerate((t_even, t_odd)):
+                for y in range(rows):
+                    q = y // 2
+                    for dx in range(3):
+
+                        def term(dy, at):
+                            first = (dy * 3 + dx) * ninth + h * channels
+                            return terms[first : first + channels, at * out_cols : (at + 1) * out_cols]
+
+                        if y % 2 == 0:
+                            value = term(1, q)
+                        else:
+                            value = term(2, q)
+                            if q + 1 < out_rows:
+                                value = value + term(0, q + 1)
+                        high, low = halves(value)
+                        first = (z * rows + y) * channels
+                        woven[first : first + channels, dx * out_cols : (dx + 1) * out_cols] = high
+                        woven[first : first + channels, (3 + dx) * out_cols : (4 + dx) * out_cols] = low
+            result = dot_t(woven[...], taps)
+            for half in range(cols // 128):
+                for k in range(planes * rows):
+                    piece = result[k * channels : (k + 1) * channels, half * 128 : (half + 1) * 128]
+                    lanes[pl.ds(k, channels, stride=planes * rows), :] = piece
+                out_refs[h][:, half * 128 : (half + 1) * 128] = lanes[...]
+
+    return pl.pallas_call(
+        kernel,
+        out_shape=[jax.ShapeDtypeStruct((channels * planes * rows, cols), F32)] * cores,
+        scratch_shapes=[
+            pltpu.VMEM((padded, 2 * count), F32),
+            pltpu.VMEM((27 * ninth, 2 * count), BF16),
+            pltpu.VMEM((8 * count, cells), BF16),
+            pltpu.VMEM((third, cells), F32),
+            pltpu.VMEM((third, cells), F32),
+            pltpu.VMEM((planes * rows * channels, 6 * out_cols), BF16),
+            pltpu.VMEM((planes * rows * channels, 128), F32),
+        ],
+        compiler_params=PARAMS,
+        name="input_partial",
+    )(*weights, *own, *[g.reshape(-1, out_cols) for g in grads])
+
+
+def below(value, bits):
+    parts, groups = lax.axis_size("gz"), lax.axis_size("af")
+    pairs = [
+        ((slab + 1) * groups + (a ^ bits), slab * groups + a) for slab in range(parts - 1) for a in range(groups)
+    ]
+    return lax.ppermute(value, ("gz", "af"), pairs)
+
+
+def fast(volume, out_grad, weight):
+    channels, planes, rows, cols = volume.shape
+    filters, out_depth, out_rows, out_cols = out_grad.shape
+    parts, cores = lax.axis_size("gz"), 2
+    factor = 1.0 / math.sqrt(out_depth * parts * out_rows * out_cols)
+    across = swapped(out_grad, "af", cores)
+    above = [below(out_grad, 0), below(out_grad, cores)]
+    mine, theirs = pack_weights(weight, cores, channels)
+    weights = [mine, swapped(theirs, "af", cores)]
+    high, low, *own = gather_taps([volume, swapped(volume, "af", 1)], out_grad)
+    terms = weight_terms(high, low, own, across)
+    sent = weight_partial(high, low, terms, above, parts)
+    arrived = [sent[0]] + [swapped(sent[k], "gz", k) for k in range(1, parts)]
+    inputs = input_partial(weights, own, [across, *above], volume.shape, cores)
+    inputs, arrived = lax.optimization_barrier((inputs, arrived))
+    input_grad = (inputs[0] + swapped(inputs[1], "af", 1)).reshape(volume.shape)
+    sums = add_slabs(arrived, 2)
+    woven = weave_channels([sums[0], swapped(sums[1], "af", cores)], channels, cores, factor)
+    pieces = [woven] + [swapped(woven, "gz", k) for k in range(1, parts)]
+    input_grad, pieces = lax.optimization_barrier((input_grad, pieces))
+    weight_grad = stack_slabs(pieces)
+    return (input_grad, weight_grad)
 
 
 def tap_matrix(extended, out_depth, out_rows, out_cols):
@@ -68,7 +468,7 @@
     return canvas[:, 1 : planes + 1, 1 : rows + 1, 1 : cols + 1]
 
 
-def local(volume, out_grad, weight):
+def general(volume, out_grad, weight):
     channels, planes, rows, cols = volume.shape
     filters, out_depth, out_rows, out_cols = out_grad.shape
     in_total = weight.shape[1] // 27
@@ -114,6 +514,17 @@
     return (input_grad, weight_grad)
 
 
+def local(volume, out_grad, weight):
+    channels, planes, rows, _ = volume.shape
+    filters, out_depth, out_rows, _ = out_grad.shape
+    parts, groups = lax.axis_size("gz"), lax.axis_size("af")
+    powers = parts & (parts - 1) == 0 and groups == 4
+    whole_tiles = channels == 16 and filters % (8 * parts) == 0 and filters == 32
+    if powers and whole_tiles and (planes, out_depth) == (2, 1):
+        return fast(volume, out_grad, weight)
+    return general(volume, out_grad, weight)
+
+
 def solution(mesh):
     return jax.shard_map(
         local,

time: 201 us -> 37.8 us (0.19)
  local copies, waits for them, and re-layouts: 118 us -> 0.93 us
  waiting for transfers between devices: 28.4 us -> 12.7 us
  matrix products: 14.4 us -> 0 us
  between operations: 14.3 us -> 0.73 us
  starting transfers between devices: 5.07 us -> 15.3 us
  blocking collectives: 10.2 us -> 0 us
  other arithmetic: 9.42 us -> 0.86 us
  Pallas kernels: 0 us -> 7.01 us
    unnamed x59 -> x2, local copies, waits for them, and re-layouts: 33.3 us -> 0.93 us
    another operation x3 -> x0, local copies, waits for them, and re-layouts: 28.7 us -> none  [the longest x1 16.1 us: place_terms(): woven = jnp.stack(depth_pairs, axis=2)]
    slice x4 -> x0, local copies, waits for them, and re-layouts: 26.4 us -> none  [the longest x2 20.7 us: tap_matrix(): split[:, dz_lo:dz_lo + out_depth, depth_tap % 2, dy_lo:dy_lo + out_rows,...]
    reshape x3 -> x0, local copies, waits for them, and re-layouts: 19.6 us -> none  [the longest x1 17.7 us: place_terms(): woven.reshape(channels, 2 * (depth_count + 1), 2 * (out_rows + 1), 2 * (o...]
    all_gather x2 -> x0, waiting for transfers between devices: 16.4 us -> none  [the longest x1 16.4 us: local(): portion = lax.all_gather(extended, 'af', axis=0, tiled=True)]
    dot_general x2 -> x0, matrix products: 14.4 us -> none  [the longest x1 10.1 us: local(): lax.dot_general(local_grads, tap_rows, (((1,), (1,)), ((), ())), precisio...]
    ppermute x2 -> x13, starting transfers between devices: 4.95 us -> 15.3 us  [the longest x11 12.7 us: swapped(): lax.ppermute(value, axis, [(source, source ^ bits) for source in range(co...]
    all_gather x1 -> x0, blocking collectives: 10.2 us -> none  [local(): lax.all_gather(weight, 'af', axis=0, tiled=True)]
  transfers between devices with their start and end apart: 5 -> 13, of which waited for: 3 -> 7; matrix products, arithmetic and copies ran while one was open for 28% -> 2% of each run, Pallas kernels for 0% -> 17%
where the time goes in v3:
time: 37.8 us; the launch traced here: 37.6 us
  starting transfers between devices  15.3 us (40%)
  waiting for transfers between devices  12.7 us (34%)
  Pallas kernels  7.01 us (19%)
  local copies, waits for them, and re-layouts  0.93 us (2%)
  other arithmetic  0.86 us (2%)
  between operations  0.73 us (2%)
    ppermute x11, starting transfers between devices, swapped(): lax.ppermute(value, axis, [(source, source ^ bits) for source in range(co...  12.7 us
    ppermute x11, waiting for transfers between devices, swapped(): lax.ppermute(value, axis, [(source, source ^ bits) for source in range(co...  9.18 us
    ppermute x2, waiting for transfers between devices, below(): return lax.ppermute(value, ('gz', 'af'), pairs)  3.55 us
    ppermute x2, starting transfers between devices, below(): return lax.ppermute(value, ('gz', 'af'), pairs)  2.57 us
    pallas_call x1, Pallas kernels, input_partial(): pl.pallas_call(kernel, out_shape=[jax.ShapeDtypeStruct((channels * planes...  2.01 us
    pallas_call x1, Pallas kernels, gather_taps(): pl.pallas_call(kernel, in_specs=[HBM, HBM] + [VMEM] * (cores - 1), out_sh...  1.96 us
    unnamed x2, local copies, waits for them, and re-layouts  0.93 us
    pallas_call x1, Pallas kernels, weight_terms(): pl.pallas_call(kernel, out_shape=jax.ShapeDtypeStruct((2 * filters, high....  0.86 us
  transfers between devices with their start and end apart: 13, of which 7 were waited for; matrix products, arithmetic and copies ran while one was open for 2% of the time, Pallas kernels for 17%

profile of v3, /device:TPU:0, one launch (start us, length us, event | category | flops | bytes accessed | tf_op | source)
XLA Modules:
  0.0 37.6 jit_solution(8604203767293524484)
XLA Ops:
  0.6 0.5 %collective-permute-start.1 = (f32[16,2,16,256]{3,2,1,0:T(8,128)}, f32[16,2,16,256]{3,2,1,0:T(8,128)S(1)}, u32[]{:S(2)}, u32[]{:S(2)}) collective-permute-start(f32[16,2,16,256]{3,2,1,0:T(8,128)} %param.3), channel_id=1, source_target_pairs={{0,1},{1,0},{2,3},{3,2},{4,5},{5,4},{6,7},{7,6},{8,9},{9,8},{10,11... | collective-permute-start | bytes 1572872 | tf_op jit(solution)/shard_map/ppermute | solution.py:25
  1.1 2.6 %collective-permute-start.2 = (f32[32,1,8,128]{3,2,1,0:T(8,128)}, f32[32,1,8,128]{3,2,1,0:T(8,128)S(1)}, u32[]{:S(2)}, u32[]{:S(2)}) collective-permute-start(f32[32,1,8,128]{3,2,1,0:T(8,128)} %param.4), channel_id=1, source_target_pairs={{0,2},{1,3},{2,0},{3,1},{4,6},{5,7},{6,4},{7,5},{8,10},{9,11},{10,... | collective-permute-start | bytes 393224 | tf_op jit(solution)/shard_map/ppermute | solution.py:25
  3.7 1.3 %collective-permute-start.3 = (f32[32,1,8,128]{3,2,1,0:T(8,128)}, f32[32,1,8,128]{3,2,1,0:T(8,128)S(1)}, u32[]{:S(2)}, u32[]{:S(2)}) collective-permute-start(f32[32,1,8,128]{3,2,1,0:T(8,128)} %param.4), channel_id=1, source_target_pairs={{4,0},{5,1},{6,2},{7,3},{8,4},{9,5},{10,6},{11,7},{12,8},{13,9},{1... | collective-permute-start | bytes 393224 | tf_op jit(solution)/shard_map/ppermute | solution.py:388
  5.0 1.3 %collective-permute-start.4 = (f32[32,1,8,128]{3,2,1,0:T(8,128)}, f32[32,1,8,128]{3,2,1,0:T(8,128)S(1)}, u32[]{:S(2)}, u32[]{:S(2)}) collective-permute-start(f32[32,1,8,128]{3,2,1,0:T(8,128)} %param.4), channel_id=1, source_target_pairs={{6,0},{7,1},{4,2},{5,3},{10,4},{11,5},{8,6},{9,7},{14,8},{15,9},{1... | collective-permute-start | bytes 393224 | tf_op jit(solution)/shard_map/ppermute | solution.py:388
  6.3 0.9 %copy-done = f32[32,1728]{1,0:T(8,128)S(1)} copy-done((f32[32,1728]{1,0:T(8,128)S(1)}, f32[32,1728]{1,0:T(8,128)}, u32[]{:S(2)}) %copy-start) | copy-done | bytes 221208
  7.2 0.4 pack_weights.1
  7.6 0.1 collective-permute-start
  7.7 0.0 collective-permute-done.1
  7.7 2.0 %gather_taps.1 = (bf16[576,1024]{1,0:T(8,128)(2,1)S(1)}, bf16[576,1024]{1,0:T(8,128)(2,1)S(1)}, bf16[32,1024]{1,0:T(8,128)(2,1)S(1)}, bf16[32,1024]{1,0:T(8,128)(2,1)S(1)}) custom-call(f32[512,256]{1,0:T(8,128)} %bitcast.16, f32[256,128]{1,0:T(8,128)} %bitcast.18, f32[512,256]{1,0:T(8,128)S(1)} %bitcast.8), custom_call_target="tpu_custom_call" | custom-call | tf_op jit(solution)/shard_map/gather_taps/pallas_call | solution.py:108
  9.7 0.9 %weight_terms.1.terms_ref = f32[64,576]{1,0:T(8,128)S(1)} custom-call(bf16[576,1024]{1,0:T(8,128)(2,1)S(1)} %get-tuple-element.33.high_ref, bf16[576,1024]{1,0:T(8,128)(2,1)S(1)} %get-tuple-element.34.low_ref, bf16[32,1024]{1,0:T(8,128)(2,1)S(1)} %get-tuple-element.29.refs_2_.own_high, bf16[32,1024]{1,0:T(8,128)(2,1)S(1)} %get-tuple-element.30.refs_3_.own_low, ...), custom_call_target="tpu_custom_call" | custom-call | tf_op jit(solution)/shard_map/weight_terms/pallas_call | solution.py:137
  10.6 1.6 %collective-permute-done.3 = f32[32,1,8,128]{3,2,1,0:T(8,128)S(1)} collective-permute-done((f32[32,1,8,128]{3,2,1,0:T(8,128)}, f32[32,1,8,128]{3,2,1,0:T(8,128)S(1)}, u32[]{:S(2)}, u32[]{:S(2)}) %collective-permute-start.3) | collective-permute-done | bytes 131104 | tf_op jit(solution)/shard_map/ppermute | solution.py:388
  12.1 2.0 %collective-permute-done.4 = f32[32,1,8,128]{3,2,1,0:T(8,128)S(1)} collective-permute-done((f32[32,1,8,128]{3,2,1,0:T(8,128)}, f32[32,1,8,128]{3,2,1,0:T(8,128)S(1)}, u32[]{:S(2)}, u32[]{:S(2)}) %collective-permute-start.4) | collective-permute-done | bytes 131104 | tf_op jit(solution)/shard_map/ppermute | solution.py:388
  14.1 0.6 %weight_partial.1 = (f32[16,864]{1,0:T(8,128)S(1)}, f32[16,864]{1,0:T(8,128)S(1)}, f32[16,864]{1,0:T(8,128)S(1)}, f32[16,864]{1,0:T(8,128)S(1)}) custom-call(bf16[576,1024]{1,0:T(8,128)(2,1)S(1)} %get-tuple-element.33.high_ref, bf16[576,1024]{1,0:T(8,128)(2,1)S(1)} %get-tuple-element.34.low_ref, f32[64,576]{1,0:T(8,128)S(1)} %weight_terms.1.terms_ref, ...), custom_call_target="tpu_custom_call" | custom-call | tf_op jit(solution)/shard_map/weight_partial/pallas_call | solution.py:168
  14.7 2.0 %collective-permute-start.5 = (f32[16,864]{1,0:T(8,128)S(1)}, f32[16,864]{1,0:T(8,128)S(1)}, u32[]{:S(2)}, u32[]{:S(2)}) collective-permute-start(f32[16,864]{1,0:T(8,128)S(1)} %get-tuple-element.36), channel_id=1, source_target_pairs={{0,4},{4,0},{8,12},{12,8},{1,5},{5,1},{9,13},{13,9},{2,6},{6,2},{1... | collective-permute-start | bytes 165896 | tf_op jit(solution)/shard_map/ppermute | solution.py:25
  16.7 2.3 %collective-permute-start.6 = (f32[16,864]{1,0:T(8,128)S(1)}, f32[16,864]{1,0:T(8,128)S(1)}, u32[]{:S(2)}, u32[]{:S(2)}) collective-permute-start(f32[16,864]{1,0:T(8,128)S(1)} %get-tuple-element.37), channel_id=1, source_target_pairs={{0,8},{4,12},{8,0},{12,4},{1,9},{5,13},{9,1},{13,5},{2,10},{6,14},... | collective-permute-start | bytes 165896 | tf_op jit(solution)/shard_map/ppermute | solution.py:25
  19.0 0.2 collective-permute-start.7
  19.2 0.0 collective-permute-done.refs_1_
  19.2 2.0 %input_partial.1 = (f32[512,256]{1,0:T(8,128)S(1)}, f32[512,256]{1,0:T(8,128)S(1)}) custom-call(f32[32,864]{1,0:T(8,128)S(1)} %get-tuple-element.27.refs_0_, f32[32,864]{1,0:T(8,128)S(1)} %collective-permute-done.refs_1_, bf16[32,1024]{1,0:T(8,128)(2,1)S(1)} %get-tuple-element.29.refs_2_.own_high, bf16[32,1024]{1,0:T(8,128)(2,1)S(1)} %get-tuple-element.30.refs_3_.own_low, ...), custom_call_target="tpu_custom_call" | custom-call | tf_op jit(solution)/shard_map/input_partial/pallas_call | solution.py:366
  21.2 0.0 collective-permute-done.5.refs_1_
  21.2 1.8 %collective-permute-done.6.refs_2_ = f32[16,864]{1,0:T(8,128)S(1)} collective-permute-done((f32[16,864]{1,0:T(8,128)S(1)}, f32[16,864]{1,0:T(8,128)S(1)}, u32[]{:S(2)}, u32[]{:S(2)}) %collective-permute-start.6) | collective-permute-done | bytes 55328 | tf_op jit(solution)/shard_map/ppermute | solution.py:25
  23.0 1.9 %collective-permute-done.7.refs_3_ = f32[16,864]{1,0:T(8,128)S(1)} collective-permute-done((f32[16,864]{1,0:T(8,128)S(1)}, f32[16,864]{1,0:T(8,128)S(1)}, u32[]{:S(2)}, u32[]{:S(2)}) %collective-permute-start.7) | collective-permute-done | bytes 55328 | tf_op jit(solution)/shard_map/ppermute | solution.py:25
  25.0 0.0 collective-permute-start.8
  25.0 0.6 %collective-permute-start.9 = (f32[8,864]{1,0:T(8,128)S(1)}, f32[8,864]{1,0:T(8,128)S(1)}, u32[]{:S(2)}, u32[]{:S(2)}) collective-permute-start(f32[8,864]{1,0:T(8,128)S(1)} %get-tuple-element.46), channel_id=1, source_target_pairs={{0,2},{1,3},{2,0},{3,1},{4,6},{5,7},{6,4},{7,5},{8,10},{9,11},{10,... | collective-permute-start | bytes 82952 | tf_op jit(solution)/shard_map/ppermute | solution.py:25
  25.6 3.3 %collective-permute-done.9.refs_1_ = f32[8,864]{1,0:T(8,128)S(1)} collective-permute-done((f32[8,864]{1,0:T(8,128)S(1)}, f32[8,864]{1,0:T(8,128)S(1)}, u32[]{:S(2)}, u32[]{:S(2)}) %collective-permute-start.9) | collective-permute-done | bytes 27680 | tf_op jit(solution)/shard_map/ppermute | solution.py:25
  28.9 0.5 %weave_channels.1.refs_0_ = f32[8,1728]{1,0:T(8,128)S(1)} custom-call(f32[8,864]{1,0:T(8,128)S(1)} %get-tuple-element.45.refs_0_, f32[8,864]{1,0:T(8,128)S(1)} %collective-permute-done.9.refs_1_), custom_call_target="tpu_custom_call" | custom-call | tf_op jit(solution)/shard_map/weave_channels/pallas_call | solution.py:236
  29.4 0.0 collective-permute-start.10
  29.5 1.4 %collective-permute-start.11 = (f32[8,1728]{1,0:T(8,128)S(1)}, f32[8,1728]{1,0:T(8,128)S(1)}, u32[]{:S(2)}, u32[]{:S(2)}) collective-permute-start(f32[8,1728]{1,0:T(8,128)S(1)} %weave_channels.1.refs_0_), channel_id=1, source_target_pairs={{0,8},{4,12},{8,0},{12,4},{1,9},{5,13},{9,1},{13,5},{2,10},{6,14},... | collective-permute-start | bytes 165896 | tf_op jit(solution)/shard_map/ppermute | solution.py:25
  30.8 3.0 %collective-permute-start.12 = (f32[8,1728]{1,0:T(8,128)S(1)}, f32[8,1728]{1,0:T(8,128)S(1)}, u32[]{:S(2)}, u32[]{:S(2)}) collective-permute-start(f32[8,1728]{1,0:T(8,128)S(1)} %weave_channels.1.refs_0_), channel_id=1, source_target_pairs={{0,12},{4,8},{8,4},{12,0},{1,13},{5,9},{9,5},{13,1},{2,14},{6,10},... | collective-permute-start | bytes 165896 | tf_op jit(solution)/shard_map/ppermute | solution.py:25
  33.8 0.9 %add.3 = f32[512,256]{1,0:T(8,128)} add(f32[512,256]{1,0:T(8,128)S(1)} %get-tuple-element.39, f32[512,256]{1,0:T(8,128)S(1)} %collective-permute-done.8) | non-fusion elementwise | flops 131072 | bytes 1572864 | tf_op jit(solution)/shard_map/add | solution.py:406
  34.7 0.8 %collective-permute-done.11.refs_2_ = f32[8,1728]{1,0:T(8,128)S(1)} collective-permute-done((f32[8,1728]{1,0:T(8,128)S(1)}, f32[8,1728]{1,0:T(8,128)S(1)}, u32[]{:S(2)}, u32[]{:S(2)}) %collective-permute-start.11) | collective-permute-done | bytes 55328 | tf_op jit(solution)/shard_map/ppermute | solution.py:25
  35.5 1.4 %collective-permute-done.12.refs_3_ = f32[8,1728]{1,0:T(8,128)S(1)} collective-permute-done((f32[8,1728]{1,0:T(8,128)S(1)}, f32[8,1728]{1,0:T(8,128)S(1)}, u32[]{:S(2)}, u32[]{:S(2)}) %collective-permute-start.12) | collective-permute-done | bytes 55328 | tf_op jit(solution)/shard_map/ppermute | solution.py:25
  36.9 0.7 %stack_slabs.1 = f32[4,8,1728]{2,1,0:T(8,128)} custom-call(f32[8,1728]{1,0:T(8,128)S(1)} %weave_channels.1.refs_0_, f32[8,1728]{1,0:T(8,128)S(1)} %collective-permute-done.10.refs_1_, f32[8,1728]{1,0:T(8,128)S(1)} %collective-permute-done.11.refs_2_, f32[8,1728]{1,0:T(8,128)S(1)} %collective-permute-done.12.refs_3_), custom_call_target="tpu_custom_call" | custom-call | tf_op jit(solution)/shard_map/stack_slabs/pallas_call | solution.py:253
  (5 shorter events, 0.0 us)
Async XLA Ops:
  0.6 7.1 %collective-permute-start.1 = (f32[16,2,16,256]{3,2,1,0:T(8,128)}, f32[16,2,16,256]{3,2,1,0:T(8,128)S(1)}, u32[]{:S(2)}, u32[]{:S(2)}) collective-permute-start(f32[16,2,16,256]{3,2,1,0:T(8,128)} %param.3), channel_id=1, source_target_pairs={{0,1},{1,0},{2,3},{3,2},{4,5},{5,4},{6,7},{7,6},{8,9},{9,8},{10,11... | collective-permute-start | bytes 1572872 | tf_op jit(solution)/shard_map/ppermute | solution.py:25
  1.1 8.5 %collective-permute-start.2 = (f32[32,1,8,128]{3,2,1,0:T(8,128)}, f32[32,1,8,128]{3,2,1,0:T(8,128)S(1)}, u32[]{:S(2)}, u32[]{:S(2)}) collective-permute-start(f32[32,1,8,128]{3,2,1,0:T(8,128)} %param.4), channel_id=1, source_target_pairs={{0,2},{1,3},{2,0},{3,1},{4,6},{5,7},{6,4},{7,5},{8,10},{9,11},{10,... | collective-permute-start | bytes 393224 | tf_op jit(solution)/shard_map/ppermute | solution.py:25
  3.7 8.4 %collective-permute-start.3 = (f32[32,1,8,128]{3,2,1,0:T(8,128)}, f32[32,1,8,128]{3,2,1,0:T(8,128)S(1)}, u32[]{:S(2)}, u32[]{:S(2)}) collective-permute-start(f32[32,1,8,128]{3,2,1,0:T(8,128)} %param.4), channel_id=1, source_target_pairs={{4,0},{5,1},{6,2},{7,3},{8,4},{9,5},{10,6},{11,7},{12,8},{13,9},{1... | collective-permute-start | bytes 393224 | tf_op jit(solution)/shard_map/ppermute | solution.py:388
  5.0 9.1 %collective-permute-start.4 = (f32[32,1,8,128]{3,2,1,0:T(8,128)}, f32[32,1,8,128]{3,2,1,0:T(8,128)S(1)}, u32[]{:S(2)}, u32[]{:S(2)}) collective-permute-start(f32[32,1,8,128]{3,2,1,0:T(8,128)} %param.4), channel_id=1, source_target_pairs={{6,0},{7,1},{4,2},{5,3},{10,4},{11,5},{8,6},{9,7},{14,8},{15,9},{1... | collective-permute-start | bytes 393224 | tf_op jit(solution)/shard_map/ppermute | solution.py:388
  6.3 0.9 %copy-start = (f32[32,1728]{1,0:T(8,128)S(1)}, f32[32,1728]{1,0:T(8,128)}, u32[]{:S(2)}) copy-start(f32[32,1728]{1,0:T(8,128)} %w_ref.1) | copy-start | bytes 663556
  7.6 11.6 %collective-permute-start = (f32[32,864]{1,0:T(8,128)S(1)}, f32[32,864]{1,0:T(8,128)S(1)}, u32[]{:S(2)}, u32[]{:S(2)}) collective-permute-start(f32[32,864]{1,0:T(8,128)S(1)} %get-tuple-element.28), channel_id=1, source_target_pairs={{0,2},{1,3},{2,0},{3,1},{4,6},{5,7},{6,4},{7,5},{8,10},{9,11},{10,... | collective-permute-start | bytes 331784 | tf_op jit(solution)/shard_map/ppermute | solution.py:25
  14.7 6.5 %collective-permute-start.5 = (f32[16,864]{1,0:T(8,128)S(1)}, f32[16,864]{1,0:T(8,128)S(1)}, u32[]{:S(2)}, u32[]{:S(2)}) collective-permute-start(f32[16,864]{1,0:T(8,128)S(1)} %get-tuple-element.36), channel_id=1, source_target_pairs={{0,4},{4,0},{8,12},{12,8},{1,5},{5,1},{9,13},{13,9},{2,6},{6,2},{1... | collective-permute-start | bytes 165896 | tf_op jit(solution)/shard_map/ppermute | solution.py:25
  16.7 6.3 %collective-permute-start.6 = (f32[16,864]{1,0:T(8,128)S(1)}, f32[16,864]{1,0:T(8,128)S(1)}, u32[]{:S(2)}, u32[]{:S(2)}) collective-permute-start(f32[16,864]{1,0:T(8,128)S(1)} %get-tuple-element.37), channel_id=1, source_target_pairs={{0,8},{4,12},{8,0},{12,4},{1,9},{5,13},{9,1},{13,5},{2,10},{6,14},... | collective-permute-start | bytes 165896 | tf_op jit(solution)/shard_map/ppermute | solution.py:25
  19.0 6.0 %collective-permute-start.7 = (f32[16,864]{1,0:T(8,128)S(1)}, f32[16,864]{1,0:T(8,128)S(1)}, u32[]{:S(2)}, u32[]{:S(2)}) collective-permute-start(f32[16,864]{1,0:T(8,128)S(1)} %get-tuple-element.38), channel_id=1, source_target_pairs={{0,12},{4,8},{8,4},{12,0},{1,13},{5,9},{9,5},{13,1},{2,14},{6,10},... | collective-permute-start | bytes 165896 | tf_op jit(solution)/shard_map/ppermute | solution.py:25
  25.0 8.9 %collective-permute-start.8 = (f32[512,256]{1,0:T(8,128)S(1)}, f32[512,256]{1,0:T(8,128)S(1)}, u32[]{:S(2)}, u32[]{:S(2)}) collective-permute-start(f32[512,256]{1,0:T(8,128)S(1)} %get-tuple-element.40), channel_id=1, source_target_pairs={{0,1},{1,0},{2,3},{3,2},{4,5},{5,4},{6,7},{7,6},{8,9},{9,8},{10,11... | collective-permute-start | bytes 1572872 | tf_op jit(solution)/shard_map/ppermute | solution.py:25
  25.0 3.9 %collective-permute-start.9 = (f32[8,864]{1,0:T(8,128)S(1)}, f32[8,864]{1,0:T(8,128)S(1)}, u32[]{:S(2)}, u32[]{:S(2)}) collective-permute-start(f32[8,864]{1,0:T(8,128)S(1)} %get-tuple-element.46), channel_id=1, source_target_pairs={{0,2},{1,3},{2,0},{3,1},{4,6},{5,7},{6,4},{7,5},{8,10},{9,11},{10,... | collective-permute-start | bytes 82952 | tf_op jit(solution)/shard_map/ppermute | solution.py:25
  29.4 5.3 %collective-permute-start.10 = (f32[8,1728]{1,0:T(8,128)S(1)}, f32[8,1728]{1,0:T(8,128)S(1)}, u32[]{:S(2)}, u32[]{:S(2)}) collective-permute-start(f32[8,1728]{1,0:T(8,128)S(1)} %weave_channels.1.refs_0_), channel_id=1, source_target_pairs={{0,4},{4,0},{8,12},{12,8},{1,5},{5,1},{9,13},{13,9},{2,6},{6,2},{1... | collective-permute-start | bytes 165896 | tf_op jit(solution)/shard_map/ppermute | solution.py:25
  29.5 6.0 %collective-permute-start.11 = (f32[8,1728]{1,0:T(8,128)S(1)}, f32[8,1728]{1,0:T(8,128)S(1)}, u32[]{:S(2)}, u32[]{:S(2)}) collective-permute-start(f32[8,1728]{1,0:T(8,128)S(1)} %weave_channels.1.refs_0_), channel_id=1, source_target_pairs={{0,8},{4,12},{8,0},{12,4},{1,9},{5,13},{9,1},{13,5},{2,10},{6,14},... | collective-permute-start | bytes 165896 | tf_op jit(solution)/shard_map/ppermute | solution.py:25
  30.8 6.0 %collective-permute-start.12 = (f32[8,1728]{1,0:T(8,128)S(1)}, f32[8,1728]{1,0:T(8,128)S(1)}, u32[]{:S(2)}, u32[]{:S(2)}) collective-permute-start(f32[8,1728]{1,0:T(8,128)S(1)} %weave_channels.1.refs_0_), channel_id=1, source_target_pairs={{0,12},{4,8},{8,4},{12,0},{1,13},{5,9},{9,5},{13,1},{2,14},{6,10},... | collective-permute-start | bytes 165896 | tf_op jit(solution)/shard_map/ppermute | solution.py:25

commit v4 on v3

--- a/solution.py
+++ b/solution.py
@@ -29,6 +29,11 @@
     return pltpu.with_memory_space_constraint(value, pltpu.HBM)
 
 
+def turned_by(value, axis, steps):
+    count = lax.axis_size(axis)
+    return lax.ppermute(value, axis, [(source, (source + steps) % count) for source in range(count)])
+
+
 def halves(value):
     high = value.astype(BF16)
     return high, (value - high.astype(F32)).astype(BF16)
@@ -56,23 +61,51 @@
             target[first : first + filters, q * out_cols : (q + 1) * out_cols] = half
 
 
-def gather_taps(volumes, out_grad):
+def pack_columns(w_ref, targets, total, kept, sides):
+    filters, width = w_ref.shape
+    span = 128 * total // kept
+    row = lax.broadcasted_iota(jnp.int32, (span, 128), 0)
+    col = lax.broadcasted_iota(jnp.int32, (span, 128), 1)
+    start = (col // kept) * total + col % kept
+    places = [jnp.where(row == start + side * kept, 1.0, 0.0).astype(BF16) for side in sides]
+    for first in range(0, width, span):
+        size = min(span, width - first)
+        value = w_ref[:, first : first + size]
+        if size < span:
+            value = jnp.concatenate([value, jnp.zeros((filters, span - size), F32)], axis=1)
+        high = value.astype(BF16).astype(F32)
+        rest = value - high
+        middle = rest.astype(BF16).astype(F32)
+        stacked = jnp.concatenate([high, middle, rest - middle], axis=0).astype(BF16)
+        at = first * kept // total
+        for place, target in zip(places, targets):
+            packed = dot(stacked, place)
+            result = packed[:filters] + packed[filters : 2 * filters] + packed[2 * filters :]
+            last = min(128, 27 * kept - at)
+            target[:, at : at + last] = result[:, :last]
+
+
+def prepare(volumes, out_grad, weight):
     filters, _, out_rows, out_cols = out_grad.shape
     channels, planes, rows, cols = volumes[0].shape
     cores = len(volumes)
     count = planes * rows * channels
     width = planes * 9 * cores * channels
     cells = out_rows * out_cols
-
-    def kernel(v_hbm, g_hbm, *refs):
+    total, kept = weight.shape[1] // 27, cores * channels
+
+    def kernel(v_hbm, g_hbm, w_hbm, *refs):
         v_refs = refs[: cores - 1]
         targets, g_targets = refs[cores - 1 : cores + 1], refs[cores + 1 : cores + 3]
-        x_refs, d_refs = refs[cores + 3 : cores + 5], refs[cores + 5 : cores + 7]
-        own_lanes, lanes, g_ref, sems = refs[cores + 7 :]
+        w_targets = refs[cores + 3 : cores + 5]
+        x_refs, d_refs = refs[cores + 5 : cores + 7], refs[cores + 7 : cores + 9]
+        own_lanes, lanes, g_ref, w_ref, sems = refs[cores + 9 :]
         copies = [
             pltpu.make_async_copy(v_hbm.at[:, h * 128 : (h + 1) * 128], own_lanes.at[h], sems.at[h])
             for h in range(cols // 128)
-        ] + [pltpu.make_async_copy(g_hbm, g_ref, sems.at[cols // 128])]
+        ]
+        copies.append(pltpu.make_async_copy(g_hbm, g_ref, sems.at[cols // 128]))
+        copies.append(pltpu.make_async_copy(w_hbm, w_ref, sems.at[cols // 128 + 1]))
         for copy in copies:
             copy.start()
         taps = column_taps(cols, out_cols)
@@ -104,23 +137,27 @@
                                     piece = d_ref[first : first + channels, dx * out_cols : (dx + 1) * out_cols]
                                 target[at : at + channels, q * out_cols : (q + 1) * out_cols] = piece
         split_rows(g_ref, filters, out_rows, out_cols, *g_targets)
-
-    return pl.pallas_call(
-        kernel,
-        in_specs=[HBM, HBM] + [VMEM] * (cores - 1),
+        chip = lax.axis_index("af") // cores
+        pack_columns(w_ref, w_targets, total, kept, (chip, 1 - chip))
+
+    return pl.pallas_call(
+        kernel,
+        in_specs=[HBM, HBM, HBM] + [VMEM] * (cores - 1),
         out_shape=[jax.ShapeDtypeStruct((width, cells), BF16)] * 2
-        + [jax.ShapeDtypeStruct((filters, cells), BF16)] * 2,
+        + [jax.ShapeDtypeStruct((filters, cells), BF16)] * 2
+        + [jax.ShapeDtypeStruct((filters, 27 * kept), F32)] * 2,
         scratch_shapes=[pltpu.VMEM((count, cols), BF16)] * 2
         + [pltpu.VMEM((count, 3 * out_cols), BF16)] * 2
         + [
             pltpu.VMEM((cols // 128, count, 128), F32),
             pltpu.VMEM((count, 128), F32),
             pltpu.VMEM((filters * out_rows, out_cols), F32),
-            pltpu.SemaphoreType.DMA((cols // 128 + 1,)),
+            pltpu.VMEM(weight.shape, F32),
+            pltpu.SemaphoreType.DMA((cols // 128 + 2,)),
         ],
         compiler_params=PARAMS,
-        name="gather_taps",
-    )(in_hbm(volumes[0].reshape(-1, cols)), in_hbm(out_grad.reshape(-1, out_cols)), *[v.reshape(-1, cols) for v in volumes[1:]])
+        name="prepare",
+    )(in_hbm(volumes[0].reshape(-1, cols)), in_hbm(out_grad.reshape(-1, out_cols)), in_hbm(weight), *[v.reshape(-1, cols) for v in volumes[1:]])
 
 
 def weight_terms(high, low, own, across):
@@ -162,7 +199,7 @@
         slab = lax.axis_index("gz")
         for k in range(parts):
             for j in range(chips):
-                first = pl.multiple_of(j * filters + (slab ^ k) * block, 8)
+                first = pl.multiple_of(j * filters + lax.rem(slab + k, parts) * block, 8)
                 out_refs[k][j * block : (j + 1) * block, :] = total[pl.ds(first, block), :]
 
     return pl.pallas_call(
@@ -196,7 +233,19 @@
     )(*pieces)
 
 
-def weave_channels(pieces, channels, cores, factor):
+def channel_places(me, chips, cores, channels):
+    total = chips * cores * channels
+    taps = 128 // (cores * channels)
+    row = lax.broadcasted_iota(jnp.int32, (chips * 128, taps * total), 0)
+    col = lax.broadcasted_iota(jnp.int32, (chips * 128, taps * total), 1)
+    j = row // 128
+    inner = row - j * 128
+    tap = inner // (cores * channels)
+    owner = me ^ (j * cores + (inner // channels) % cores)
+    return jnp.where(col == tap * total + owner * channels + inner % channels, 1.0, 0.0).astype(BF16)
+
+
+def weave_channels(pieces, place, channels, cores, factor):
     chips = len(pieces)
     block, width = pieces[0].shape
     total = chips * cores * channels
@@ -204,16 +253,8 @@
     taps = span // (cores * channels)
     chunks = -(-width // span)
 
-    def kernel(*refs):
-        me = lax.axis_index("af")
-        row = lax.broadcasted_iota(jnp.int32, (chips * span, taps * total), 0)
-        col = lax.broadcasted_iota(jnp.int32, (chips * span, taps * total), 1)
-        j = row // span
-        inner = row - j * span
-        tap = inner // (cores * channels)
-        core = (inner // channels) % cores
-        owner = me ^ (j * cores + core)
-        place = jnp.where(col == tap * total + owner * channels + inner % channels, 1.0, 0.0).astype(BF16)
+    def kernel(place_ref, *refs):
+        place = place_ref[...]
         for c in range(chunks):
             size = min(span, width - c * span)
             columns = []
@@ -238,7 +279,7 @@
         out_shape=jax.ShapeDtypeStruct((block, 27 * total), F32),
         compiler_params=PARAMS,
         name="weave_channels",
-    )(*pieces)
+    )(place, *pieces)
 
 
 def stack_slabs(pieces):
@@ -248,7 +289,7 @@
     def kernel(*refs):
         slab = lax.axis_index("gz")
         for k in range(parts):
-            refs[parts][slab ^ k] = refs[k][...]
+            refs[parts][lax.rem(slab + parts - k, parts)] = refs[k][...]
 
     return pl.pallas_call(
         kernel,
@@ -256,42 +297,6 @@
         compiler_params=PARAMS,
         name="stack_slabs",
     )(*pieces).reshape(parts * block, width)
-
-
-def pack_weights(weight, cores, channels):
-    filters, width = weight.shape
-    total = width // 27
-    kept = cores * channels
-    span = 128 * total // kept
-    chunks = -(-width // span)
-
-    def kernel(w_ref, own_ref, other_ref):
-        chip = lax.axis_index("af") // cores
-        row = lax.broadcasted_iota(jnp.int32, (span, 128), 0)
-        col = lax.broadcasted_iota(jnp.int32, (span, 128), 1)
-        start = (col // kept) * total + col % kept
-        for target, side in ((own_ref, chip), (other_ref, 1 - chip)):
-            place = jnp.where(row == start + side * kept, 1.0, 0.0).astype(BF16)
-            for c in range(chunks):
-                size = min(span, width - c * span)
-                value = w_ref[:, c * span : c * span + size]
-                if size < span:
-                    value = jnp.concatenate([value, jnp.zeros((filters, span - size), F32)], axis=1)
-                high = value.astype(BF16).astype(F32)
-                rest = value - high
-                middle = rest.astype(BF16).astype(F32)
-                stacked = jnp.concatenate([high, middle, rest - middle], axis=0).astype(BF16)
-                packed = dot(stacked, place)
-                result = packed[:filters] + packed[filters : 2 * filters] + packed[2 * filters :]
-                last = min(128, 27 * kept - c * 128)
-                target[:, c * 128 : c * 128 + last] = result[:, :last]
-
-    return pl.pallas_call(
-        kernel,
-        out_shape=[jax.ShapeDtypeStruct((filters, 27 * kept), F32)] * 2,
-        compiler_params=PARAMS,
-        name="pack_weights",
-    )(weight)
 
 
 def input_partial(weights, own, grads, volume_shape, cores):
@@ -306,8 +311,10 @@
 
     def kernel(*refs):
         w_refs, own_refs, g_refs = refs[:chips], refs[chips : chips + 2], refs[chips + 2 : 3 * chips + 1]
-        out_refs = refs[3 * chips + 1 : 3 * chips + 1 + cores]
-        turned, a_both, g_all, t_even, t_odd, woven, lanes = refs[3 * chips + 1 + cores :]
+        out_refs, place_ref = refs[3 * chips + 1 : 3 * chips + 1 + cores], refs[3 * chips + 1 + cores]
+        turned, a_both, g_all, t_even, t_odd, woven, lanes = refs[3 * chips + 2 + cores :]
+        me = lax.axis_index("af")
+        place_ref[...] = channel_places(me, chips, cores, channels)
         for first in range(0, padded, 128):
             size = min(128, 27 * ninth - first)
             value = jnp.concatenate([w[:, first : first + size] for w in w_refs], axis=0)
@@ -316,7 +323,7 @@
             if size < 128:
                 value = jnp.concatenate([value, jnp.zeros((2 * count, 128 - size), F32)], axis=1)
             turned[first : first + 128, :] = value.T
-        core = lax.axis_index("af") % cores
+        core = me % cores
         for tap in range(27):
             for h in range(cores):
                 first = pl.multiple_of(tap * ninth + (core ^ h) * channels, 8)
@@ -325,7 +332,7 @@
         for half in range(2):
             g_all[2 * half * count : 2 * half * count + filters, :] = own_refs[half][...]
         for k, g_ref in enumerate(g_refs):
-            side, j = (k + 1) // chips, (k + 1) % chips
+            side, j = (1, k) if k < chips else (0, k - chips + 1)
             first = side * 4 * count
             split_rows(g_ref, filters, out_rows, out_cols, g_all.at[first:], g_all.at[first + 2 * count :], j * filters)
         for at in range(0, 8 * count, 2 * count):
@@ -365,7 +372,8 @@
 
     return pl.pallas_call(
         kernel,
-        out_shape=[jax.ShapeDtypeStruct((channels * planes * rows, cols), F32)] * cores,
+        out_shape=[jax.ShapeDtypeStruct((channels * planes * rows, cols), F32)] * cores
+        + [jax.ShapeDtypeStruct((chips * 128, 128 * chips), BF16)],
         scratch_shapes=[
             pltpu.VMEM((padded, 2 * count), F32),
             pltpu.VMEM((27 * ninth, 2 * count), BF16),
@@ -395,18 +403,18 @@
     factor = 1.0 / math.sqrt(out_depth * parts * out_rows * out_cols)
     across = swapped(out_grad, "af", cores)
     above = [below(out_grad, 0), below(out_grad, cores)]
-    mine, theirs = pack_weights(weight, cores, channels)
+    high, low, *own, mine, theirs = prepare([volume, swapped(volume, "af", 1)], out_grad, weight)
     weights = [mine, swapped(theirs, "af", cores)]
-    high, low, *own = gather_taps([volume, swapped(volume, "af", 1)], out_grad)
     terms = weight_terms(high, low, own, across)
     sent = weight_partial(high, low, terms, above, parts)
-    arrived = [sent[0]] + [swapped(sent[k], "gz", k) for k in range(1, parts)]
-    inputs = input_partial(weights, own, [across, *above], volume.shape, cores)
+    arrived = [sent[0]] + [turned_by(sent[k], "gz", k) for k in (1, 3, 2)]
+    *inputs, place = input_partial(weights, own, [*above, across], volume.shape, cores)
     inputs, arrived = lax.optimization_barrier((inputs, arrived))
     input_grad = (inputs[0] + swapped(inputs[1], "af", 1)).reshape(volume.shape)
     sums = add_slabs(arrived, 2)
-    woven = weave_channels([sums[0], swapped(sums[1], "af", cores)], channels, cores, factor)
-    pieces = [woven] + [swapped(woven, "gz", k) for k in range(1, parts)]
+    woven = weave_channels([sums[0], swapped(sums[1], "af", cores)], place, channels, cores, factor)
+    gathered = {k: turned_by(woven, "gz", k) for k in (1, 2, 3)}
+    pieces = [woven] + [gathered[k] for k in range(1, parts)]
     input_grad, pieces = lax.optimization_barrier((input_grad, pieces))
     weight_grad = stack_slabs(pieces)
     return (input_grad, weight_grad)

time: 37.8 us -> 36.2 us (0.958)
  waiting for transfers between devices: 12.7 us -> 11.3 us
  starting transfers between devices: 15.3 us -> 16.3 us
  local copies, waits for them, and re-layouts: 0.93 us -> 0 us
    ppermute x0 -> x6, starting transfers between devices: none -> 9.03 us  [turned_by(): lax.ppermute(value, axis, [(source, (source + steps) % count) for source...]
    ppermute x11 -> x5, starting transfers between devices: 12.7 us -> 4.69 us  [swapped(): lax.ppermute(value, axis, [(source, source ^ bits) for source in range(co...]
    ppermute x11 -> x5, waiting for transfers between devices: 9.18 us -> 2.42 us  [swapped(): lax.ppermute(value, axis, [(source, source ^ bits) for source in range(co...]
    ppermute x0 -> x6, waiting for transfers between devices: none -> 4.27 us  [turned_by(): lax.ppermute(value, axis, [(source, (source + steps) % count) for source...]
    ppermute x2, waiting for transfers between devices: 3.55 us -> 4.58 us  [below(): return lax.ppermute(value, ('gz', 'af'), pairs)]
    unnamed x2 -> x0, local copies, waits for them, and re-layouts: 0.93 us -> none
    pallas_call x2 -> x1, Pallas kernels: 2.32 us -> 2.24 us  [prepare(): pl.pallas_call(kernel, in_specs=[HBM, HBM, HBM] + [VMEM] * (cores - 1), o...]
  transfers between devices with their start and end apart: 13 -> 13, of which waited for: 7 -> 6; matrix products, arithmetic and copies ran while one was open for 2% -> 2% of each run, Pallas kernels for 17% -> 17%
where the time goes in v4:
time: 36.2 us; the launch traced here: 36 us
  starting transfers between devices  16.3 us (45%)
  waiting for transfers between devices  11.3 us (31%)
  Pallas kernels  6.86 us (19%)
  other arithmetic  0.86 us (2%)
  between operations  0.72 us (2%)
    ppermute x6, starting transfers between devices, turned_by(): lax.ppermute(value, axis, [(source, (source + steps) % count) for source...  9.03 us
    ppermute x5, starting transfers between devices, swapped(): lax.ppermute(value, axis, [(source, source ^ bits) for source in range(co...  4.69 us
    ppermute x2, waiting for transfers between devices, below(): return lax.ppermute(value, ('gz', 'af'), pairs)  4.58 us
    ppermute x6, waiting for transfers between devices, turned_by(): lax.ppermute(value, axis, [(source, (source + steps) % count) for source...  4.27 us
    ppermute x2, starting transfers between devices, below(): return lax.ppermute(value, ('gz', 'af'), pairs)  2.57 us
    ppermute x5, waiting for transfers between devices, swapped(): lax.ppermute(value, axis, [(source, source ^ bits) for source in range(co...  2.42 us
    pallas_call x1, Pallas kernels, prepare(): pl.pallas_call(kernel, in_specs=[HBM, HBM, HBM] + [VMEM] * (cores - 1), o...  2.24 us
    pallas_call x1, Pallas kernels, input_partial(): pl.pallas_call(kernel, out_shape=[jax.ShapeDtypeStruct((channels * planes...  2.17 us
  transfers between devices with their start and end apart: 13, of which 6 were waited for; matrix products, arithmetic and copies ran while one was open for 2% of the time, Pallas kernels for 17%

profile of v4, /device:TPU:0, one launch (start us, length us, event | category | flops | bytes accessed | tf_op | source)
XLA Modules:
  0.0 36.0 jit_solution(17702967773385841154)
XLA Ops:
  0.6 0.5 %collective-permute-start = (f32[16,2,16,256]{3,2,1,0:T(8,128)}, f32[16,2,16,256]{3,2,1,0:T(8,128)S(1)}, u32[]{:S(2)}, u32[]{:S(2)}) collective-permute-start(f32[16,2,16,256]{3,2,1,0:T(8,128)} %param.3), channel_id=1, source_target_pairs={{0,1},{1,0},{2,3},{3,2},{4,5},{5,4},{6,7},{7,6},{8,9},{9,8},{10,11... | collective-permute-start | bytes 1572872 | tf_op jit(solution)/shard_map/ppermute | solution.py:25
  1.1 2.6 %collective-permute-start.4 = (f32[32,1,8,128]{3,2,1,0:T(8,128)}, f32[32,1,8,128]{3,2,1,0:T(8,128)S(1)}, u32[]{:S(2)}, u32[]{:S(2)}) collective-permute-start(f32[32,1,8,128]{3,2,1,0:T(8,128)} %param.4), channel_id=1, source_target_pairs={{0,2},{1,3},{2,0},{3,1},{4,6},{5,7},{6,4},{7,5},{8,10},{9,11},{10,... | collective-permute-start | bytes 393224 | tf_op jit(solution)/shard_map/ppermute | solution.py:25
  3.7 1.3 %collective-permute-start.2 = (f32[32,1,8,128]{3,2,1,0:T(8,128)}, f32[32,1,8,128]{3,2,1,0:T(8,128)S(1)}, u32[]{:S(2)}, u32[]{:S(2)}) collective-permute-start(f32[32,1,8,128]{3,2,1,0:T(8,128)} %param.4), channel_id=1, source_target_pairs={{4,0},{5,1},{6,2},{7,3},{8,4},{9,5},{10,6},{11,7},{12,8},{13,9},{1... | collective-permute-start | bytes 393224 | tf_op jit(solution)/shard_map/ppermute | solution.py:396
  5.0 1.3 %collective-permute-start.3 = (f32[32,1,8,128]{3,2,1,0:T(8,128)}, f32[32,1,8,128]{3,2,1,0:T(8,128)S(1)}, u32[]{:S(2)}, u32[]{:S(2)}) collective-permute-start(f32[32,1,8,128]{3,2,1,0:T(8,128)} %param.4), channel_id=1, source_target_pairs={{6,0},{7,1},{4,2},{5,3},{10,4},{11,5},{8,6},{9,7},{14,8},{15,9},{1... | collective-permute-start | bytes 393224 | tf_op jit(solution)/shard_map/ppermute | solution.py:396
  6.3 0.0 collective-permute-done
  6.3 2.2 %prepare.1 = (bf16[576,1024]{1,0:T(8,128)(2,1)S(1)}, bf16[576,1024]{1,0:T(8,128)(2,1)S(1)}, bf16[32,1024]{1,0:T(8,128)(2,1)S(1)}, bf16[32,1024]{1,0:T(8,128)(2,1...) custom-call(f32[512,256]{1,0:T(8,128)} %bitcast.16, f32[256,128]{1,0:T(8,128)} %bitcast.18, f32[32,1728]{1,0:T(8,128)} %w_hbm.1, ...), custom_call_target="tpu_custom_call" | custom-call | tf_op jit(solution)/shard_map/prepare/pallas_call | solution.py:143
  8.6 0.1 collective-permute-start.1
  8.7 0.0 collective-permute-done.4
  8.7 0.9 %weight_terms.1.terms_ref = f32[64,576]{1,0:T(8,128)S(1)} custom-call(bf16[576,1024]{1,0:T(8,128)(2,1)S(1)} %get-tuple-element.34.high_ref, bf16[576,1024]{1,0:T(8,128)(2,1)S(1)} %get-tuple-element.35.low_ref, bf16[32,1024]{1,0:T(8,128)(2,1)S(1)} %get-tuple-element.30.refs_2_.own_high, bf16[32,1024]{1,0:T(8,128)(2,1)S(1)} %get-tuple-element.31.refs_3_.own_low, ...), custom_call_target="tpu_custom_call" | custom-call | tf_op jit(solution)/shard_map/weight_terms/pallas_call | solution.py:174
  9.5 2.6 %collective-permute-done.2 = f32[32,1,8,128]{3,2,1,0:T(8,128)S(1)} collective-permute-done((f32[32,1,8,128]{3,2,1,0:T(8,128)}, f32[32,1,8,128]{3,2,1,0:T(8,128)S(1)}, u32[]{:S(2)}, u32[]{:S(2)}) %collective-permute-start.2) | collective-permute-done | bytes 131104 | tf_op jit(solution)/shard_map/ppermute | solution.py:396
  12.1 2.0 %collective-permute-done.3 = f32[32,1,8,128]{3,2,1,0:T(8,128)S(1)} collective-permute-done((f32[32,1,8,128]{3,2,1,0:T(8,128)}, f32[32,1,8,128]{3,2,1,0:T(8,128)S(1)}, u32[]{:S(2)}, u32[]{:S(2)}) %collective-permute-start.3) | collective-permute-done | bytes 131104 | tf_op jit(solution)/shard_map/ppermute | solution.py:396
  14.1 0.6 %weight_partial.1 = (f32[16,864]{1,0:T(8,128)S(1)}, f32[16,864]{1,0:T(8,128)S(1)}, f32[16,864]{1,0:T(8,128)S(1)}, f32[16,864]{1,0:T(8,128)S(1)}) custom-call(bf16[576,1024]{1,0:T(8,128)(2,1)S(1)} %get-tuple-element.34.high_ref, bf16[576,1024]{1,0:T(8,128)(2,1)S(1)} %get-tuple-element.35.low_ref, f32[64,576]{1,0:T(8,128)S(1)} %weight_terms.1.terms_ref, ...), custom_call_target="tpu_custom_call" | custom-call | tf_op jit(solution)/shard_map/weight_partial/pallas_call | solution.py:205
  14.7 2.0 %collective-permute-start.5 = (f32[16,864]{1,0:T(8,128)S(1)}, f32[16,864]{1,0:T(8,128)S(1)}, u32[]{:S(2)}, u32[]{:S(2)}) collective-permute-start(f32[16,864]{1,0:T(8,128)S(1)} %get-tuple-element.37), channel_id=1, source_target_pairs={{0,4},{4,8},{8,12},{12,0},{1,5},{5,9},{9,13},{13,1},{2,6},{6,10},{... | collective-permute-start | bytes 165896 | tf_op jit(solution)/shard_map/ppermute | solution.py:34
  16.7 1.9 %collective-permute-start.6 = (f32[16,864]{1,0:T(8,128)S(1)}, f32[16,864]{1,0:T(8,128)S(1)}, u32[]{:S(2)}, u32[]{:S(2)}) collective-permute-start(f32[16,864]{1,0:T(8,128)S(1)} %get-tuple-element.38), channel_id=1, source_target_pairs={{0,12},{4,0},{8,4},{12,8},{1,13},{5,1},{9,5},{13,9},{2,14},{6,2},{... | collective-permute-start | bytes 165896 | tf_op jit(solution)/shard_map/ppermute | solution.py:34
  18.6 1.1 %collective-permute-start.7 = (f32[16,864]{1,0:T(8,128)S(1)}, f32[16,864]{1,0:T(8,128)S(1)}, u32[]{:S(2)}, u32[]{:S(2)}) collective-permute-start(f32[16,864]{1,0:T(8,128)S(1)} %get-tuple-element.39), channel_id=1, source_target_pairs={{0,8},{4,12},{8,0},{12,4},{1,9},{5,13},{9,1},{13,5},{2,10},{6,14},... | collective-permute-start | bytes 165896 | tf_op jit(solution)/shard_map/ppermute | solution.py:34
  19.7 2.2 %input_partial.1 = (f32[512,256]{1,0:T(8,128)S(1)}, f32[512,256]{1,0:T(8,128)S(1)}, bf16[256,256]{1,0:T(8,128)(2,1)S(1)}) custom-call(f32[32,864]{1,0:T(8,128)S(1)} %get-tuple-element.28.refs_0_, f32[32,864]{1,0:T(8,128)S(1)} %collective-permute-done.1.refs_1_, bf16[32,1024]{1,0:T(8,128)(2,1)S(1)} %get-tuple-element.30.refs_2_.own_high, ...), custom_call_target="tpu_custom_call" | custom-call | tf_op jit(solution)/shard_map/input_partial/pallas_call | solution.py:373
  21.9 0.0 collective-permute-done.5.refs_1_
  21.9 0.0 collective-permute-done.6.refs_2_
  21.9 1.9 %collective-permute-done.7.refs_3_ = f32[16,864]{1,0:T(8,128)S(1)} collective-permute-done((f32[16,864]{1,0:T(8,128)S(1)}, f32[16,864]{1,0:T(8,128)S(1)}, u32[]{:S(2)}, u32[]{:S(2)}) %collective-permute-start.7) | collective-permute-done | bytes 55328 | tf_op jit(solution)/shard_map/ppermute | solution.py:34
  23.8 0.0 collective-permute-start.8
  23.9 1.5 %collective-permute-start.9 = (f32[8,864]{1,0:T(8,128)S(1)}, f32[8,864]{1,0:T(8,128)S(1)}, u32[]{:S(2)}, u32[]{:S(2)}) collective-permute-start(f32[8,864]{1,0:T(8,128)S(1)} %get-tuple-element.48), channel_id=1, source_target_pairs={{0,2},{1,3},{2,0},{3,1},{4,6},{5,7},{6,4},{7,5},{8,10},{9,11},{10,... | collective-permute-start | bytes 82952 | tf_op jit(solution)/shard_map/ppermute | solution.py:25
  25.4 2.4 %collective-permute-done.9.refs_1_ = f32[8,864]{1,0:T(8,128)S(1)} collective-permute-done((f32[8,864]{1,0:T(8,128)S(1)}, f32[8,864]{1,0:T(8,128)S(1)}, u32[]{:S(2)}, u32[]{:S(2)}) %collective-permute-start.9) | collective-permute-done | bytes 27680 | tf_op jit(solution)/shard_map/ppermute | solution.py:25
  27.8 0.3 weave_channels.1.refs_0_
  28.1 0.0 collective-permute-start.10
  28.1 2.7 %collective-permute-start.11 = (f32[8,1728]{1,0:T(8,128)S(1)}, f32[8,1728]{1,0:T(8,128)S(1)}, u32[]{:S(2)}, u32[]{:S(2)}) collective-permute-start(f32[8,1728]{1,0:T(8,128)S(1)} %weave_channels.1.refs_0_), channel_id=1, source_target_pairs={{0,8},{4,12},{8,0},{12,4},{1,9},{5,13},{9,1},{13,5},{2,10},{6,14},... | collective-permute-start | bytes 165896 | tf_op jit(solution)/shard_map/ppermute | solution.py:34
  30.8 1.3 %collective-permute-start.12 = (f32[8,1728]{1,0:T(8,128)S(1)}, f32[8,1728]{1,0:T(8,128)S(1)}, u32[]{:S(2)}, u32[]{:S(2)}) collective-permute-start(f32[8,1728]{1,0:T(8,128)S(1)} %weave_channels.1.refs_0_), channel_id=1, source_target_pairs={{0,12},{4,0},{8,4},{12,8},{1,13},{5,1},{9,5},{13,9},{2,14},{6,2},{... | collective-permute-start | bytes 165896 | tf_op jit(solution)/shard_map/ppermute | solution.py:34
  32.1 0.0 collective-permute-done.8
  32.1 0.9 %add.3 = f32[512,256]{1,0:T(8,128)} add(f32[512,256]{1,0:T(8,128)S(1)} %get-tuple-element.40, f32[512,256]{1,0:T(8,128)S(1)} %collective-permute-done.8) | non-fusion elementwise | flops 131072 | bytes 1572864 | tf_op jit(solution)/shard_map/add | solution.py:413
  33.0 1.4 %collective-permute-done.10.refs_1_ = f32[8,1728]{1,0:T(8,128)S(1)} collective-permute-done((f32[8,1728]{1,0:T(8,128)S(1)}, f32[8,1728]{1,0:T(8,128)S(1)}, u32[]{:S(2)}, u32[]{:S(2)}) %collective-permute-start.10) | collective-permute-done | bytes 55328 | tf_op jit(solution)/shard_map/ppermute | solution.py:34
  34.3 1.0 %collective-permute-done.11.refs_2_ = f32[8,1728]{1,0:T(8,128)S(1)} collective-permute-done((f32[8,1728]{1,0:T(8,128)S(1)}, f32[8,1728]{1,0:T(8,128)S(1)}, u32[]{:S(2)}, u32[]{:S(2)}) %collective-permute-start.11) | collective-permute-done | bytes 55328 | tf_op jit(solution)/shard_map/ppermute | solution.py:34
  35.3 0.0 collective-permute-done.12.refs_3_
  35.3 0.7 %stack_slabs.1 = f32[4,8,1728]{2,1,0:T(8,128)} custom-call(f32[8,1728]{1,0:T(8,128)S(1)} %weave_channels.1.refs_0_, f32[8,1728]{1,0:T(8,128)S(1)} %collective-permute-done.10.refs_1_, f32[8,1728]{1,0:T(8,128)S(1)} %collective-permute-done.11.refs_2_, f32[8,1728]{1,0:T(8,128)S(1)} %collective-permute-done.12.refs_3_), custom_call_target="tpu_custom_call" | custom-call | tf_op jit(solution)/shard_map/stack_slabs/pallas_call | solution.py:294
  (2 shorter events, 0.0 us)
Async XLA Ops:
  0.6 5.7 %collective-permute-start = (f32[16,2,16,256]{3,2,1,0:T(8,128)}, f32[16,2,16,256]{3,2,1,0:T(8,128)S(1)}, u32[]{:S(2)}, u32[]{:S(2)}) collective-permute-start(f32[16,2,16,256]{3,2,1,0:T(8,128)} %param.3), channel_id=1, source_target_pairs={{0,1},{1,0},{2,3},{3,2},{4,5},{5,4},{6,7},{7,6},{8,9},{9,8},{10,11... | collective-permute-start | bytes 1572872 | tf_op jit(solution)/shard_map/ppermute | solution.py:25
  1.1 7.5 %collective-permute-start.4 = (f32[32,1,8,128]{3,2,1,0:T(8,128)}, f32[32,1,8,128]{3,2,1,0:T(8,128)S(1)}, u32[]{:S(2)}, u32[]{:S(2)}) collective-permute-start(f32[32,1,8,128]{3,2,1,0:T(8,128)} %param.4), channel_id=1, source_target_pairs={{0,2},{1,3},{2,0},{3,1},{4,6},{5,7},{6,4},{7,5},{8,10},{9,11},{10,... | collective-permute-start | bytes 393224 | tf_op jit(solution)/shard_map/ppermute | solution.py:25
  3.7 8.4 %collective-permute-start.2 = (f32[32,1,8,128]{3,2,1,0:T(8,128)}, f32[32,1,8,128]{3,2,1,0:T(8,128)S(1)}, u32[]{:S(2)}, u32[]{:S(2)}) collective-permute-start(f32[32,1,8,128]{3,2,1,0:T(8,128)} %param.4), channel_id=1, source_target_pairs={{4,0},{5,1},{6,2},{7,3},{8,4},{9,5},{10,6},{11,7},{12,8},{13,9},{1... | collective-permute-start | bytes 393224 | tf_op jit(solution)/shard_map/ppermute | solution.py:396
  5.0 9.1 %collective-permute-start.3 = (f32[32,1,8,128]{3,2,1,0:T(8,128)}, f32[32,1,8,128]{3,2,1,0:T(8,128)S(1)}, u32[]{:S(2)}, u32[]{:S(2)}) collective-permute-start(f32[32,1,8,128]{3,2,1,0:T(8,128)} %param.4), channel_id=1, source_target_pairs={{6,0},{7,1},{4,2},{5,3},{10,4},{11,5},{8,6},{9,7},{14,8},{15,9},{1... | collective-permute-start | bytes 393224 | tf_op jit(solution)/shard_map/ppermute | solution.py:396
  8.6 11.2 %collective-permute-start.1 = (f32[32,864]{1,0:T(8,128)S(1)}, f32[32,864]{1,0:T(8,128)S(1)}, u32[]{:S(2)}, u32[]{:S(2)}) collective-permute-start(f32[32,864]{1,0:T(8,128)S(1)} %get-tuple-element.29), channel_id=1, source_target_pairs={{0,2},{1,3},{2,0},{3,1},{4,6},{5,7},{6,4},{7,5},{8,10},{9,11},{10,... | collective-permute-start | bytes 331784 | tf_op jit(solution)/shard_map/ppermute | solution.py:25
  14.7 7.2 %collective-permute-start.5 = (f32[16,864]{1,0:T(8,128)S(1)}, f32[16,864]{1,0:T(8,128)S(1)}, u32[]{:S(2)}, u32[]{:S(2)}) collective-permute-start(f32[16,864]{1,0:T(8,128)S(1)} %get-tuple-element.37), channel_id=1, source_target_pairs={{0,4},{4,8},{8,12},{12,0},{1,5},{5,9},{9,13},{13,1},{2,6},{6,10},{... | collective-permute-start | bytes 165896 | tf_op jit(solution)/shard_map/ppermute | solution.py:34
  16.7 5.2 %collective-permute-start.6 = (f32[16,864]{1,0:T(8,128)S(1)}, f32[16,864]{1,0:T(8,128)S(1)}, u32[]{:S(2)}, u32[]{:S(2)}) collective-permute-start(f32[16,864]{1,0:T(8,128)S(1)} %get-tuple-element.38), channel_id=1, source_target_pairs={{0,12},{4,0},{8,4},{12,8},{1,13},{5,1},{9,5},{13,9},{2,14},{6,2},{... | collective-permute-start | bytes 165896 | tf_op jit(solution)/shard_map/ppermute | solution.py:34
  18.6 5.3 %collective-permute-start.7 = (f32[16,864]{1,0:T(8,128)S(1)}, f32[16,864]{1,0:T(8,128)S(1)}, u32[]{:S(2)}, u32[]{:S(2)}) collective-permute-start(f32[16,864]{1,0:T(8,128)S(1)} %get-tuple-element.39), channel_id=1, source_target_pairs={{0,8},{4,12},{8,0},{12,4},{1,9},{5,13},{9,1},{13,5},{2,10},{6,14},... | collective-permute-start | bytes 165896 | tf_op jit(solution)/shard_map/ppermute | solution.py:34
  23.8 8.2 %collective-permute-start.8 = (f32[512,256]{1,0:T(8,128)S(1)}, f32[512,256]{1,0:T(8,128)S(1)}, u32[]{:S(2)}, u32[]{:S(2)}) collective-permute-start(f32[512,256]{1,0:T(8,128)S(1)} %get-tuple-element.41), channel_id=1, source_target_pairs={{0,1},{1,0},{2,3},{3,2},{4,5},{5,4},{6,7},{7,6},{8,9},{9,8},{10,11... | collective-permute-start | bytes 1572872 | tf_op jit(solution)/shard_map/ppermute | solution.py:25
  23.9 3.9 %collective-permute-start.9 = (f32[8,864]{1,0:T(8,128)S(1)}, f32[8,864]{1,0:T(8,128)S(1)}, u32[]{:S(2)}, u32[]{:S(2)}) collective-permute-start(f32[8,864]{1,0:T(8,128)S(1)} %get-tuple-element.48), channel_id=1, source_target_pairs={{0,2},{1,3},{2,0},{3,1},{4,6},{5,7},{6,4},{7,5},{8,10},{9,11},{10,... | collective-permute-start | bytes 82952 | tf_op jit(solution)/shard_map/ppermute | solution.py:25
  28.1 6.2 %collective-permute-start.10 = (f32[8,1728]{1,0:T(8,128)S(1)}, f32[8,1728]{1,0:T(8,128)S(1)}, u32[]{:S(2)}, u32[]{:S(2)}) collective-permute-start(f32[8,1728]{1,0:T(8,128)S(1)} %weave_channels.1.refs_0_), channel_id=1, source_target_pairs={{0,4},{4,8},{8,12},{12,0},{1,5},{5,9},{9,13},{13,1},{2,6},{6,10},{... | collective-permute-start | bytes 165896 | tf_op jit(solution)/shard_map/ppermute | solution.py:34
  28.1 7.2 %collective-permute-start.11 = (f32[8,1728]{1,0:T(8,128)S(1)}, f32[8,1728]{1,0:T(8,128)S(1)}, u32[]{:S(2)}, u32[]{:S(2)}) collective-permute-start(f32[8,1728]{1,0:T(8,128)S(1)} %weave_channels.1.refs_0_), channel_id=1, source_target_pairs={{0,8},{4,12},{8,0},{12,4},{1,9},{5,13},{9,1},{13,5},{2,10},{6,14},... | collective-permute-start | bytes 165896 | tf_op jit(solution)/shard_map/ppermute | solution.py:34
  30.8 4.5 %collective-permute-start.12 = (f32[8,1728]{1,0:T(8,128)S(1)}, f32[8,1728]{1,0:T(8,128)S(1)}, u32[]{:S(2)}, u32[]{:S(2)}) collective-permute-start(f32[8,1728]{1,0:T(8,128)S(1)} %weave_channels.1.refs_0_), channel_id=1, source_target_pairs={{0,12},{4,0},{8,4},{12,8},{1,13},{5,1},{9,5},{13,9},{2,14},{6,2},{... | collective-permute-start | bytes 165896 | tf_op jit(solution)/shard_map/ppermute | solution.py:34

commit v5 on v4

--- a/solution.py
+++ b/solution.py
@@ -29,9 +29,20 @@
     return pltpu.with_memory_space_constraint(value, pltpu.HBM)
 
 
-def turned_by(value, axis, steps):
-    count = lax.axis_size(axis)
-    return lax.ppermute(value, axis, [(source, (source + steps) % count) for source in range(count)])
+def routes(count, ring, steps):
+    place = {slab: at for at, slab in enumerate(ring)}
+    return [ring[(place[slab] + steps) % count] for slab in range(count)]
+
+
+def routed(value, axis, route):
+    return lax.ppermute(value, axis, list(enumerate(route)))
+
+
+def entry(table, index):
+    value = table[0]
+    for at in range(1, len(table)):
+        value = jnp.where(index == at, table[at], value)
+    return value
 
 
 def halves(value):
@@ -180,7 +191,8 @@
     )(high, low, *own, across.reshape(-1, out_cols))
 
 
-def weight_partial(high, low, terms, above, parts):
+def weight_partial(high, low, terms, above, routes_out):
+    parts = len(routes_out) + 1
     filters, _, out_rows, out_cols = above[0].shape
     cells = out_rows * out_cols
     third = high.shape[0] // 2
@@ -198,8 +210,9 @@
         total[:, third:] = terms_ref[...]
         slab = lax.axis_index("gz")
         for k in range(parts):
+            target = slab if k == 0 else entry(routes_out[k - 1], slab)
             for j in range(chips):
-                first = pl.multiple_of(j * filters + lax.rem(slab + k, parts) * block, 8)
+                first = pl.multiple_of(j * filters + target * block, 8)
                 out_refs[k][j * block : (j + 1) * block, :] = total[pl.ds(first, block), :]
 
     return pl.pallas_call(
@@ -282,14 +295,15 @@
     )(place, *pieces)
 
 
-def stack_slabs(pieces):
+def stack_slabs(pieces, back_routes):
     block, width = pieces[0].shape
     parts = len(pieces)
 
     def kernel(*refs):
         slab = lax.axis_index("gz")
         for k in range(parts):
-            refs[parts][lax.rem(slab + parts - k, parts)] = refs[k][...]
+            source = slab if k == 0 else entry([back_routes[k - 1].index(at) for at in range(parts)], slab)
+            refs[parts][source] = refs[k][...]
 
     return pl.pallas_call(
         kernel,
@@ -400,23 +414,24 @@
     channels, planes, rows, cols = volume.shape
     filters, out_depth, out_rows, out_cols = out_grad.shape
     parts, cores = lax.axis_size("gz"), 2
+    out_routes = [routes(parts, [place ^ (place >> 1) for place in range(parts)], k) for k in range(1, parts)]
+    back_routes = [routes(parts, range(parts), k) for k in range(1, parts)]
     factor = 1.0 / math.sqrt(out_depth * parts * out_rows * out_cols)
     across = swapped(out_grad, "af", cores)
     above = [below(out_grad, 0), below(out_grad, cores)]
     high, low, *own, mine, theirs = prepare([volume, swapped(volume, "af", 1)], out_grad, weight)
     weights = [mine, swapped(theirs, "af", cores)]
     terms = weight_terms(high, low, own, across)
-    sent = weight_partial(high, low, terms, above, parts)
-    arrived = [sent[0]] + [turned_by(sent[k], "gz", k) for k in (1, 3, 2)]
+    sent = weight_partial(high, low, terms, above, out_routes)
+    arrived = [sent[0]] + [routed(piece, "gz", route) for piece, route in zip(sent[1:], out_routes)]
     *inputs, place = input_partial(weights, own, [*above, across], volume.shape, cores)
     inputs, arrived = lax.optimization_barrier((inputs, arrived))
     input_grad = (inputs[0] + swapped(inputs[1], "af", 1)).reshape(volume.shape)
     sums = add_slabs(arrived, 2)
     woven = weave_channels([sums[0], swapped(sums[1], "af", cores)], place, channels, cores, factor)
-    gathered = {k: turned_by(woven, "gz", k) for k in (1, 2, 3)}
-    pieces = [woven] + [gathered[k] for k in range(1, parts)]
+    pieces = [woven] + [routed(woven, "gz", route) for route in back_routes]
     input_grad, pieces = lax.optimization_barrier((input_grad, pieces))
-    weight_grad = stack_slabs(pieces)
+    weight_grad = stack_slabs(pieces, back_routes)
     return (input_grad, weight_grad)
 
 

time: 36.2 us -> 35.7 us (0.986)
  waiting for transfers between devices: 11.3 us -> 10.8 us
    ppermute x6, waiting for transfers between devices: 4.27 us -> 3.67 us  [routed(): return lax.ppermute(value, axis, list(enumerate(route)))]
  transfers between devices with their start and end apart: 13 -> 13, of which waited for: 6 -> 7; matrix products, arithmetic and copies ran while one was open for 2% -> 2% of each run, Pallas kernels for 17% -> 17%
where the time goes in v5:
time: 35.7 us; the launch traced here: 35.5 us
  starting transfers between devices  16.3 us (46%)
  waiting for transfers between devices  10.8 us (30%)
  Pallas kernels  6.86 us (19%)
  other arithmetic  0.86 us (2%)
  between operations  0.7 us (2%)
    ppermute x6, starting transfers between devices, routed(): return lax.ppermute(value, axis, list(enumerate(route)))  9.16 us
    ppermute x2, waiting for transfers between devices, below(): return lax.ppermute(value, ('gz', 'af'), pairs)  4.58 us
    ppermute x5, starting transfers between devices, swapped(): lax.ppermute(value, axis, [(source, source ^ bits) for source in range(co...  4.53 us
    ppermute x6, waiting for transfers between devices, routed(): return lax.ppermute(value, axis, list(enumerate(route)))  3.67 us
    ppermute x5, waiting for transfers between devices, swapped(): lax.ppermute(value, axis, [(source, source ^ bits) for source in range(co...  2.59 us
    ppermute x2, starting transfers between devices, below(): return lax.ppermute(value, ('gz', 'af'), pairs)  2.57 us
    pallas_call x1, Pallas kernels, prepare(): pl.pallas_call(kernel, in_specs=[HBM, HBM, HBM] + [VMEM] * (cores - 1), o...  2.24 us
    pallas_call x1, Pallas kernels, input_partial(): pl.pallas_call(kernel, out_shape=[jax.ShapeDtypeStruct((channels * planes...  2.17 us
  transfers between devices with their start and end apart: 13, of which 7 were waited for; matrix products, arithmetic and copies ran while one was open for 2% of the time, Pallas kernels for 17%

profile of v5, /device:TPU:0, one launch (start us, length us, event | category | flops | bytes accessed | tf_op | source)
XLA Modules:
  0.0 35.5 jit_solution(3656705212648390710)
XLA Ops:
  0.6 0.5 %collective-permute-start = (f32[16,2,16,256]{3,2,1,0:T(8,128)}, f32[16,2,16,256]{3,2,1,0:T(8,128)S(1)}, u32[]{:S(2)}, u32[]{:S(2)}) collective-permute-start(f32[16,2,16,256]{3,2,1,0:T(8,128)} %param.3), channel_id=1, source_target_pairs={{0,1},{1,0},{2,3},{3,2},{4,5},{5,4},{6,7},{7,6},{8,9},{9,8},{10,11... | collective-permute-start | bytes 1572872 | tf_op jit(solution)/shard_map/ppermute | solution.py:25
  1.1 2.6 %collective-permute-start.4 = (f32[32,1,8,128]{3,2,1,0:T(8,128)}, f32[32,1,8,128]{3,2,1,0:T(8,128)S(1)}, u32[]{:S(2)}, u32[]{:S(2)}) collective-permute-start(f32[32,1,8,128]{3,2,1,0:T(8,128)} %param.4), channel_id=1, source_target_pairs={{0,2},{1,3},{2,0},{3,1},{4,6},{5,7},{6,4},{7,5},{8,10},{9,11},{10,... | collective-permute-start | bytes 393224 | tf_op jit(solution)/shard_map/ppermute | solution.py:25
  3.7 1.3 %collective-permute-start.2 = (f32[32,1,8,128]{3,2,1,0:T(8,128)}, f32[32,1,8,128]{3,2,1,0:T(8,128)S(1)}, u32[]{:S(2)}, u32[]{:S(2)}) collective-permute-start(f32[32,1,8,128]{3,2,1,0:T(8,128)} %param.4), channel_id=1, source_target_pairs={{4,0},{5,1},{6,2},{7,3},{8,4},{9,5},{10,6},{11,7},{12,8},{13,9},{1... | collective-permute-start | bytes 393224 | tf_op jit(solution)/shard_map/ppermute | solution.py:410
  5.0 1.3 %collective-permute-start.3 = (f32[32,1,8,128]{3,2,1,0:T(8,128)}, f32[32,1,8,128]{3,2,1,0:T(8,128)S(1)}, u32[]{:S(2)}, u32[]{:S(2)}) collective-permute-start(f32[32,1,8,128]{3,2,1,0:T(8,128)} %param.4), channel_id=1, source_target_pairs={{6,0},{7,1},{4,2},{5,3},{10,4},{11,5},{8,6},{9,7},{14,8},{15,9},{1... | collective-permute-start | bytes 393224 | tf_op jit(solution)/shard_map/ppermute | solution.py:410
  6.3 0.0 collective-permute-done
  6.3 2.2 %prepare.1 = (bf16[576,1024]{1,0:T(8,128)(2,1)S(1)}, bf16[576,1024]{1,0:T(8,128)(2,1)S(1)}, bf16[32,1024]{1,0:T(8,128)(2,1)S(1)}, bf16[32,1024]{1,0:T(8,128)(2,1...) custom-call(f32[512,256]{1,0:T(8,128)} %bitcast.16, f32[256,128]{1,0:T(8,128)} %bitcast.18, f32[32,1728]{1,0:T(8,128)} %w_hbm.1, ...), custom_call_target="tpu_custom_call" | custom-call | tf_op jit(solution)/shard_map/prepare/pallas_call | solution.py:154
  8.6 0.1 collective-permute-start.1
  8.7 0.0 collective-permute-done.4
  8.7 0.9 %weight_terms.1.terms_ref = f32[64,576]{1,0:T(8,128)S(1)} custom-call(bf16[576,1024]{1,0:T(8,128)(2,1)S(1)} %get-tuple-element.34.high_ref, bf16[576,1024]{1,0:T(8,128)(2,1)S(1)} %get-tuple-element.35.low_ref, bf16[32,1024]{1,0:T(8,128)(2,1)S(1)} %get-tuple-element.30.refs_2_.own_high, bf16[32,1024]{1,0:T(8,128)(2,1)S(1)} %get-tuple-element.31.refs_3_.own_low, ...), custom_call_target="tpu_custom_call" | custom-call | tf_op jit(solution)/shard_map/weight_terms/pallas_call | solution.py:185
  9.5 2.6 %collective-permute-done.2 = f32[32,1,8,128]{3,2,1,0:T(8,128)S(1)} collective-permute-done((f32[32,1,8,128]{3,2,1,0:T(8,128)}, f32[32,1,8,128]{3,2,1,0:T(8,128)S(1)}, u32[]{:S(2)}, u32[]{:S(2)}) %collective-permute-start.2) | collective-permute-done | bytes 131104 | tf_op jit(solution)/shard_map/ppermute | solution.py:410
  12.1 2.0 %collective-permute-done.3 = f32[32,1,8,128]{3,2,1,0:T(8,128)S(1)} collective-permute-done((f32[32,1,8,128]{3,2,1,0:T(8,128)}, f32[32,1,8,128]{3,2,1,0:T(8,128)S(1)}, u32[]{:S(2)}, u32[]{:S(2)}) %collective-permute-start.3) | collective-permute-done | bytes 131104 | tf_op jit(solution)/shard_map/ppermute | solution.py:410
  14.1 0.6 %weight_partial.1 = (f32[16,864]{1,0:T(8,128)S(1)}, f32[16,864]{1,0:T(8,128)S(1)}, f32[16,864]{1,0:T(8,128)S(1)}, f32[16,864]{1,0:T(8,128)S(1)}) custom-call(bf16[576,1024]{1,0:T(8,128)(2,1)S(1)} %get-tuple-element.34.high_ref, bf16[576,1024]{1,0:T(8,128)(2,1)S(1)} %get-tuple-element.35.low_ref, f32[64,576]{1,0:T(8,128)S(1)} %weight_terms.1.terms_ref, ...), custom_call_target="tpu_custom_call" | custom-call | tf_op jit(solution)/shard_map/weight_partial/pallas_call | solution.py:218
  14.7 2.0 %collective-permute-start.5 = (f32[16,864]{1,0:T(8,128)S(1)}, f32[16,864]{1,0:T(8,128)S(1)}, u32[]{:S(2)}, u32[]{:S(2)}) collective-permute-start(f32[16,864]{1,0:T(8,128)S(1)} %get-tuple-element.37), channel_id=1, source_target_pairs={{0,4},{4,12},{8,0},{12,8},{1,5},{5,13},{9,1},{13,9},{2,6},{6,14},{... | collective-permute-start | bytes 165896 | tf_op jit(solution)/shard_map/ppermute | solution.py:38
  16.7 2.5 %collective-permute-start.6 = (f32[16,864]{1,0:T(8,128)S(1)}, f32[16,864]{1,0:T(8,128)S(1)}, u32[]{:S(2)}, u32[]{:S(2)}) collective-permute-start(f32[16,864]{1,0:T(8,128)S(1)} %get-tuple-element.38), channel_id=1, source_target_pairs={{0,12},{4,8},{8,4},{12,0},{1,13},{5,9},{9,5},{13,1},{2,14},{6,10},... | collective-permute-start | bytes 165896 | tf_op jit(solution)/shard_map/ppermute | solution.py:38
  19.2 0.2 collective-permute-start.7
  19.4 0.0 collective-permute-done.1.refs_1_
  19.4 2.2 %input_partial.1 = (f32[512,256]{1,0:T(8,128)S(1)}, f32[512,256]{1,0:T(8,128)S(1)}, bf16[256,256]{1,0:T(8,128)(2,1)S(1)}) custom-call(f32[32,864]{1,0:T(8,128)S(1)} %get-tuple-element.28.refs_0_, f32[32,864]{1,0:T(8,128)S(1)} %collective-permute-done.1.refs_1_, bf16[32,1024]{1,0:T(8,128)(2,1)S(1)} %get-tuple-element.30.refs_2_.own_high, ...), custom_call_target="tpu_custom_call" | custom-call | tf_op jit(solution)/shard_map/input_partial/pallas_call | solution.py:387
  21.6 0.0 collective-permute-done.5.refs_1_
  21.6 1.1 %collective-permute-done.6.refs_2_ = f32[16,864]{1,0:T(8,128)S(1)} collective-permute-done((f32[16,864]{1,0:T(8,128)S(1)}, f32[16,864]{1,0:T(8,128)S(1)}, u32[]{:S(2)}, u32[]{:S(2)}) %collective-permute-start.6) | collective-permute-done | bytes 55328 | tf_op jit(solution)/shard_map/ppermute | solution.py:38
  22.7 0.7 %collective-permute-done.7.refs_3_ = f32[16,864]{1,0:T(8,128)S(1)} collective-permute-done((f32[16,864]{1,0:T(8,128)S(1)}, f32[16,864]{1,0:T(8,128)S(1)}, u32[]{:S(2)}, u32[]{:S(2)}) %collective-permute-start.7) | collective-permute-done | bytes 55328 | tf_op jit(solution)/shard_map/ppermute | solution.py:38
  23.4 1.4 %collective-permute-start.9 = (f32[8,864]{1,0:T(8,128)S(1)}, f32[8,864]{1,0:T(8,128)S(1)}, u32[]{:S(2)}, u32[]{:S(2)}) collective-permute-start(f32[8,864]{1,0:T(8,128)S(1)} %get-tuple-element.48), channel_id=1, source_target_pairs={{0,2},{1,3},{2,0},{3,1},{4,6},{5,7},{6,4},{7,5},{8,10},{9,11},{10,... | collective-permute-start | bytes 82952 | tf_op jit(solution)/shard_map/ppermute | solution.py:25
  24.7 2.6 %collective-permute-done.9.refs_1_ = f32[8,864]{1,0:T(8,128)S(1)} collective-permute-done((f32[8,864]{1,0:T(8,128)S(1)}, f32[8,864]{1,0:T(8,128)S(1)}, u32[]{:S(2)}, u32[]{:S(2)}) %collective-permute-start.9) | collective-permute-done | bytes 27680 | tf_op jit(solution)/shard_map/ppermute | solution.py:25
  27.3 0.3 weave_channels.1.refs_0_
  27.6 0.6 %collective-permute-start.10 = (f32[8,1728]{1,0:T(8,128)S(1)}, f32[8,1728]{1,0:T(8,128)S(1)}, u32[]{:S(2)}, u32[]{:S(2)}) collective-permute-start(f32[8,1728]{1,0:T(8,128)S(1)} %weave_channels.1.refs_0_), channel_id=1, source_target_pairs={{0,4},{4,8},{8,12},{12,0},{1,5},{5,9},{9,13},{13,1},{2,6},{6,10},{... | collective-permute-start | bytes 165896 | tf_op jit(solution)/shard_map/ppermute | solution.py:38
  28.1 2.0 %collective-permute-start.11 = (f32[8,1728]{1,0:T(8,128)S(1)}, f32[8,1728]{1,0:T(8,128)S(1)}, u32[]{:S(2)}, u32[]{:S(2)}) collective-permute-start(f32[8,1728]{1,0:T(8,128)S(1)} %weave_channels.1.refs_0_), channel_id=1, source_target_pairs={{0,8},{4,12},{8,0},{12,4},{1,9},{5,13},{9,1},{13,5},{2,10},{6,14},... | collective-permute-start | bytes 165896 | tf_op jit(solution)/shard_map/ppermute | solution.py:38
  30.1 1.9 %collective-permute-start.12 = (f32[8,1728]{1,0:T(8,128)S(1)}, f32[8,1728]{1,0:T(8,128)S(1)}, u32[]{:S(2)}, u32[]{:S(2)}) collective-permute-start(f32[8,1728]{1,0:T(8,128)S(1)} %weave_channels.1.refs_0_), channel_id=1, source_target_pairs={{0,12},{4,0},{8,4},{12,8},{1,13},{5,1},{9,5},{13,9},{2,14},{6,2},{... | collective-permute-start | bytes 165896 | tf_op jit(solution)/shard_map/ppermute | solution.py:38
  32.0 0.0 collective-permute-done.8
  32.0 0.9 %add.3 = f32[512,256]{1,0:T(8,128)} add(f32[512,256]{1,0:T(8,128)S(1)} %get-tuple-element.40, f32[512,256]{1,0:T(8,128)S(1)} %collective-permute-done.8) | non-fusion elementwise | flops 131072 | bytes 1572864 | tf_op jit(solution)/shard_map/add | solution.py:429
  32.9 1.0 %collective-permute-done.10.refs_1_ = f32[8,1728]{1,0:T(8,128)S(1)} collective-permute-done((f32[8,1728]{1,0:T(8,128)S(1)}, f32[8,1728]{1,0:T(8,128)S(1)}, u32[]{:S(2)}, u32[]{:S(2)}) %collective-permute-start.10) | collective-permute-done | bytes 55328 | tf_op jit(solution)/shard_map/ppermute | solution.py:38
  33.9 0.9 %collective-permute-done.11.refs_2_ = f32[8,1728]{1,0:T(8,128)S(1)} collective-permute-done((f32[8,1728]{1,0:T(8,128)S(1)}, f32[8,1728]{1,0:T(8,128)S(1)}, u32[]{:S(2)}, u32[]{:S(2)}) %collective-permute-start.11) | collective-permute-done | bytes 55328 | tf_op jit(solution)/shard_map/ppermute | solution.py:38
  34.8 0.0 collective-permute-done.12.refs_3_
  34.8 0.7 %stack_slabs.1 = f32[4,8,1728]{2,1,0:T(8,128)} custom-call(f32[8,1728]{1,0:T(8,128)S(1)} %weave_channels.1.refs_0_, f32[8,1728]{1,0:T(8,128)S(1)} %collective-permute-done.10.refs_1_, f32[8,1728]{1,0:T(8,128)S(1)} %collective-permute-done.11.refs_2_, f32[8,1728]{1,0:T(8,128)S(1)} %collective-permute-done.12.refs_3_), custom_call_target="tpu_custom_call" | custom-call | tf_op jit(solution)/shard_map/stack_slabs/pallas_call | solution.py:308
  (2 shorter events, 0.0 us)
Async XLA Ops:
  0.6 5.7 %collective-permute-start = (f32[16,2,16,256]{3,2,1,0:T(8,128)}, f32[16,2,16,256]{3,2,1,0:T(8,128)S(1)}, u32[]{:S(2)}, u32[]{:S(2)}) collective-permute-start(f32[16,2,16,256]{3,2,1,0:T(8,128)} %param.3), channel_id=1, source_target_pairs={{0,1},{1,0},{2,3},{3,2},{4,5},{5,4},{6,7},{7,6},{8,9},{9,8},{10,11... | collective-permute-start | bytes 1572872 | tf_op jit(solution)/shard_map/ppermute | solution.py:25
  1.1 7.5 %collective-permute-start.4 = (f32[32,1,8,128]{3,2,1,0:T(8,128)}, f32[32,1,8,128]{3,2,1,0:T(8,128)S(1)}, u32[]{:S(2)}, u32[]{:S(2)}) collective-permute-start(f32[32,1,8,128]{3,2,1,0:T(8,128)} %param.4), channel_id=1, source_target_pairs={{0,2},{1,3},{2,0},{3,1},{4,6},{5,7},{6,4},{7,5},{8,10},{9,11},{10,... | collective-permute-start | bytes 393224 | tf_op jit(solution)/shard_map/ppermute | solution.py:25
  3.7 8.4 %collective-permute-start.2 = (f32[32,1,8,128]{3,2,1,0:T(8,128)}, f32[32,1,8,128]{3,2,1,0:T(8,128)S(1)}, u32[]{:S(2)}, u32[]{:S(2)}) collective-permute-start(f32[32,1,8,128]{3,2,1,0:T(8,128)} %param.4), channel_id=1, source_target_pairs={{4,0},{5,1},{6,2},{7,3},{8,4},{9,5},{10,6},{11,7},{12,8},{13,9},{1... | collective-permute-start | bytes 393224 | tf_op jit(solution)/shard_map/ppermute | solution.py:410
  5.0 9.1 %collective-permute-start.3 = (f32[32,1,8,128]{3,2,1,0:T(8,128)}, f32[32,1,8,128]{3,2,1,0:T(8,128)S(1)}, u32[]{:S(2)}, u32[]{:S(2)}) collective-permute-start(f32[32,1,8,128]{3,2,1,0:T(8,128)} %param.4), channel_id=1, source_target_pairs={{6,0},{7,1},{4,2},{5,3},{10,4},{11,5},{8,6},{9,7},{14,8},{15,9},{1... | collective-permute-start | bytes 393224 | tf_op jit(solution)/shard_map/ppermute | solution.py:410
  8.6 10.8 %collective-permute-start.1 = (f32[32,864]{1,0:T(8,128)S(1)}, f32[32,864]{1,0:T(8,128)S(1)}, u32[]{:S(2)}, u32[]{:S(2)}) collective-permute-start(f32[32,864]{1,0:T(8,128)S(1)} %get-tuple-element.29), channel_id=1, source_target_pairs={{0,2},{1,3},{2,0},{3,1},{4,6},{5,7},{6,4},{7,5},{8,10},{9,11},{10,... | collective-permute-start | bytes 331784 | tf_op jit(solution)/shard_map/ppermute | solution.py:25
  14.7 6.9 %collective-permute-start.5 = (f32[16,864]{1,0:T(8,128)S(1)}, f32[16,864]{1,0:T(8,128)S(1)}, u32[]{:S(2)}, u32[]{:S(2)}) collective-permute-start(f32[16,864]{1,0:T(8,128)S(1)} %get-tuple-element.37), channel_id=1, source_target_pairs={{0,4},{4,12},{8,0},{12,8},{1,5},{5,13},{9,1},{13,9},{2,6},{6,14},{... | collective-permute-start | bytes 165896 | tf_op jit(solution)/shard_map/ppermute | solution.py:38
  16.7 6.0 %collective-permute-start.6 = (f32[16,864]{1,0:T(8,128)S(1)}, f32[16,864]{1,0:T(8,128)S(1)}, u32[]{:S(2)}, u32[]{:S(2)}) collective-permute-start(f32[16,864]{1,0:T(8,128)S(1)} %get-tuple-element.38), channel_id=1, source_target_pairs={{0,12},{4,8},{8,4},{12,0},{1,13},{5,9},{9,5},{13,1},{2,14},{6,10},... | collective-permute-start | bytes 165896 | tf_op jit(solution)/shard_map/ppermute | solution.py:38
  19.2 4.2 %collective-permute-start.7 = (f32[16,864]{1,0:T(8,128)S(1)}, f32[16,864]{1,0:T(8,128)S(1)}, u32[]{:S(2)}, u32[]{:S(2)}) collective-permute-start(f32[16,864]{1,0:T(8,128)S(1)} %get-tuple-element.39), channel_id=1, source_target_pairs={{0,8},{4,0},{8,12},{12,4},{1,9},{5,1},{9,13},{13,5},{2,10},{6,2},{... | collective-permute-start | bytes 165896 | tf_op jit(solution)/shard_map/ppermute | solution.py:38
  23.3 8.7 %collective-permute-start.8 = (f32[512,256]{1,0:T(8,128)S(1)}, f32[512,256]{1,0:T(8,128)S(1)}, u32[]{:S(2)}, u32[]{:S(2)}) collective-permute-start(f32[512,256]{1,0:T(8,128)S(1)} %get-tuple-element.41), channel_id=1, source_target_pairs={{0,1},{1,0},{2,3},{3,2},{4,5},{5,4},{6,7},{7,6},{8,9},{9,8},{10,11... | collective-permute-start | bytes 1572872 | tf_op jit(solution)/shard_map/ppermute | solution.py:25
  23.4 3.9 %collective-permute-start.9 = (f32[8,864]{1,0:T(8,128)S(1)}, f32[8,864]{1,0:T(8,128)S(1)}, u32[]{:S(2)}, u32[]{:S(2)}) collective-permute-start(f32[8,864]{1,0:T(8,128)S(1)} %get-tuple-element.48), channel_id=1, source_target_pairs={{0,2},{1,3},{2,0},{3,1},{4,6},{5,7},{6,4},{7,5},{8,10},{9,11},{10,... | collective-permute-start | bytes 82952 | tf_op jit(solution)/shard_map/ppermute | solution.py:25
  27.6 6.4 %collective-permute-start.10 = (f32[8,1728]{1,0:T(8,128)S(1)}, f32[8,1728]{1,0:T(8,128)S(1)}, u32[]{:S(2)}, u32[]{:S(2)}) collective-permute-start(f32[8,1728]{1,0:T(8,128)S(1)} %weave_channels.1.refs_0_), channel_id=1, source_target_pairs={{0,4},{4,8},{8,12},{12,0},{1,5},{5,9},{9,13},{13,1},{2,6},{6,10},{... | collective-permute-start | bytes 165896 | tf_op jit(solution)/shard_map/ppermute | solution.py:38
  28.1 6.7 %collective-permute-start.11 = (f32[8,1728]{1,0:T(8,128)S(1)}, f32[8,1728]{1,0:T(8,128)S(1)}, u32[]{:S(2)}, u32[]{:S(2)}) collective-permute-start(f32[8,1728]{1,0:T(8,128)S(1)} %weave_channels.1.refs_0_), channel_id=1, source_target_pairs={{0,8},{4,12},{8,0},{12,4},{1,9},{5,13},{9,1},{13,5},{2,10},{6,14},... | collective-permute-start | bytes 165896 | tf_op jit(solution)/shard_map/ppermute | solution.py:38
  30.1 4.7 %collective-permute-start.12 = (f32[8,1728]{1,0:T(8,128)S(1)}, f32[8,1728]{1,0:T(8,128)S(1)}, u32[]{:S(2)}, u32[]{:S(2)}) collective-permute-start(f32[8,1728]{1,0:T(8,128)S(1)} %weave_channels.1.refs_0_), channel_id=1, source_target_pairs={{0,12},{4,0},{8,4},{12,8},{1,13},{5,1},{9,5},{13,9},{2,14},{6,2},{... | collective-permute-start | bytes 165896 | tf_op jit(solution)/shard_map/ppermute | solution.py:38

commit v6 on v5

--- a/solution.py
+++ b/solution.py
@@ -11,6 +11,7 @@
 BF16 = jnp.bfloat16
 VMEM = pl.BlockSpec(memory_space=pltpu.VMEM)
 HBM = pl.BlockSpec(memory_space=pltpu.HBM)
+COVER = 8000000000
 PARAMS = pltpu.CompilerParams(vmem_limit_bytes=48 * 1024 * 1024)
 
 
@@ -227,11 +228,11 @@
     )(high, low, terms, *[g.reshape(-1, out_cols) for g in above])
 
 
-def add_slabs(pieces, chips):
+def add_slabs(pieces, chips, after):
     rows, width = pieces[0].shape
     block = rows // chips
 
-    def kernel(*refs):
+    def kernel(after_ref, *refs):
         for j in range(chips):
             value = refs[0][j * block : (j + 1) * block, :]
             for piece in refs[1 : len(pieces)]:
@@ -240,10 +241,11 @@
 
     return pl.pallas_call(
         kernel,
+        in_specs=[pl.BlockSpec(memory_space=pl.ANY)] + [VMEM] * len(pieces),
         out_shape=[jax.ShapeDtypeStruct((block, width), F32)] * chips,
         compiler_params=PARAMS,
         name="add_slabs",
-    )(*pieces)
+    )(after, *pieces)
 
 
 def channel_places(me, chips, cores, channels):
@@ -290,6 +292,7 @@
     return pl.pallas_call(
         kernel,
         out_shape=jax.ShapeDtypeStruct((block, 27 * total), F32),
+        cost_estimate=pl.CostEstimate(flops=COVER, bytes_accessed=8000000, transcendentals=0),
         compiler_params=PARAMS,
         name="weave_channels",
     )(place, *pieces)
@@ -397,6 +400,7 @@
             pltpu.VMEM((planes * rows * channels, 6 * out_cols), BF16),
             pltpu.VMEM((planes * rows * channels, 128), F32),
         ],
+        cost_estimate=pl.CostEstimate(flops=COVER, bytes_accessed=8000000, transcendentals=0),
         compiler_params=PARAMS,
         name="input_partial",
     )(*weights, *own, *[g.reshape(-1, out_cols) for g in grads])
@@ -425,9 +429,8 @@
     sent = weight_partial(high, low, terms, above, out_routes)
     arrived = [sent[0]] + [routed(piece, "gz", route) for piece, route in zip(sent[1:], out_routes)]
     *inputs, place = input_partial(weights, own, [*above, across], volume.shape, cores)
-    inputs, arrived = lax.optimization_barrier((inputs, arrived))
     input_grad = (inputs[0] + swapped(inputs[1], "af", 1)).reshape(volume.shape)
-    sums = add_slabs(arrived, 2)
+    sums = add_slabs(arrived, 2, inputs[0])
     woven = weave_channels([sums[0], swapped(sums[1], "af", cores)], place, channels, cores, factor)
     pieces = [woven] + [routed(woven, "gz", route) for route in back_routes]
     input_grad, pieces = lax.optimization_barrier((input_grad, pieces))

time: 35.7 us -> 35.3 us (0.989)
    ppermute x6, waiting for transfers between devices: 3.67 us -> 3.3 us  [routed(): return lax.ppermute(value, axis, list(enumerate(route)))]
where the time goes in v6:
time: 35.3 us; the launch traced here: 35.2 us
  starting transfers between devices  16.3 us (46%)
  waiting for transfers between devices  10.5 us (30%)
  Pallas kernels  6.86 us (19%)
  other arithmetic  0.86 us (2%)
  between operations  0.7 us (2%)
    ppermute x6, starting transfers between devices, routed(): return lax.ppermute(value, axis, list(enumerate(route)))  9.16 us
    ppermute x2, waiting for transfers between devices, below(): return lax.ppermute(value, ('gz', 'af'), pairs)  4.58 us
    ppermute x5, starting transfers between devices, swapped(): lax.ppermute(value, axis, [(source, source ^ bits) for source in range(co...  4.53 us
    ppermute x6, waiting for transfers between devices, routed(): return lax.ppermute(value, axis, list(enumerate(route)))  3.3 us
    ppermute x5, waiting for transfers between devices, swapped(): lax.ppermute(value, axis, [(source, source ^ bits) for source in range(co...  2.58 us
    ppermute x2, starting transfers between devices, below(): return lax.ppermute(value, ('gz', 'af'), pairs)  2.57 us
    pallas_call x1, Pallas kernels, prepare(): pl.pallas_call(kernel, in_specs=[HBM, HBM, HBM] + [VMEM] * (cores - 1), o...  2.24 us
    pallas_call x1, Pallas kernels, input_partial(): pl.pallas_call(kernel, out_shape=[jax.ShapeDtypeStruct((channels * planes...  2.17 us
  transfers between devices with their start and end apart: 13, of which 7 were waited for; matrix products, arithmetic and copies ran while one was open for 2% of the time, Pallas kernels for 17%

profile of v6, /device:TPU:0, one launch (start us, length us, event | category | flops | bytes accessed | tf_op | source)
XLA Modules:
  0.0 35.2 jit_solution(16528931676927706899)
XLA Ops:
  0.6 0.5 %collective-permute-start = (f32[16,2,16,256]{3,2,1,0:T(8,128)}, f32[16,2,16,256]{3,2,1,0:T(8,128)S(1)}, u32[]{:S(2)}, u32[]{:S(2)}) collective-permute-start(f32[16,2,16,256]{3,2,1,0:T(8,128)} %param.3), channel_id=1, source_target_pairs={{0,1},{1,0},{2,3},{3,2},{4,5},{5,4},{6,7},{7,6},{8,9},{9,8},{10,11... | collective-permute-start | bytes 1572872 | tf_op jit(solution)/shard_map/ppermute | solution.py:26
  1.1 2.6 %collective-permute-start.4 = (f32[32,1,8,128]{3,2,1,0:T(8,128)}, f32[32,1,8,128]{3,2,1,0:T(8,128)S(1)}, u32[]{:S(2)}, u32[]{:S(2)}) collective-permute-start(f32[32,1,8,128]{3,2,1,0:T(8,128)} %param.4), channel_id=1, source_target_pairs={{0,2},{1,3},{2,0},{3,1},{4,6},{5,7},{6,4},{7,5},{8,10},{9,11},{10,... | collective-permute-start | bytes 393224 | tf_op jit(solution)/shard_map/ppermute | solution.py:26
  3.7 1.3 %collective-permute-start.2 = (f32[32,1,8,128]{3,2,1,0:T(8,128)}, f32[32,1,8,128]{3,2,1,0:T(8,128)S(1)}, u32[]{:S(2)}, u32[]{:S(2)}) collective-permute-start(f32[32,1,8,128]{3,2,1,0:T(8,128)} %param.4), channel_id=1, source_target_pairs={{4,0},{5,1},{6,2},{7,3},{8,4},{9,5},{10,6},{11,7},{12,8},{13,9},{1... | collective-permute-start | bytes 393224 | tf_op jit(solution)/shard_map/ppermute | solution.py:414
  5.0 1.3 %collective-permute-start.3 = (f32[32,1,8,128]{3,2,1,0:T(8,128)}, f32[32,1,8,128]{3,2,1,0:T(8,128)S(1)}, u32[]{:S(2)}, u32[]{:S(2)}) collective-permute-start(f32[32,1,8,128]{3,2,1,0:T(8,128)} %param.4), channel_id=1, source_target_pairs={{6,0},{7,1},{4,2},{5,3},{10,4},{11,5},{8,6},{9,7},{14,8},{15,9},{1... | collective-permute-start | bytes 393224 | tf_op jit(solution)/shard_map/ppermute | solution.py:414
  6.3 0.0 collective-permute-done
  6.3 2.2 %prepare.1 = (bf16[576,1024]{1,0:T(8,128)(2,1)S(1)}, bf16[576,1024]{1,0:T(8,128)(2,1)S(1)}, bf16[32,1024]{1,0:T(8,128)(2,1)S(1)}, bf16[32,1024]{1,0:T(8,128)(2,1...) custom-call(f32[512,256]{1,0:T(8,128)} %bitcast.16, f32[256,128]{1,0:T(8,128)} %bitcast.18, f32[32,1728]{1,0:T(8,128)} %w_hbm.1, ...), custom_call_target="tpu_custom_call" | custom-call | tf_op jit(solution)/shard_map/prepare/pallas_call | solution.py:155
  8.6 0.1 collective-permute-start.1
  8.7 0.0 collective-permute-done.4
  8.7 0.9 %weight_terms.1.terms_ref = f32[64,576]{1,0:T(8,128)S(1)} custom-call(bf16[576,1024]{1,0:T(8,128)(2,1)S(1)} %get-tuple-element.29.high_ref, bf16[576,1024]{1,0:T(8,128)(2,1)S(1)} %get-tuple-element.30.low_ref, bf16[32,1024]{1,0:T(8,128)(2,1)S(1)} %get-tuple-element.24.refs_2_.own_high, bf16[32,1024]{1,0:T(8,128)(2,1)S(1)} %get-tuple-element.25.refs_3_.own_low, ...), custom_call_target="tpu_custom_call" | custom-call | tf_op jit(solution)/shard_map/weight_terms/pallas_call | solution.py:186
  9.5 2.6 %collective-permute-done.2 = f32[32,1,8,128]{3,2,1,0:T(8,128)S(1)} collective-permute-done((f32[32,1,8,128]{3,2,1,0:T(8,128)}, f32[32,1,8,128]{3,2,1,0:T(8,128)S(1)}, u32[]{:S(2)}, u32[]{:S(2)}) %collective-permute-start.2) | collective-permute-done | bytes 131104 | tf_op jit(solution)/shard_map/ppermute | solution.py:414
  12.1 2.0 %collective-permute-done.3 = f32[32,1,8,128]{3,2,1,0:T(8,128)S(1)} collective-permute-done((f32[32,1,8,128]{3,2,1,0:T(8,128)}, f32[32,1,8,128]{3,2,1,0:T(8,128)S(1)}, u32[]{:S(2)}, u32[]{:S(2)}) %collective-permute-start.3) | collective-permute-done | bytes 131104 | tf_op jit(solution)/shard_map/ppermute | solution.py:414
  14.1 0.6 %weight_partial.1 = (f32[16,864]{1,0:T(8,128)S(1)}, f32[16,864]{1,0:T(8,128)S(1)}, f32[16,864]{1,0:T(8,128)S(1)}, f32[16,864]{1,0:T(8,128)S(1)}) custom-call(bf16[576,1024]{1,0:T(8,128)(2,1)S(1)} %get-tuple-element.29.high_ref, bf16[576,1024]{1,0:T(8,128)(2,1)S(1)} %get-tuple-element.30.low_ref, f32[64,576]{1,0:T(8,128)S(1)} %weight_terms.1.terms_ref, ...), custom_call_target="tpu_custom_call" | custom-call | tf_op jit(solution)/shard_map/weight_partial/pallas_call | solution.py:219
  14.7 2.0 %collective-permute-start.6 = (f32[16,864]{1,0:T(8,128)S(1)}, f32[16,864]{1,0:T(8,128)S(1)}, u32[]{:S(2)}, u32[]{:S(2)}) collective-permute-start(f32[16,864]{1,0:T(8,128)S(1)} %get-tuple-element.32), channel_id=1, source_target_pairs={{0,4},{4,12},{8,0},{12,8},{1,5},{5,13},{9,1},{13,9},{2,6},{6,14},{... | collective-permute-start | bytes 165896 | tf_op jit(solution)/shard_map/ppermute | solution.py:39
  16.7 2.5 %collective-permute-start.7 = (f32[16,864]{1,0:T(8,128)S(1)}, f32[16,864]{1,0:T(8,128)S(1)}, u32[]{:S(2)}, u32[]{:S(2)}) collective-permute-start(f32[16,864]{1,0:T(8,128)S(1)} %get-tuple-element.33), channel_id=1, source_target_pairs={{0,12},{4,8},{8,4},{12,0},{1,13},{5,9},{9,5},{13,1},{2,14},{6,10},... | collective-permute-start | bytes 165896 | tf_op jit(solution)/shard_map/ppermute | solution.py:39
  19.2 0.2 collective-permute-start.8
  19.4 0.0 collective-permute-done.1.refs_1_
  19.4 2.2 %input_partial.1 = (f32[512,256]{1,0:T(8,128)S(1)}, f32[512,256]{1,0:T(8,128)S(1)}, bf16[256,256]{1,0:T(8,128)(2,1)S(1)}) custom-call(f32[32,864]{1,0:T(8,128)S(1)} %get-tuple-element.22.refs_0_, f32[32,864]{1,0:T(8,128)S(1)} %collective-permute-done.1.refs_1_, bf16[32,1024]{1,0:T(8,128)(2,1)S(1)} %get-tuple-element.24.refs_2_.own_high, ...), custom_call_target="tpu_custom_call" | custom-call | flops 8000000000 | bytes 8000000 | tf_op jit(solution)/shard_map/input_partial/pallas_call | solution.py:390
  21.6 0.0 collective-permute-done.6.refs_1_
  21.6 1.1 %collective-permute-done.7.refs_2_ = f32[16,864]{1,0:T(8,128)S(1)} collective-permute-done((f32[16,864]{1,0:T(8,128)S(1)}, f32[16,864]{1,0:T(8,128)S(1)}, u32[]{:S(2)}, u32[]{:S(2)}) %collective-permute-start.7) | collective-permute-done | bytes 55328 | tf_op jit(solution)/shard_map/ppermute | solution.py:39
  22.7 0.7 %collective-permute-done.8.refs_3_ = f32[16,864]{1,0:T(8,128)S(1)} collective-permute-done((f32[16,864]{1,0:T(8,128)S(1)}, f32[16,864]{1,0:T(8,128)S(1)}, u32[]{:S(2)}, u32[]{:S(2)}) %collective-permute-start.8) | collective-permute-done | bytes 55328 | tf_op jit(solution)/shard_map/ppermute | solution.py:39
  23.4 1.4 %collective-permute-start.9 = (f32[8,864]{1,0:T(8,128)S(1)}, f32[8,864]{1,0:T(8,128)S(1)}, u32[]{:S(2)}, u32[]{:S(2)}) collective-permute-start(f32[8,864]{1,0:T(8,128)S(1)} %get-tuple-element.36), channel_id=1, source_target_pairs={{0,2},{1,3},{2,0},{3,1},{4,6},{5,7},{6,4},{7,5},{8,10},{9,11},{10,... | collective-permute-start | bytes 82952 | tf_op jit(solution)/shard_map/ppermute | solution.py:26
  24.7 2.6 %collective-permute-done.9.refs_1_ = f32[8,864]{1,0:T(8,128)S(1)} collective-permute-done((f32[8,864]{1,0:T(8,128)S(1)}, f32[8,864]{1,0:T(8,128)S(1)}, u32[]{:S(2)}, u32[]{:S(2)}) %collective-permute-start.9) | collective-permute-done | bytes 27680 | tf_op jit(solution)/shard_map/ppermute | solution.py:26
  27.3 0.3 weave_channels.1.refs_0_
  27.6 0.6 %collective-permute-start.10 = (f32[8,1728]{1,0:T(8,128)S(1)}, f32[8,1728]{1,0:T(8,128)S(1)}, u32[]{:S(2)}, u32[]{:S(2)}) collective-permute-start(f32[8,1728]{1,0:T(8,128)S(1)} %weave_channels.1.refs_0_), channel_id=1, source_target_pairs={{0,4},{4,8},{8,12},{12,0},{1,5},{5,9},{9,13},{13,1},{2,6},{6,10},{... | collective-permute-start | bytes 165896 | tf_op jit(solution)/shard_map/ppermute | solution.py:39
  28.1 2.0 %collective-permute-start.11 = (f32[8,1728]{1,0:T(8,128)S(1)}, f32[8,1728]{1,0:T(8,128)S(1)}, u32[]{:S(2)}, u32[]{:S(2)}) collective-permute-start(f32[8,1728]{1,0:T(8,128)S(1)} %weave_channels.1.refs_0_), channel_id=1, source_target_pairs={{0,8},{4,12},{8,0},{12,4},{1,9},{5,13},{9,1},{13,5},{2,10},{6,14},... | collective-permute-start | bytes 165896 | tf_op jit(solution)/shard_map/ppermute | solution.py:39
  30.1 1.9 %collective-permute-start.12 = (f32[8,1728]{1,0:T(8,128)S(1)}, f32[8,1728]{1,0:T(8,128)S(1)}, u32[]{:S(2)}, u32[]{:S(2)}) collective-permute-start(f32[8,1728]{1,0:T(8,128)S(1)} %weave_channels.1.refs_0_), channel_id=1, source_target_pairs={{0,12},{4,0},{8,4},{12,8},{1,13},{5,1},{9,5},{13,9},{2,14},{6,2},{... | collective-permute-start | bytes 165896 | tf_op jit(solution)/shard_map/ppermute | solution.py:39
  32.0 0.0 collective-permute-done.5
  32.0 0.9 %add.3 = f32[512,256]{1,0:T(8,128)} add(f32[512,256]{1,0:T(8,128)S(1)} %get-tuple-element.26.after_ref, f32[512,256]{1,0:T(8,128)S(1)} %collective-permute-done.5) | non-fusion elementwise | flops 131072 | bytes 1572864 | tf_op jit(solution)/shard_map/add | solution.py:432
  32.9 0.8 %collective-permute-done.10.refs_1_ = f32[8,1728]{1,0:T(8,128)S(1)} collective-permute-done((f32[8,1728]{1,0:T(8,128)S(1)}, f32[8,1728]{1,0:T(8,128)S(1)}, u32[]{:S(2)}, u32[]{:S(2)}) %collective-permute-start.10) | collective-permute-done | bytes 55328 | tf_op jit(solution)/shard_map/ppermute | solution.py:39
  33.7 0.8 %collective-permute-done.11.refs_2_ = f32[8,1728]{1,0:T(8,128)S(1)} collective-permute-done((f32[8,1728]{1,0:T(8,128)S(1)}, f32[8,1728]{1,0:T(8,128)S(1)}, u32[]{:S(2)}, u32[]{:S(2)}) %collective-permute-start.11) | collective-permute-done | bytes 55328 | tf_op jit(solution)/shard_map/ppermute | solution.py:39
  34.4 0.0 collective-permute-done.12.refs_3_
  34.4 0.7 %stack_slabs.1 = f32[4,8,1728]{2,1,0:T(8,128)} custom-call(f32[8,1728]{1,0:T(8,128)S(1)} %weave_channels.1.refs_0_, f32[8,1728]{1,0:T(8,128)S(1)} %collective-permute-done.10.refs_1_, f32[8,1728]{1,0:T(8,128)S(1)} %collective-permute-done.11.refs_2_, f32[8,1728]{1,0:T(8,128)S(1)} %collective-permute-done.12.refs_3_), custom_call_target="tpu_custom_call" | custom-call | tf_op jit(solution)/shard_map/stack_slabs/pallas_call | solution.py:311
  (2 shorter events, 0.0 us)
Async XLA Ops:
  0.6 5.7 %collective-permute-start = (f32[16,2,16,256]{3,2,1,0:T(8,128)}, f32[16,2,16,256]{3,2,1,0:T(8,128)S(1)}, u32[]{:S(2)}, u32[]{:S(2)}) collective-permute-start(f32[16,2,16,256]{3,2,1,0:T(8,128)} %param.3), channel_id=1, source_target_pairs={{0,1},{1,0},{2,3},{3,2},{4,5},{5,4},{6,7},{7,6},{8,9},{9,8},{10,11... | collective-permute-start | bytes 1572872 | tf_op jit(solution)/shard_map/ppermute | solution.py:26
  1.1 7.5 %collective-permute-start.4 = (f32[32,1,8,128]{3,2,1,0:T(8,128)}, f32[32,1,8,128]{3,2,1,0:T(8,128)S(1)}, u32[]{:S(2)}, u32[]{:S(2)}) collective-permute-start(f32[32,1,8,128]{3,2,1,0:T(8,128)} %param.4), channel_id=1, source_target_pairs={{0,2},{1,3},{2,0},{3,1},{4,6},{5,7},{6,4},{7,5},{8,10},{9,11},{10,... | collective-permute-start | bytes 393224 | tf_op jit(solution)/shard_map/ppermute | solution.py:26
  3.7 8.4 %collective-permute-start.2 = (f32[32,1,8,128]{3,2,1,0:T(8,128)}, f32[32,1,8,128]{3,2,1,0:T(8,128)S(1)}, u32[]{:S(2)}, u32[]{:S(2)}) collective-permute-start(f32[32,1,8,128]{3,2,1,0:T(8,128)} %param.4), channel_id=1, source_target_pairs={{4,0},{5,1},{6,2},{7,3},{8,4},{9,5},{10,6},{11,7},{12,8},{13,9},{1... | collective-permute-start | bytes 393224 | tf_op jit(solution)/shard_map/ppermute | solution.py:414
  5.0 9.1 %collective-permute-start.3 = (f32[32,1,8,128]{3,2,1,0:T(8,128)}, f32[32,1,8,128]{3,2,1,0:T(8,128)S(1)}, u32[]{:S(2)}, u32[]{:S(2)}) collective-permute-start(f32[32,1,8,128]{3,2,1,0:T(8,128)} %param.4), channel_id=1, source_target_pairs={{6,0},{7,1},{4,2},{5,3},{10,4},{11,5},{8,6},{9,7},{14,8},{15,9},{1... | collective-permute-start | bytes 393224 | tf_op jit(solution)/shard_map/ppermute | solution.py:414
  8.6 10.8 %collective-permute-start.1 = (f32[32,864]{1,0:T(8,128)S(1)}, f32[32,864]{1,0:T(8,128)S(1)}, u32[]{:S(2)}, u32[]{:S(2)}) collective-permute-start(f32[32,864]{1,0:T(8,128)S(1)} %get-tuple-element.23), channel_id=1, source_target_pairs={{0,2},{1,3},{2,0},{3,1},{4,6},{5,7},{6,4},{7,5},{8,10},{9,11},{10,... | collective-permute-start | bytes 331784 | tf_op jit(solution)/shard_map/ppermute | solution.py:26
  14.7 6.9 %collective-permute-start.6 = (f32[16,864]{1,0:T(8,128)S(1)}, f32[16,864]{1,0:T(8,128)S(1)}, u32[]{:S(2)}, u32[]{:S(2)}) collective-permute-start(f32[16,864]{1,0:T(8,128)S(1)} %get-tuple-element.32), channel_id=1, source_target_pairs={{0,4},{4,12},{8,0},{12,8},{1,5},{5,13},{9,1},{13,9},{2,6},{6,14},{... | collective-permute-start | bytes 165896 | tf_op jit(solution)/shard_map/ppermute | solution.py:39
  16.7 6.0 %collective-permute-start.7 = (f32[16,864]{1,0:T(8,128)S(1)}, f32[16,864]{1,0:T(8,128)S(1)}, u32[]{:S(2)}, u32[]{:S(2)}) collective-permute-start(f32[16,864]{1,0:T(8,128)S(1)} %get-tuple-element.33), channel_id=1, source_target_pairs={{0,12},{4,8},{8,4},{12,0},{1,13},{5,9},{9,5},{13,1},{2,14},{6,10},... | collective-permute-start | bytes 165896 | tf_op jit(solution)/shard_map/ppermute | solution.py:39
  19.2 4.2 %collective-permute-start.8 = (f32[16,864]{1,0:T(8,128)S(1)}, f32[16,864]{1,0:T(8,128)S(1)}, u32[]{:S(2)}, u32[]{:S(2)}) collective-permute-start(f32[16,864]{1,0:T(8,128)S(1)} %get-tuple-element.34), channel_id=1, source_target_pairs={{0,8},{4,0},{8,12},{12,4},{1,9},{5,1},{9,13},{13,5},{2,10},{6,2},{... | collective-permute-start | bytes 165896 | tf_op jit(solution)/shard_map/ppermute | solution.py:39
  23.4 3.9 %collective-permute-start.9 = (f32[8,864]{1,0:T(8,128)S(1)}, f32[8,864]{1,0:T(8,128)S(1)}, u32[]{:S(2)}, u32[]{:S(2)}) collective-permute-start(f32[8,864]{1,0:T(8,128)S(1)} %get-tuple-element.36), channel_id=1, source_target_pairs={{0,2},{1,3},{2,0},{3,1},{4,6},{5,7},{6,4},{7,5},{8,10},{9,11},{10,... | collective-permute-start | bytes 82952 | tf_op jit(solution)/shard_map/ppermute | solution.py:26
  24.7 7.3 %collective-permute-start.5 = (f32[512,256]{1,0:T(8,128)S(1)}, f32[512,256]{1,0:T(8,128)S(1)}, u32[]{:S(2)}, u32[]{:S(2)}) collective-permute-start(f32[512,256]{1,0:T(8,128)S(1)} %get-tuple-element.27), channel_id=1, source_target_pairs={{0,1},{1,0},{2,3},{3,2},{4,5},{5,4},{6,7},{7,6},{8,9},{9,8},{10,11... | collective-permute-start | bytes 1572872 | tf_op jit(solution)/shard_map/ppermute | solution.py:26
  27.6 6.1 %collective-permute-start.10 = (f32[8,1728]{1,0:T(8,128)S(1)}, f32[8,1728]{1,0:T(8,128)S(1)}, u32[]{:S(2)}, u32[]{:S(2)}) collective-permute-start(f32[8,1728]{1,0:T(8,128)S(1)} %weave_channels.1.refs_0_), channel_id=1, source_target_pairs={{0,4},{4,8},{8,12},{12,0},{1,5},{5,9},{9,13},{13,1},{2,6},{6,10},{... | collective-permute-start | bytes 165896 | tf_op jit(solution)/shard_map/ppermute | solution.py:39
  28.1 6.3 %collective-permute-start.11 = (f32[8,1728]{1,0:T(8,128)S(1)}, f32[8,1728]{1,0:T(8,128)S(1)}, u32[]{:S(2)}, u32[]{:S(2)}) collective-permute-start(f32[8,1728]{1,0:T(8,128)S(1)} %weave_channels.1.refs_0_), channel_id=1, source_target_pairs={{0,8},{4,12},{8,0},{12,4},{1,9},{5,13},{9,1},{13,5},{2,10},{6,14},... | collective-permute-start | bytes 165896 | tf_op jit(solution)/shard_map/ppermute | solution.py:39
  30.1 4.3 %collective-permute-start.12 = (f32[8,1728]{1,0:T(8,128)S(1)}, f32[8,1728]{1,0:T(8,128)S(1)}, u32[]{:S(2)}, u32[]{:S(2)}) collective-permute-start(f32[8,1728]{1,0:T(8,128)S(1)} %weave_channels.1.refs_0_), channel_id=1, source_target_pairs={{0,12},{4,0},{8,4},{12,8},{1,13},{5,1},{9,5},{13,9},{2,14},{6,2},{... | collective-permute-start | bytes 165896 | tf_op jit(solution)/shard_map/ppermute | solution.py:39

commit v7 on v6

--- a/solution.py
+++ b/solution.py
@@ -301,16 +301,24 @@
 def stack_slabs(pieces, back_routes):
     block, width = pieces[0].shape
     parts = len(pieces)
+    anywhere = pl.BlockSpec(memory_space=pl.ANY)
 
     def kernel(*refs):
         slab = lax.axis_index("gz")
+        copies = []
         for k in range(parts):
             source = slab if k == 0 else entry([back_routes[k - 1].index(at) for at in range(parts)], slab)
-            refs[parts][source] = refs[k][...]
-
-    return pl.pallas_call(
-        kernel,
+            copies.append(pltpu.make_async_copy(refs[k], refs[parts].at[source], refs[parts + 1].at[k]))
+            copies[-1].start()
+        for copy in copies:
+            copy.wait()
+
+    return pl.pallas_call(
+        kernel,
+        in_specs=[anywhere] * parts,
+        out_specs=anywhere,
         out_shape=jax.ShapeDtypeStruct((parts, block, width), F32),
+        scratch_shapes=[pltpu.SemaphoreType.DMA((parts,))],
         compiler_params=PARAMS,
         name="stack_slabs",
     )(*pieces).reshape(parts * block, width)

time: 35.3 us -> 35.3 us (level)
  no operation moved by 1% of the time
where the time goes in v7:
time: 35.3 us; the launch traced here: 35.2 us
  starting transfers between devices  16.3 us (46%)
  waiting for transfers between devices  10.5 us (30%)
  Pallas kernels  6.86 us (19%)
  other arithmetic  0.86 us (2%)
  between operations  0.7 us (2%)
    ppermute x6, starting transfers between devices, routed(): return lax.ppermute(value, axis, list(enumerate(route)))  9.16 us
    ppermute x2, waiting for transfers between devices, below(): return lax.ppermute(value, ('gz', 'af'), pairs)  4.58 us
    ppermute x5, starting transfers between devices, swapped(): lax.ppermute(value, axis, [(source, source ^ bits) for source in range(co...  4.53 us
    ppermute x6, waiting for transfers between devices, routed(): return lax.ppermute(value, axis, list(enumerate(route)))  3.3 us
    ppermute x5, waiting for transfers between devices, swapped(): lax.ppermute(value, axis, [(source, source ^ bits) for source in range(co...  2.58 us
    ppermute x2, starting transfers between devices, below(): return lax.ppermute(value, ('gz', 'af'), pairs)  2.57 us
    pallas_call x1, Pallas kernels, prepare(): pl.pallas_call(kernel, in_specs=[HBM, HBM, HBM] + [VMEM] * (cores - 1), o...  2.24 us
    pallas_call x1, Pallas kernels, input_partial(): pl.pallas_call(kernel, out_shape=[jax.ShapeDtypeStruct((channels * planes...  2.17 us
  transfers between devices with their start and end apart: 13, of which 7 were waited for; matrix products, arithmetic and copies ran while one was open for 2% of the time, Pallas kernels for 17%

profile of v7, /device:TPU:0, one launch (start us, length us, event | category | flops | bytes accessed | tf_op | source)
XLA Modules:
  0.0 35.2 jit_solution(13253100187634935947)
XLA Ops:
  0.6 0.5 %collective-permute-start = (f32[16,2,16,256]{3,2,1,0:T(8,128)}, f32[16,2,16,256]{3,2,1,0:T(8,128)S(1)}, u32[]{:S(2)}, u32[]{:S(2)}) collective-permute-start(f32[16,2,16,256]{3,2,1,0:T(8,128)} %param.3), channel_id=1, source_target_pairs={{0,1},{1,0},{2,3},{3,2},{4,5},{5,4},{6,7},{7,6},{8,9},{9,8},{10,11... | collective-permute-start | bytes 1572872 | tf_op jit(solution)/shard_map/ppermute | solution.py:26
  1.1 2.6 %collective-permute-start.4 = (f32[32,1,8,128]{3,2,1,0:T(8,128)}, f32[32,1,8,128]{3,2,1,0:T(8,128)S(1)}, u32[]{:S(2)}, u32[]{:S(2)}) collective-permute-start(f32[32,1,8,128]{3,2,1,0:T(8,128)} %param.4), channel_id=1, source_target_pairs={{0,2},{1,3},{2,0},{3,1},{4,6},{5,7},{6,4},{7,5},{8,10},{9,11},{10,... | collective-permute-start | bytes 393224 | tf_op jit(solution)/shard_map/ppermute | solution.py:26
  3.7 1.3 %collective-permute-start.2 = (f32[32,1,8,128]{3,2,1,0:T(8,128)}, f32[32,1,8,128]{3,2,1,0:T(8,128)S(1)}, u32[]{:S(2)}, u32[]{:S(2)}) collective-permute-start(f32[32,1,8,128]{3,2,1,0:T(8,128)} %param.4), channel_id=1, source_target_pairs={{4,0},{5,1},{6,2},{7,3},{8,4},{9,5},{10,6},{11,7},{12,8},{13,9},{1... | collective-permute-start | bytes 393224 | tf_op jit(solution)/shard_map/ppermute | solution.py:422
  5.0 1.3 %collective-permute-start.3 = (f32[32,1,8,128]{3,2,1,0:T(8,128)}, f32[32,1,8,128]{3,2,1,0:T(8,128)S(1)}, u32[]{:S(2)}, u32[]{:S(2)}) collective-permute-start(f32[32,1,8,128]{3,2,1,0:T(8,128)} %param.4), channel_id=1, source_target_pairs={{6,0},{7,1},{4,2},{5,3},{10,4},{11,5},{8,6},{9,7},{14,8},{15,9},{1... | collective-permute-start | bytes 393224 | tf_op jit(solution)/shard_map/ppermute | solution.py:422
  6.3 0.0 collective-permute-done
  6.3 2.2 %prepare.1 = (bf16[576,1024]{1,0:T(8,128)(2,1)S(1)}, bf16[576,1024]{1,0:T(8,128)(2,1)S(1)}, bf16[32,1024]{1,0:T(8,128)(2,1)S(1)}, bf16[32,1024]{1,0:T(8,128)(2,1...) custom-call(f32[512,256]{1,0:T(8,128)} %bitcast.16, f32[256,128]{1,0:T(8,128)} %bitcast.18, f32[32,1728]{1,0:T(8,128)} %w_hbm.1, ...), custom_call_target="tpu_custom_call" | custom-call | tf_op jit(solution)/shard_map/prepare/pallas_call | solution.py:155
  8.6 0.1 collective-permute-start.1
  8.7 0.0 collective-permute-done.4
  8.7 0.9 %weight_terms.1.terms_ref = f32[64,576]{1,0:T(8,128)S(1)} custom-call(bf16[576,1024]{1,0:T(8,128)(2,1)S(1)} %get-tuple-element.29.high_ref, bf16[576,1024]{1,0:T(8,128)(2,1)S(1)} %get-tuple-element.30.low_ref, bf16[32,1024]{1,0:T(8,128)(2,1)S(1)} %get-tuple-element.24.refs_2_.own_high, bf16[32,1024]{1,0:T(8,128)(2,1)S(1)} %get-tuple-element.25.refs_3_.own_low, ...), custom_call_target="tpu_custom_call" | custom-call | tf_op jit(solution)/shard_map/weight_terms/pallas_call | solution.py:186
  9.5 2.6 %collective-permute-done.2 = f32[32,1,8,128]{3,2,1,0:T(8,128)S(1)} collective-permute-done((f32[32,1,8,128]{3,2,1,0:T(8,128)}, f32[32,1,8,128]{3,2,1,0:T(8,128)S(1)}, u32[]{:S(2)}, u32[]{:S(2)}) %collective-permute-start.2) | collective-permute-done | bytes 131104 | tf_op jit(solution)/shard_map/ppermute | solution.py:422
  12.1 2.0 %collective-permute-done.3 = f32[32,1,8,128]{3,2,1,0:T(8,128)S(1)} collective-permute-done((f32[32,1,8,128]{3,2,1,0:T(8,128)}, f32[32,1,8,128]{3,2,1,0:T(8,128)S(1)}, u32[]{:S(2)}, u32[]{:S(2)}) %collective-permute-start.3) | collective-permute-done | bytes 131104 | tf_op jit(solution)/shard_map/ppermute | solution.py:422
  14.1 0.6 %weight_partial.1 = (f32[16,864]{1,0:T(8,128)S(1)}, f32[16,864]{1,0:T(8,128)S(1)}, f32[16,864]{1,0:T(8,128)S(1)}, f32[16,864]{1,0:T(8,128)S(1)}) custom-call(bf16[576,1024]{1,0:T(8,128)(2,1)S(1)} %get-tuple-element.29.high_ref, bf16[576,1024]{1,0:T(8,128)(2,1)S(1)} %get-tuple-element.30.low_ref, f32[64,576]{1,0:T(8,128)S(1)} %weight_terms.1.terms_ref, ...), custom_call_target="tpu_custom_call" | custom-call | tf_op jit(solution)/shard_map/weight_partial/pallas_call | solution.py:219
  14.7 2.0 %collective-permute-start.6 = (f32[16,864]{1,0:T(8,128)S(1)}, f32[16,864]{1,0:T(8,128)S(1)}, u32[]{:S(2)}, u32[]{:S(2)}) collective-permute-start(f32[16,864]{1,0:T(8,128)S(1)} %get-tuple-element.32), channel_id=1, source_target_pairs={{0,4},{4,12},{8,0},{12,8},{1,5},{5,13},{9,1},{13,9},{2,6},{6,14},{... | collective-permute-start | bytes 165896 | tf_op jit(solution)/shard_map/ppermute | solution.py:39
  16.7 2.5 %collective-permute-start.7 = (f32[16,864]{1,0:T(8,128)S(1)}, f32[16,864]{1,0:T(8,128)S(1)}, u32[]{:S(2)}, u32[]{:S(2)}) collective-permute-start(f32[16,864]{1,0:T(8,128)S(1)} %get-tuple-element.33), channel_id=1, source_target_pairs={{0,12},{4,8},{8,4},{12,0},{1,13},{5,9},{9,5},{13,1},{2,14},{6,10},... | collective-permute-start | bytes 165896 | tf_op jit(solution)/shard_map/ppermute | solution.py:39
  19.2 0.2 collective-permute-start.8
  19.4 0.0 collective-permute-done.1.refs_1_
  19.4 2.2 %input_partial.1 = (f32[512,256]{1,0:T(8,128)S(1)}, f32[512,256]{1,0:T(8,128)S(1)}, bf16[256,256]{1,0:T(8,128)(2,1)S(1)}) custom-call(f32[32,864]{1,0:T(8,128)S(1)} %get-tuple-element.22.refs_0_, f32[32,864]{1,0:T(8,128)S(1)} %collective-permute-done.1.refs_1_, bf16[32,1024]{1,0:T(8,128)(2,1)S(1)} %get-tuple-element.24.refs_2_.own_high, ...), custom_call_target="tpu_custom_call" | custom-call | flops 8000000000 | bytes 8000000 | tf_op jit(solution)/shard_map/input_partial/pallas_call | solution.py:398
  21.6 0.0 collective-permute-done.6.refs_1_
  21.6 1.1 %collective-permute-done.7.refs_2_ = f32[16,864]{1,0:T(8,128)S(1)} collective-permute-done((f32[16,864]{1,0:T(8,128)S(1)}, f32[16,864]{1,0:T(8,128)S(1)}, u32[]{:S(2)}, u32[]{:S(2)}) %collective-permute-start.7) | collective-permute-done | bytes 55328 | tf_op jit(solution)/shard_map/ppermute | solution.py:39
  22.7 0.7 %collective-permute-done.8.refs_3_ = f32[16,864]{1,0:T(8,128)S(1)} collective-permute-done((f32[16,864]{1,0:T(8,128)S(1)}, f32[16,864]{1,0:T(8,128)S(1)}, u32[]{:S(2)}, u32[]{:S(2)}) %collective-permute-start.8) | collective-permute-done | bytes 55328 | tf_op jit(solution)/shard_map/ppermute | solution.py:39
  23.4 1.4 %collective-permute-start.9 = (f32[8,864]{1,0:T(8,128)S(1)}, f32[8,864]{1,0:T(8,128)S(1)}, u32[]{:S(2)}, u32[]{:S(2)}) collective-permute-start(f32[8,864]{1,0:T(8,128)S(1)} %get-tuple-element.36), channel_id=1, source_target_pairs={{0,2},{1,3},{2,0},{3,1},{4,6},{5,7},{6,4},{7,5},{8,10},{9,11},{10,... | collective-permute-start | bytes 82952 | tf_op jit(solution)/shard_map/ppermute | solution.py:26
  24.7 0.0 collective-permute-start.5
  24.7 2.6 %collective-permute-done.9.refs_1_ = f32[8,864]{1,0:T(8,128)S(1)} collective-permute-done((f32[8,864]{1,0:T(8,128)S(1)}, f32[8,864]{1,0:T(8,128)S(1)}, u32[]{:S(2)}, u32[]{:S(2)}) %collective-permute-start.9) | collective-permute-done | bytes 27680 | tf_op jit(solution)/shard_map/ppermute | solution.py:26
  27.3 0.3 weave_channels.1.refs_0_
  27.6 0.6 %collective-permute-start.10 = (f32[8,1728]{1,0:T(8,128)S(1)}, f32[8,1728]{1,0:T(8,128)S(1)}, u32[]{:S(2)}, u32[]{:S(2)}) collective-permute-start(f32[8,1728]{1,0:T(8,128)S(1)} %weave_channels.1.refs_0_), channel_id=1, source_target_pairs={{0,4},{4,8},{8,12},{12,0},{1,5},{5,9},{9,13},{13,1},{2,6},{6,10},{... | collective-permute-start | bytes 165896 | tf_op jit(solution)/shard_map/ppermute | solution.py:39
  28.1 2.0 %collective-permute-start.11 = (f32[8,1728]{1,0:T(8,128)S(1)}, f32[8,1728]{1,0:T(8,128)S(1)}, u32[]{:S(2)}, u32[]{:S(2)}) collective-permute-start(f32[8,1728]{1,0:T(8,128)S(1)} %weave_channels.1.refs_0_), channel_id=1, source_target_pairs={{0,8},{4,12},{8,0},{12,4},{1,9},{5,13},{9,1},{13,5},{2,10},{6,14},... | collective-permute-start | bytes 165896 | tf_op jit(solution)/shard_map/ppermute | solution.py:39
  30.1 1.9 %collective-permute-start.12 = (f32[8,1728]{1,0:T(8,128)S(1)}, f32[8,1728]{1,0:T(8,128)S(1)}, u32[]{:S(2)}, u32[]{:S(2)}) collective-permute-start(f32[8,1728]{1,0:T(8,128)S(1)} %weave_channels.1.refs_0_), channel_id=1, source_target_pairs={{0,12},{4,0},{8,4},{12,8},{1,13},{5,1},{9,5},{13,9},{2,14},{6,2},{... | collective-permute-start | bytes 165896 | tf_op jit(solution)/shard_map/ppermute | solution.py:39
  32.0 0.0 collective-permute-done.5
  32.0 0.9 %add.3 = f32[512,256]{1,0:T(8,128)} add(f32[512,256]{1,0:T(8,128)S(1)} %get-tuple-element.26.after_ref, f32[512,256]{1,0:T(8,128)S(1)} %collective-permute-done.5) | non-fusion elementwise | flops 131072 | bytes 1572864 | tf_op jit(solution)/shard_map/add | solution.py:440
  32.9 0.8 %collective-permute-done.10.refs_1_ = f32[8,1728]{1,0:T(8,128)S(1)} collective-permute-done((f32[8,1728]{1,0:T(8,128)S(1)}, f32[8,1728]{1,0:T(8,128)S(1)}, u32[]{:S(2)}, u32[]{:S(2)}) %collective-permute-start.10) | collective-permute-done | bytes 55328 | tf_op jit(solution)/shard_map/ppermute | solution.py:39
  33.7 0.8 %collective-permute-done.11.refs_2_ = f32[8,1728]{1,0:T(8,128)S(1)} collective-permute-done((f32[8,1728]{1,0:T(8,128)S(1)}, f32[8,1728]{1,0:T(8,128)S(1)}, u32[]{:S(2)}, u32[]{:S(2)}) %collective-permute-start.11) | collective-permute-done | bytes 55328 | tf_op jit(solution)/shard_map/ppermute | solution.py:39
  34.4 0.7 %stack_slabs.1 = f32[4,8,1728]{2,1,0:T(8,128)} custom-call(f32[8,1728]{1,0:T(8,128)S(1)} %weave_channels.1.refs_0_, f32[8,1728]{1,0:T(8,128)S(1)} %collective-permute-done.10.refs_1_, f32[8,1728]{1,0:T(8,128)S(1)} %collective-permute-done.11.refs_2_, f32[8,1728]{1,0:T(8,128)S(1)} %collective-permute-done.12.refs_3_), custom_call_target="tpu_custom_call" | custom-call | tf_op jit(solution)/shard_map/stack_slabs/pallas_call | solution.py:316
  (2 shorter events, 0.0 us)
Async XLA Ops:
  0.6 5.7 %collective-permute-start = (f32[16,2,16,256]{3,2,1,0:T(8,128)}, f32[16,2,16,256]{3,2,1,0:T(8,128)S(1)}, u32[]{:S(2)}, u32[]{:S(2)}) collective-permute-start(f32[16,2,16,256]{3,2,1,0:T(8,128)} %param.3), channel_id=1, source_target_pairs={{0,1},{1,0},{2,3},{3,2},{4,5},{5,4},{6,7},{7,6},{8,9},{9,8},{10,11... | collective-permute-start | bytes 1572872 | tf_op jit(solution)/shard_map/ppermute | solution.py:26
  1.1 7.5 %collective-permute-start.4 = (f32[32,1,8,128]{3,2,1,0:T(8,128)}, f32[32,1,8,128]{3,2,1,0:T(8,128)S(1)}, u32[]{:S(2)}, u32[]{:S(2)}) collective-permute-start(f32[32,1,8,128]{3,2,1,0:T(8,128)} %param.4), channel_id=1, source_target_pairs={{0,2},{1,3},{2,0},{3,1},{4,6},{5,7},{6,4},{7,5},{8,10},{9,11},{10,... | collective-permute-start | bytes 393224 | tf_op jit(solution)/shard_map/ppermute | solution.py:26
  3.7 8.4 %collective-permute-start.2 = (f32[32,1,8,128]{3,2,1,0:T(8,128)}, f32[32,1,8,128]{3,2,1,0:T(8,128)S(1)}, u32[]{:S(2)}, u32[]{:S(2)}) collective-permute-start(f32[32,1,8,128]{3,2,1,0:T(8,128)} %param.4), channel_id=1, source_target_pairs={{4,0},{5,1},{6,2},{7,3},{8,4},{9,5},{10,6},{11,7},{12,8},{13,9},{1... | collective-permute-start | bytes 393224 | tf_op jit(solution)/shard_map/ppermute | solution.py:422
  5.0 9.1 %collective-permute-start.3 = (f32[32,1,8,128]{3,2,1,0:T(8,128)}, f32[32,1,8,128]{3,2,1,0:T(8,128)S(1)}, u32[]{:S(2)}, u32[]{:S(2)}) collective-permute-start(f32[32,1,8,128]{3,2,1,0:T(8,128)} %param.4), channel_id=1, source_target_pairs={{6,0},{7,1},{4,2},{5,3},{10,4},{11,5},{8,6},{9,7},{14,8},{15,9},{1... | collective-permute-start | bytes 393224 | tf_op jit(solution)/shard_map/ppermute | solution.py:422
  8.6 10.8 %collective-permute-start.1 = (f32[32,864]{1,0:T(8,128)S(1)}, f32[32,864]{1,0:T(8,128)S(1)}, u32[]{:S(2)}, u32[]{:S(2)}) collective-permute-start(f32[32,864]{1,0:T(8,128)S(1)} %get-tuple-element.23), channel_id=1, source_target_pairs={{0,2},{1,3},{2,0},{3,1},{4,6},{5,7},{6,4},{7,5},{8,10},{9,11},{10,... | collective-permute-start | bytes 331784 | tf_op jit(solution)/shard_map/ppermute | solution.py:26
  14.7 6.9 %collective-permute-start.6 = (f32[16,864]{1,0:T(8,128)S(1)}, f32[16,864]{1,0:T(8,128)S(1)}, u32[]{:S(2)}, u32[]{:S(2)}) collective-permute-start(f32[16,864]{1,0:T(8,128)S(1)} %get-tuple-element.32), channel_id=1, source_target_pairs={{0,4},{4,12},{8,0},{12,8},{1,5},{5,13},{9,1},{13,9},{2,6},{6,14},{... | collective-permute-start | bytes 165896 | tf_op jit(solution)/shard_map/ppermute | solution.py:39
  16.7 6.0 %collective-permute-start.7 = (f32[16,864]{1,0:T(8,128)S(1)}, f32[16,864]{1,0:T(8,128)S(1)}, u32[]{:S(2)}, u32[]{:S(2)}) collective-permute-start(f32[16,864]{1,0:T(8,128)S(1)} %get-tuple-element.33), channel_id=1, source_target_pairs={{0,12},{4,8},{8,4},{12,0},{1,13},{5,9},{9,5},{13,1},{2,14},{6,10},... | collective-permute-start | bytes 165896 | tf_op jit(solution)/shard_map/ppermute | solution.py:39
  19.2 4.2 %collective-permute-start.8 = (f32[16,864]{1,0:T(8,128)S(1)}, f32[16,864]{1,0:T(8,128)S(1)}, u32[]{:S(2)}, u32[]{:S(2)}) collective-permute-start(f32[16,864]{1,0:T(8,128)S(1)} %get-tuple-element.34), channel_id=1, source_target_pairs={{0,8},{4,0},{8,12},{12,4},{1,9},{5,1},{9,13},{13,5},{2,10},{6,2},{... | collective-permute-start | bytes 165896 | tf_op jit(solution)/shard_map/ppermute | solution.py:39
  23.4 3.9 %collective-permute-start.9 = (f32[8,864]{1,0:T(8,128)S(1)}, f32[8,864]{1,0:T(8,128)S(1)}, u32[]{:S(2)}, u32[]{:S(2)}) collective-permute-start(f32[8,864]{1,0:T(8,128)S(1)} %get-tuple-element.36), channel_id=1, source_target_pairs={{0,2},{1,3},{2,0},{3,1},{4,6},{5,7},{6,4},{7,5},{8,10},{9,11},{10,... | collective-permute-start | bytes 82952 | tf_op jit(solution)/shard_map/ppermute | solution.py:26
  24.7 7.3 %collective-permute-start.5 = (f32[512,256]{1,0:T(8,128)S(1)}, f32[512,256]{1,0:T(8,128)S(1)}, u32[]{:S(2)}, u32[]{:S(2)}) collective-permute-start(f32[512,256]{1,0:T(8,128)S(1)} %get-tuple-element.27), channel_id=1, source_target_pairs={{0,1},{1,0},{2,3},{3,2},{4,5},{5,4},{6,7},{7,6},{8,9},{9,8},{10,11... | collective-permute-start | bytes 1572872 | tf_op jit(solution)/shard_map/ppermute | solution.py:26
  27.6 6.1 %collective-permute-start.10 = (f32[8,1728]{1,0:T(8,128)S(1)}, f32[8,1728]{1,0:T(8,128)S(1)}, u32[]{:S(2)}, u32[]{:S(2)}) collective-permute-start(f32[8,1728]{1,0:T(8,128)S(1)} %weave_channels.1.refs_0_), channel_id=1, source_target_pairs={{0,4},{4,8},{8,12},{12,0},{1,5},{5,9},{9,13},{13,1},{2,6},{6,10},{... | collective-permute-start | bytes 165896 | tf_op jit(solution)/shard_map/ppermute | solution.py:39
  28.1 6.3 %collective-permute-start.11 = (f32[8,1728]{1,0:T(8,128)S(1)}, f32[8,1728]{1,0:T(8,128)S(1)}, u32[]{:S(2)}, u32[]{:S(2)}) collective-permute-start(f32[8,1728]{1,0:T(8,128)S(1)} %weave_channels.1.refs_0_), channel_id=1, source_target_pairs={{0,8},{4,12},{8,0},{12,4},{1,9},{5,13},{9,1},{13,5},{2,10},{6,14},... | collective-permute-start | bytes 165896 | tf_op jit(solution)/shard_map/ppermute | solution.py:39
  30.1 4.3 %collective-permute-start.12 = (f32[8,1728]{1,0:T(8,128)S(1)}, f32[8,1728]{1,0:T(8,128)S(1)}, u32[]{:S(2)}, u32[]{:S(2)}) collective-permute-start(f32[8,1728]{1,0:T(8,128)S(1)} %weave_channels.1.refs_0_), channel_id=1, source_target_pairs={{0,12},{4,0},{8,4},{12,8},{1,13},{5,1},{9,5},{13,9},{2,14},{6,2},{... | collective-permute-start | bytes 165896 | tf_op jit(solution)/shard_map/ppermute | solution.py:39
